TPU v7x, 32 devices: a whole 2x2x4 slice. The times are simulated.
32 devices in a mesh: section: 2 (over y), batch: 4 (over x, core), tensor: 4 (over z).
Axes of the slice: x: 2, y: 2, z: 4, core: 2. Of those that a mesh axis runs over, the one named last changes fastest.
Arguments:
- ids_beam: int32 [8, 256], P('batch'), may hold values from 0 to 15999
- beam_map: int32 [8], replicated, may hold values from 0 to 7, each once
- lengths: int32 [8], replicated, may hold values from 1 to 256, 1536 in all
- embed_table: bfloat16 [16000, 4096], P(None, ('section', 'tensor')), may hold values from -6 to 6
- gain_attn: bfloat16 [2, 4096], P('section'), may hold values from 0.099609375 to 1.8984375
- w_query: bfloat16 [2, 4096, 4096], P('section', None, 'tensor'), may hold values from -1 to 1
- w_key: bfloat16 [2, 4096, 4096], P('section', None, 'tensor'), may hold values from -3 to 3
- w_value: bfloat16 [2, 4096, 4096], P('section', None, 'tensor'), may hold values from -0.09375 to 0.09375
- w_out: bfloat16 [2, 4096, 4096], P('section', 'tensor'), may hold values from -0.09375 to 0.09375
- gain_mlp: bfloat16 [2, 4096], P('section'), may hold values from 0.099609375 to 1.8984375
- w_gate: bfloat16 [2, 4096, 8192], P('section', None, 'tensor'), may hold values from -0.09375 to 0.09375
- w_up: bfloat16 [2, 4096, 8192], P('section', None, 'tensor'), may hold values from -0.09375 to 0.09375
- w_down: bfloat16 [2, 8192, 4096], P('section', 'tensor'), may hold values from -0.0625 to 0.0625
- final_gain: bfloat16 [4096], replicated, may hold values from 0.099609375 to 1.8984375
- score_weight: bfloat16 [4096], replicated, may hold values from -0.09375 to 0.09375
Outputs:
- residual_output: bfloat16 [8, 256, 4096], P('batch', 'tensor', 'section')
- scores: float32 [8], P('batch')
Inputs may be any that keep to these rules, and one draw needn't show every extreme that they name: A permutation: candidate c reads row beam_map[c] of ids_beam. `lengths`: the score is read at the last token before the padding.
All inputs are finite; a program needn't handle non-finite values.
Results may differ from a plain program's by a relative error of at most 0.04.
Values may be sent and summed in bfloat16 or wider, within the bound.
No kernel may reach another device: no remote copies, remote signals or barrier semaphores. Data moves between devices by JAX's collectives and lax.ppermute only.
A program may use at most 256 MiB of HBM per device.

v0:
```python
import jax
import jax.numpy as jnp
from jax import lax
from jax.sharding import PartitionSpec as P

HEAD_DIM = 128


EPSILON = 1e-05
ROTARY_FREQ_BASE = 10000.0


def shifted(value, axis, steps):
    count = lax.axis_size(axis)
    leading, last = (max(0, -steps), min(count, count - steps))
    return lax.ppermute(value, axis, [(source, source + steps) for source in range(leading, last)])


def rms_norm(hidden, scale_gain):
    values = hidden.astype(jnp.float32)
    inverse = lax.rsqrt(jnp.mean(values * values, axis=-1, keepdims=True) + EPSILON)
    return (values * inverse * scale_gain.astype(jnp.float32)).astype(jnp.bfloat16)


def rope_tables(length, head_dim):
    half_dim = head_dim // 2
    frequency = ROTARY_FREQ_BASE ** (-(jnp.arange(half_dim, dtype=jnp.float32) / half_dim))
    angles = jnp.arange(length, dtype=jnp.float32)[:, None] * frequency[None, :]
    return (jnp.cos(angles), jnp.sin(angles))


def rotate(values, cosine_table, sine_table):
    half_dim = values.shape[-1] // 2
    first_half = values[..., :half_dim]
    second_half = values[..., half_dim:]
    cosine_wide = cosine_table[:, None, :]
    sine_wide = sine_table[:, None, :]
    return jnp.concatenate(
        [
            first_half * cosine_wide - second_half * sine_wide,
            second_half * cosine_wide + first_half * sine_wide,
        ],
        axis=-1,
    )


def final_score(last_row, final_gain, score_weight):
    values = last_row.astype(jnp.float32)
    inverse = lax.rsqrt(jnp.mean(values * values, axis=-1, keepdims=True) + EPSILON)
    return jnp.sum(
        values * inverse * final_gain.astype(jnp.float32) * score_weight.astype(jnp.float32),
        axis=-1,
    )


def project_three(normed, w_query, w_key, w_value):
    return jnp.stack(
        [
            jnp.dot(normed, w_query, preferred_element_type=jnp.float32),
            jnp.dot(normed, w_key, preferred_element_type=jnp.float32),
            jnp.dot(normed, w_value, preferred_element_type=jnp.float32),
        ],
        axis=0,
    )


def project_two(normed, w_gate, w_up):
    return jnp.stack(
        [
            jnp.dot(normed, w_gate, preferred_element_type=jnp.float32),
            jnp.dot(normed, w_up, preferred_element_type=jnp.float32),
        ],
        axis=0,
    )


def attend(projected, cosine_table, sine_table, causal):
    length = projected.shape[1]
    local_head_count = projected.shape[2] // HEAD_DIM
    query_rot = rotate(
        projected[0].reshape(length, local_head_count, HEAD_DIM), cosine_table, sine_table
    ).astype(jnp.bfloat16)
    key_rot = rotate(
        projected[1].reshape(length, local_head_count, HEAD_DIM), cosine_table, sine_table
    ).astype(jnp.bfloat16)
    value_proj = projected[2].astype(jnp.bfloat16).reshape(length, local_head_count, HEAD_DIM)
    scores = jnp.einsum(
        "qhd,khd->hqk", query_rot, key_rot, preferred_element_type=jnp.float32
    ) * HEAD_DIM ** (-0.5)
    scores = jnp.where(causal[None], scores, -jnp.inf)
    weights_soft = jax.nn.softmax(scores, axis=-1).astype(jnp.bfloat16)
    attended = jnp.einsum(
        "hqk,khd->qhd", weights_soft, value_proj, preferred_element_type=jnp.float32
    )
    return attended.astype(jnp.bfloat16).reshape(length, local_head_count * HEAD_DIM)


def activate(projected):
    return (jax.nn.silu(projected[0]) * projected[1]).astype(jnp.bfloat16)


def tensor_total(term_rows):
    return lax.psum(term_rows.astype(jnp.bfloat16), "tensor").astype(jnp.float32)


def layer_whole(hidden, layer_weights, cosine_table, sine_table, causal):
    gain_attn, w_query, w_key, w_value, w_out, gain_mlp, w_gate, w_up, w_down = layer_weights
    normed = rms_norm(hidden, gain_attn)
    attended = attend(
        project_three(normed, w_query, w_key, w_value), cosine_table, sine_table, causal
    )
    attn_sum = tensor_total(jnp.dot(attended, w_out, preferred_element_type=jnp.float32))
    middle = (hidden.astype(jnp.float32) + attn_sum).astype(jnp.bfloat16)
    inner_act = activate(project_two(rms_norm(middle, gain_mlp), w_gate, w_up))
    mlp_sum = tensor_total(jnp.dot(inner_act, w_down, preferred_element_type=jnp.float32))
    return (middle.astype(jnp.float32) + mlp_sum).astype(jnp.bfloat16)


def body(
    ids_beam,
    beam_map,
    lengths,
    embed_table,
    gain_attn,
    w_query,
    w_key,
    w_value,
    w_out,
    gain_mlp,
    w_gate,
    w_up,
    w_down,
    final_gain,
    score_weight,
):
    section_index = lax.axis_index("section")
    batch_index = lax.axis_index("batch")
    tensor_index = lax.axis_index("tensor")
    per_device = ids_beam.shape[0]
    length = ids_beam.shape[1]
    all_cands = beam_map.shape[0]
    owned_cands = batch_index * per_device + jnp.arange(per_device, dtype=jnp.int32)
    matches = jnp.arange(all_cands, dtype=jnp.int32)[None, :] == owned_cands[:, None]
    beams_owned = jnp.sum(jnp.where(matches, beam_map[None, :], 0), axis=1)
    lengths_owned = jnp.sum(jnp.where(matches, lengths[None, :], 0), axis=1)
    looked = jnp.take(embed_table, ids_beam, axis=0)
    every_beam = lax.all_gather(looked, "batch", axis=0, tiled=True)
    picked = jnp.take(every_beam, beams_owned, axis=0)
    embedded = lax.all_gather(picked, ("section", "tensor"), axis=2, tiled=True)
    stacked = (gain_attn, w_query, w_key, w_value, w_out, gain_mlp, w_gate, w_up, w_down)
    layer_weights = tuple((tensor_arg[0] for tensor_arg in stacked))
    cosine_table, sine_table = rope_tables(length, HEAD_DIM)
    token_positions = jnp.arange(length)
    causal = token_positions[:, None] >= token_positions[None, :]
    share_rows = length // lax.axis_size("tensor")
    incoming = jnp.zeros((length, embedded.shape[2]), jnp.bfloat16)
    results = []
    for step_index in range(per_device + 1):
        source = embedded[min(step_index, per_device - 1)]
        current = jnp.where(section_index == 0, source, incoming)
        produced_rows = layer_whole(current, layer_weights, cosine_table, sine_table, causal)
        if step_index < per_device:
            incoming = shifted(produced_rows, "section", 1)
        if step_index >= 1:
            results.append(produced_rows)
    finals = jnp.stack(results, axis=0)
    own_rows = lax.dynamic_slice_in_dim(finals, tensor_index * share_rows, share_rows, 1)
    pooled = jnp.take_along_axis(finals, (lengths_owned - 1)[:, None, None], axis=1)[:, 0, :]
    half_width = own_rows.shape[2] // lax.axis_size("section")
    keep_half = lax.dynamic_slice_in_dim(own_rows, section_index * half_width, half_width, 2)
    received_half, received_pooled = shifted((own_rows[:, :, :half_width], pooled), "section", -1)
    first_section = section_index == 0
    shown_rows = jnp.where(first_section, received_half, keep_half)
    shown_pooled = jnp.where(first_section, received_pooled, pooled)
    scores = final_score(shown_pooled, final_gain, score_weight)
    return (shown_rows, scores)


def solution(mesh):
    placed = (
        P("batch", None),
        P(),
        P(),
        P(None, ("section", "tensor")),
        P("section", None),
        P("section", None, "tensor"),
        P("section", None, "tensor"),
        P("section", None, "tensor"),
        P("section", "tensor", None),
        P("section", None),
        P("section", None, "tensor"),
        P("section", None, "tensor"),
        P("section", "tensor", None),
        P(),
        P(),
    )
    return jax.shard_map(
        body,
        mesh=mesh,
        in_specs=placed,
        out_specs=(P("batch", "tensor", "section"), P("batch")),
        check_vma=False,
    )
```

profile of v0, /device:TPU:0, one launch (start us, length us, event | category | flops | bytes accessed | tf_op | source)
XLA Modules:
  0.0 956.4 jit_solution(13317318694306459853)
XLA Ops:
  8.6 9.8 %gather_fusion = bf16[512,512]{1,0:T(8,128)(2,1)S(1)} fusion(bf16[16000,512]{1,0:T(8,128)(2,1)} %param.18, s32[1024]{0:T(1024)S(1)} %pad_clamp_fusion.1), kind=kCustom, calls=%fused_computation | custom fusion | bytes 1050624 | tf_op jit(solution)/shard_map/jit(_take)/gather | solution.py:146
  20.2 24.6 %all-gather.3.cloned.1.call-done = bf16[8,256,512]{2,1,0:T(8,128)(2,1)} async-done(((bf16[2,256,512]{2,1,0:T(8,128)(2,1)}), bf16[8,256,512]{2,1,0:T(8,128)(2,1)}) %all-gather.3.cloned.1.call-update) | async-done | bytes 2097168 | tf_op jit(solution)/shard_map/all_gather | solution.py:147
  48.2 11.4 %copy.94 = bf16[1024,4096]{1,0:T(8,128)(2,1)} copy(bf16[1024,4096]{0,1:T(8,128)(2,1)} %bitcast.155) | data formatting | bytes 16777216 | tf_op jit(solution)/shard_map/dot_general | solution.py:59
  59.6 11.3 %copy.95 = bf16[1024,4096]{1,0:T(8,128)(2,1)} copy(bf16[1024,4096]{0,1:T(8,128)(2,1)} %bitcast.156) | data formatting | bytes 16777216 | tf_op jit(solution)/shard_map/dot_general | solution.py:60
  71.2 51.9 %all-gather.5.cloned.1.call-done = bf16[2,256,4096]{2,1,0:T(8,128)(2,1)} async-done(((bf16[2,256,512]{2,1,0:T(8,128)(2,1)}), bf16[2,256,4096]{2,1,0:T(8,128)(2,1)}) %all-gather.5.cloned.1.call-update) | async-done | bytes 4194320 | tf_op jit(solution)/shard_map/all_gather | solution.py:149
  125.3 6.4 fusion.100
  131.9 6.6 fusion.94
  138.6 5.8 fusion.92
  148.9 7.2 fusion.35
  156.8 84.1 %all-reduce.7.cloned.1.call-done = bf16[256,4096]{1,0:T(8,128)(2,1)} async-done(((bf16[256,4096]{1,0:T(8,128)(2,1)}), bf16[256,4096]{1,0:T(8,128)(2,1)}) %all-reduce.7.cloned.1.call-update) | async-done | bytes 2097168 | tf_op jit(solution)/shard_map/psum | solution.py:103
  244.4 8.3 fusion.19
  253.8 4.7 fusion.80
  258.5 11.6 %fusion.44 = bf16[256,4096]{1,0:T(8,128)(2,1)} fusion(bf16[256,2048]{1,0:T(8,128)(2,1)S(1)} %fusion.80, bf16[1,2048,4096]{2,1,0:T(8,128)(2,1)} %param.27), kind=kOutput, calls=%fused_computation.63 | convolution fusion | flops 4296015872 | bytes 19922944 | tf_op jit(solution)/shard_map/dot_general | solution.py:115
  270.1 85.6 %all-reduce.9.cloned.1.call-done = bf16[256,4096]{1,0:T(8,128)(2,1)} async-done(((bf16[256,4096]{1,0:T(8,128)(2,1)}), bf16[256,4096]{1,0:T(8,128)(2,1)}) %all-reduce.9.cloned.1.call-update) | async-done | bytes 2097168 | tf_op jit(solution)/shard_map/psum | solution.py:103
  362.1 44.3 %collective-permute-done = bf16[256,4096]{1,0:T(8,128)(2,1)S(1)} collective-permute-done((bf16[256,4096]{1,0:T(8,128)(2,1)S(1)}, bf16[256,4096]{1,0:T(8,128)(2,1)S(1)}, u32[]{:S(2)}, u32[]{:S(2)}) %collective-permute-start) | collective-permute-done | bytes 2097184 | tf_op jit(solution)/shard_map/ppermute | solution.py:16
  407.5 6.1 fusion.90
  424.7 4.0 fusion.230
  430.6 7.2 fusion.38
  438.0 86.6 %all-reduce.11.cloned.1.call-done = bf16[256,4096]{1,0:T(8,128)(2,1)} async-done(((bf16[256,4096]{1,0:T(8,128)(2,1)}), bf16[256,4096]{1,0:T(8,128)(2,1)}) %all-reduce.11.cloned.1.call-update) | async-done | bytes 2097168 | tf_op jit(solution)/shard_map/psum | solution.py:103
  527.4 9.0 fusion.17
  537.4 4.7 fusion.11
  542.1 11.8 %fusion.47 = bf16[256,4096]{1,0:T(8,128)(2,1)} fusion(bf16[1,2048,4096]{2,1,0:T(8,128)(2,1)} %param.27, f32[256,2048]{1,0:T(8,128)S(1)} %fusion.11, f32[256,2048]{1,0:T(8,128)S(1)} %fusion.17), kind=kOutput, calls=%fused_computation.64 | convolution fusion | flops 4299161600 | bytes 23068672 | tf_op jit(solution)/shard_map/dot_general | solution.py:115
  554.0 85.6 %all-reduce.13.cloned.1.call-done = bf16[256,4096]{1,0:T(8,128)(2,1)} async-done(((bf16[256,4096]{1,0:T(8,128)(2,1)}), bf16[256,4096]{1,0:T(8,128)(2,1)}) %all-reduce.13.cloned.1.call-update) | async-done | bytes 2097168 | tf_op jit(solution)/shard_map/psum | solution.py:103
  646.4 44.5 %collective-permute-done.1 = bf16[256,4096]{1,0:T(8,128)(2,1)S(1)} collective-permute-done((bf16[256,4096]{1,0:T(8,128)(2,1)S(1)}, bf16[256,4096]{1,0:T(8,128)(2,1)S(1)}, u32[]{:S(2)}, u32[]{:S(2)}) %collective-permute-start.1) | collective-permute-done | bytes 2097184 | tf_op jit(solution)/shard_map/ppermute | solution.py:16
  691.9 6.9 fusion.86
  715.1 7.1 fusion.41
  722.6 86.5 %all-reduce.15.cloned.1.call-done = bf16[256,4096]{1,0:T(8,128)(2,1)} async-done(((bf16[256,4096]{1,0:T(8,128)(2,1)}), bf16[256,4096]{1,0:T(8,128)(2,1)}) %all-reduce.15.cloned.1.call-update) | async-done | bytes 2097168 | tf_op jit(solution)/shard_map/psum | solution.py:103
  812.5 9.0 fusion.15
  822.6 4.7 fusion.9
  827.3 11.7 %fusion.50 = bf16[256,4096]{1,0:T(8,128)(2,1)} fusion(bf16[1,2048,4096]{2,1,0:T(8,128)(2,1)} %param.27, f32[256,2048]{1,0:T(8,128)S(1)} %fusion.9, f32[256,2048]{1,0:T(8,128)S(1)} %fusion.15), kind=kOutput, calls=%fused_computation.65 | convolution fusion | flops 4299161600 | bytes 23068672 | tf_op jit(solution)/shard_map/dot_general | solution.py:115
  839.7 84.9 %all-reduce.17.cloned.1.call-done = bf16[256,4096]{1,0:T(8,128)(2,1)} async-done(((bf16[256,4096]{1,0:T(8,128)(2,1)}), bf16[256,4096]{1,0:T(8,128)(2,1)}) %all-reduce.17.cloned.1.call-update) | async-done | bytes 2097168 | tf_op jit(solution)/shard_map/psum | solution.py:103
  934.6 11.6 %collective-permute-done.3 = bf16[2,4096]{1,0:T(2,128)(2,1)S(1)} collective-permute-done((bf16[2,4096]{1,0:T(2,128)(2,1)S(1)}, bf16[2,4096]{1,0:T(2,128)(2,1)S(1)}, u32[]{:S(2)}, u32[]{:S(2)}) %collective-permute-start.3) | collective-permute-done | bytes 16416 | tf_op jit(solution)/shard_map/ppermute | solution.py:16
  (170 shorter events, 85.8 us)
Async XLA Ops:
  7.2 37.6 %all-gather.3.cloned.1.call-start = ((), (), s32[]{:S(2)}) async-start(), calls=%async_computation | async-start | bytes 2621440 | tf_op jit(solution)/shard_map/all_gather | solution.py:147
  8.6 10.8 %copy-start.17 = (s32[8]{0:T(128)S(1)}, s32[8]{0:T(128)}, u32[]{:S(2)}) copy-start(s32[8]{0:T(128)} %param.17) | copy-start | bytes 100
  8.6 10.8 %copy-start.18 = (s32[8]{0:T(128)S(1)}, s32[8]{0:T(128)}, u32[]{:S(2)}) copy-start(s32[8]{0:T(128)} %param.16) | copy-start | bytes 100
  18.4 29.7 %copy-start.10 = (bf16[1,4096]{1,0:T(2,128)(2,1)S(1)}, bf16[1,4096]{1,0:T(2,128)(2,1)}, u32[]{:S(2)}) copy-start(bf16[1,4096]{1,0:T(2,128)(2,1)} %param.19) | copy-start | bytes 24580
  19.4 103.7 %all-gather.5.cloned.1.call-start = ((), (), s32[]{:S(2)}) async-start(), calls=%async_computation.1 | async-start | bytes 4718592 | tf_op jit(solution)/shard_map/all_gather | solution.py:149
  47.9 193.0 %all-reduce.7.cloned.1.call-start = ((), (), s32[]{:S(2)}) async-start(), calls=%async_computation.2 | async-start | bytes 4194304 | tf_op jit(solution)/shard_map/psum | solution.py:103
  70.9 73.8 %copy-start.9 = (pred[256,256]{0,1:T(8,128)(4,1)}, pred[256,256]{0,1:T(8,128)(4,1)S(1)}, u32[]{:S(2)}) copy-start(pred[256,256]{0,1:T(8,128)(4,1)S(1)} %iota_compare_fusion) | copy-start | bytes 196612
  156.0 199.7 %all-reduce.9.cloned.1.call-start = ((), (), s32[]{:S(2)}) async-start(), calls=%async_computation.3 | async-start | bytes 4194304 | tf_op jit(solution)/shard_map/psum | solution.py:103
  156.7 96.0 %copy-start.12 = (f32[1,4096]{1,0:T(1,128)}, f32[1,4096]{1,0:T(1,128)S(1)}, u32[]{:S(2)}) copy-start(f32[1,4096]{1,0:T(1,128)S(1)} %mul.617) | copy-start | bytes 49156
  240.9 11.9 %slice-start.4 = ((s8[16777216]{0:T(1024)(128)(4,1)}), s8[4194304]{0:T(1024)(128)(4,1)S(1)}, s32[]{:S(2)}) async-start(s8[16777216]{0:T(1024)(128)(4,1)} %bitcast.190), calls=%async_computation.12 | async-start | bytes 8388608
  244.4 9.4 slice-start.7
  270.1 254.5 %all-reduce.11.cloned.1.call-start = ((), (), s32[]{:S(2)}) async-start(), calls=%async_computation.4 | async-start | bytes 4194304 | tf_op jit(solution)/shard_map/psum | solution.py:103
  355.7 50.8 %copy-start.2 = (bf16[2,256,4096]{2,1,0:T(8,128)(2,1)S(1)}, bf16[2,256,4096]{2,1,0:T(8,128)(2,1)}, u32[]{:S(2)}) copy-start(bf16[2,256,4096]{2,1,0:T(8,128)(2,1)} %all-gather.5.cloned.1.call-done) | copy-start | bytes 12582916
  358.2 48.3 %collective-permute-start = (bf16[256,4096]{1,0:T(8,128)(2,1)S(1)}, bf16[256,4096]{1,0:T(8,128)(2,1)S(1)}, u32[]{:S(2)}, u32[]{:S(2)}) collective-permute-start(bf16[256,4096]{1,0:T(8,128)(2,1)S(1)} %fusion.60), channel_id=1, source_target_pairs={{0,16},{1,17},{2,18},{3,19},{4,20},{5,21},{6,22},{7,23},{8,24},{9,... | collective-permute-start | bytes 6291464 | tf_op jit(solution)/shard_map/ppermute | solution.py:16
  407.5 9.6 %slice-start.16 = ((s8[8388608]{0:T(1024)(128)(4,1)}), s8[4194304]{0:T(1024)(128)(4,1)S(1)}, s32[]{:S(2)}) async-start(s8[8388608]{0:T(1024)(128)(4,1)} %bitcast.196), calls=%async_computation.24 | async-start | bytes 8388608
  437.7 89.6 %copy-start.13 = (f32[1,4096]{1,0:T(1,128)S(1)}, f32[1,4096]{1,0:T(1,128)}, u32[]{:S(2)}) copy-start(f32[1,4096]{1,0:T(1,128)} %copy-done.12) | copy-start | bytes 49156
  437.8 201.8 %all-reduce.13.cloned.1.call-start = ((), (), s32[]{:S(2)}) async-start(), calls=%async_computation.5 | async-start | bytes 4194304 | tf_op jit(solution)/shard_map/psum | solution.py:103
  524.6 11.8 %slice-start.8 = ((s8[16777216]{0:T(1024)(128)(4,1)}), s8[4194304]{0:T(1024)(128)(4,1)S(1)}, s32[]{:S(2)}) async-start(s8[16777216]{0:T(1024)(128)(4,1)} %bitcast.192), calls=%async_computation.16 | async-start | bytes 8388608
  527.3 10.1 %slice-start.11 = ((s8[16777216]{0:T(1024)(128)(4,1)}), s8[4194304]{0:T(1024)(128)(4,1)S(1)}, s32[]{:S(2)}) async-start(s8[16777216]{0:T(1024)(128)(4,1)} %bitcast.192), calls=%async_computation.19 | async-start | bytes 8388608
  553.9 255.2 %all-reduce.15.cloned.1.call-start = ((), (), s32[]{:S(2)}) async-start(), calls=%async_computation.6 | async-start | bytes 4194304 | tf_op jit(solution)/shard_map/psum | solution.py:103
  639.5 51.4 %copy-start.3 = (bf16[2,256,4096]{2,1,0:T(8,128)(2,1)S(1)}, bf16[2,256,4096]{2,1,0:T(8,128)(2,1)}, u32[]{:S(2)}) copy-start(bf16[2,256,4096]{2,1,0:T(8,128)(2,1)} %all-gather.5.cloned.1.call-done) | copy-start | bytes 12582916
  642.7 48.3 %collective-permute-start.1 = (bf16[256,4096]{1,0:T(8,128)(2,1)S(1)}, bf16[256,4096]{1,0:T(8,128)(2,1)S(1)}, u32[]{:S(2)}, u32[]{:S(2)}) collective-permute-start(bf16[256,4096]{1,0:T(8,128)(2,1)S(1)} %fusion.68), channel_id=1, source_target_pairs={{0,16},{1,17},{2,18},{3,19},{4,20},{5,21},{6,22},{7,23},{8,24},{9,... | collective-permute-start | bytes 6291464 | tf_op jit(solution)/shard_map/ppermute | solution.py:16
  691.9 10.4 %copy-start.6 = (bf16[256,4096]{1,0:T(8,128)(2,1)}, bf16[256,4096]{1,0:T(8,128)(2,1)S(1)}, u32[]{:S(2)}) copy-start(bf16[256,4096]{1,0:T(8,128)(2,1)S(1)} %get-tuple-element.7) | copy-start | bytes 6291460
  691.9 10.4 %slice-start.18 = ((s8[8388608]{0:T(1024)(128)(4,1)}), s8[4194304]{0:T(1024)(128)(4,1)S(1)}, s32[]{:S(2)}) async-start(s8[8388608]{0:T(1024)(128)(4,1)} %bitcast.198), calls=%async_computation.26 | async-start | bytes 8388608
  722.3 90.2 %copy-start.14 = (f32[1,4096]{1,0:T(1,128)S(1)}, f32[1,4096]{1,0:T(1,128)}, u32[]{:S(2)}) copy-start(f32[1,4096]{1,0:T(1,128)} %copy-done.12) | copy-start | bytes 49156
  722.3 202.4 %all-reduce.17.cloned.1.call-start = ((), (), s32[]{:S(2)}) async-start(), calls=%async_computation.7 | async-start | bytes 4194304 | tf_op jit(solution)/shard_map/psum | solution.py:103
  809.1 12.4 %slice-start.12 = ((s8[16777216]{0:T(1024)(128)(4,1)}), s8[4194304]{0:T(1024)(128)(4,1)S(1)}, s32[]{:S(2)}) async-start(s8[16777216]{0:T(1024)(128)(4,1)} %bitcast.194), calls=%async_computation.20 | async-start | bytes 8388608
  812.4 9.1 copy-start.4
  812.5 9.1 slice-start.13
  812.5 10.1 %slice-start.15 = ((s8[16777216]{0:T(1024)(128)(4,1)}), s8[4194304]{0:T(1024)(128)(4,1)S(1)}, s32[]{:S(2)}) async-start(s8[16777216]{0:T(1024)(128)(4,1)} %bitcast.194), calls=%async_computation.23 | async-start | bytes 8388608
  930.3 16.9 %collective-permute-start.2 = (bf16[2,64,2048]{2,1,0:T(8,128)(2,1)S(1)}, bf16[2,64,2048]{2,1,0:T(8,128)(2,1)S(1)}, u32[]{:S(2)}, u32[]{:S(2)}) collective-permute-start(bf16[2,64,2048]{2,1,0:T(8,128)(2,1)S(1)} %fusion.128), channel_id=1, source_target_pairs={{16,0},{17,1},{18,2},{19,3},{20,4},{21,5},{22,6},{23,7},{24,8},{25... | collective-permute-start | bytes 1572872 | tf_op jit(solution)/shard_map/ppermute | solution.py:16
  933.3 13.0 %collective-permute-start.3 = (bf16[2,4096]{1,0:T(2,128)(2,1)S(1)}, bf16[2,4096]{1,0:T(2,128)(2,1)S(1)}, u32[]{:S(2)}, u32[]{:S(2)}) collective-permute-start(bf16[2,4096]{1,0:T(2,128)(2,1)S(1)} %broadcast_select_fusion.4), channel_id=1, source_target_pairs={{16,0},{17,1},{18,2},{19,3},{20,4},{21,5},{22,6},{23,7},{24,8},{25... | collective-permute-start | bytes 49160 | tf_op jit(solution)/shard_map/ppermute | solution.py:16
  (20 other events, 114.5 us)
Sparse Core Ops, SparseCore 0:
  19.5 25.2 all-gather.2
  48.0 75.0 all-gather.4
  156.1 84.6 all-reduce.6
  270.2 85.4 all-reduce.8
  437.9 86.6 all-reduce.10
  554.0 85.4 all-reduce.12
  722.4 86.6 all-reduce.14
  839.2 85.4 all-reduce.16
where the time goes:
time: 961 us; the launch traced here: 956 us
  waiting for transfers between devices  690 us (72%)
  matrix products  157 us (16%)
  local copies, waits for them, and re-layouts  44.8 us (5%)
  other arithmetic  37.3 us (4%)
  between operations  15.2 us (2%)
  starting transfers between devices  11.4 us (1%)
    psum x6, waiting for transfers between devices, tensor_total(): lax.psum(term_rows.astype(jnp.bfloat16), 'tensor').astype(jnp.float32)  513 us
    ppermute x4, waiting for transfers between devices, shifted(): lax.ppermute(value, axis, [(source, source + steps) for source in range(l...  100 us
    all_gather x1, waiting for transfers between devices, body(): embedded = lax.all_gather(picked, ('section', 'tensor'), axis=2, tiled=True)  51.9 us
    dot_general x3, matrix products, layer_whole(): jnp.dot(inner_act, w_down, preferred_element_type=jnp.float32)  35.1 us
    dot_general x3, matrix products, project_two(): jnp.dot(normed, w_gate, preferred_element_type=jnp.float32)  26.3 us
    all_gather x1, waiting for transfers between devices, body(): every_beam = lax.all_gather(looked, 'batch', axis=0, tiled=True)  24.6 us
    dot_general x3, matrix products, layer_whole(): jnp.dot(attended, w_out, preferred_element_type=jnp.float32)  21.4 us
    dot_general x3, matrix products, project_three(): jnp.dot(normed, w_query, preferred_element_type=jnp.float32)  19.6 us
  transfers between devices with their start and end apart: 12, of which 11 were waited for; matrix products, arithmetic and copies ran while one was open for 3% of the time, Pallas kernels for 0%

commit v1 on v0

v1 whole, which is shorter than its diff:
```python
import functools

import jax
import jax.numpy as jnp
import numpy as np
from jax import lax
from jax.experimental import pallas as pl
from jax.experimental.pallas import tpu as pltpu
from jax.sharding import PartitionSpec as P

HEAD_DIM = 128
EPSILON = 1e-05
ROTARY_FREQ_BASE = 10000.0
BOTH = ("section", "tensor")
WIDE = 256
VMEM_LIMIT = 50 * 2**20


def rms_norm(hidden, scale_gain):
    values = hidden.astype(jnp.float32)
    inverse = lax.rsqrt(jnp.mean(values * values, axis=-1, keepdims=True) + EPSILON)
    return (values * inverse * scale_gain.astype(jnp.float32)).astype(jnp.bfloat16)


def rope_tables(length):
    half_dim = HEAD_DIM // 2
    frequency = ROTARY_FREQ_BASE ** (-(np.arange(half_dim, dtype=np.float64) / half_dim))
    angles = np.arange(length, dtype=np.float64)[:, None] * frequency[None, :]
    cosine, sine = np.cos(angles), np.sin(angles)
    cosine = np.concatenate([cosine, cosine], axis=1).astype(np.float32)
    sine = np.concatenate([-sine, sine], axis=1).astype(np.float32)
    return cosine, sine


def dot(left, right):
    return jnp.dot(left, right, preferred_element_type=jnp.float32)


def split_refs(refs, pieces):
    return refs[:pieces], refs[pieces : 2 * pieces], refs[2 * pieces :]


def attention_kernel(pieces, cos_ref, sin_ref, row_ref, col_ref, wq_ref, wk_ref, wv_ref, wo_ref, *refs):
    x_refs, out_refs, (x_all, total) = split_refs(refs, pieces)
    step = pl.program_id(0)
    share = x_refs[0].shape[0]

    @pl.when(step == 0)
    def _():
        for j in range(pieces):
            x_all[j * share : (j + 1) * share, :] = x_refs[j][...]

    x = x_all[...]
    cosine, sine = cos_ref[...], sin_ref[...]
    visible = row_ref[...] >= col_ref[...]
    query, key, value = dot(x, wq_ref[0]), dot(x, wk_ref[0]), dot(x, wv_ref[0])
    value = value.astype(jnp.bfloat16)
    outs = []
    for head in range(query.shape[1] // HEAD_DIM):
        cut = slice(head * HEAD_DIM, (head + 1) * HEAD_DIM)
        q, k, v = query[:, cut], key[:, cut], value[:, cut]
        q = (q * cosine + pltpu.roll(q, HEAD_DIM // 2, 1) * sine).astype(jnp.bfloat16)
        k = (k * cosine + pltpu.roll(k, HEAD_DIM // 2, 1) * sine).astype(jnp.bfloat16)
        scores = lax.dot_general(
            q, k, (((1,), (1,)), ((), ())), preferred_element_type=jnp.float32
        ) * HEAD_DIM ** (-0.5)
        scores = jnp.where(visible, scores, -jnp.inf)
        scores = jnp.exp(scores - jnp.max(scores, axis=-1, keepdims=True))
        probs = scores / jnp.sum(scores, axis=-1, keepdims=True)
        outs.append(dot(probs.astype(jnp.bfloat16), v).astype(jnp.bfloat16))
    part = dot(jnp.concatenate(outs, axis=1), wo_ref[0])

    @pl.when(step == 0)
    def _():
        total[...] = part

    @pl.when(step > 0)
    def _():
        total[...] += part

    @pl.when(step == pl.num_programs(0) - 1)
    def _():
        for j in range(pieces):
            out_refs[j][...] = total[j * share : (j + 1) * share, :].astype(jnp.bfloat16)


def mlp_kernel(pieces, wg_ref, wu_ref, wd_ref, *refs):
    x_refs, out_refs, (x_all, total) = split_refs(refs, pieces)
    step = pl.program_id(0)
    share = x_refs[0].shape[0]

    @pl.when(step == 0)
    def _():
        for j in range(pieces):
            x_all[j * share : (j + 1) * share, :] = x_refs[j][...]

    x = x_all[...]
    gate, up = dot(x, wg_ref[0]), dot(x, wu_ref[0])
    inner = (gate / (1.0 + jnp.exp(-gate)) * up).astype(jnp.bfloat16)
    part = dot(inner, wd_ref[0])

    @pl.when(step == 0)
    def _():
        total[...] = part

    @pl.when(step > 0)
    def _():
        total[...] += part

    @pl.when(step == pl.num_programs(0) - 1)
    def _():
        for j in range(pieces):
            out_refs[j][...] = total[j * share : (j + 1) * share, :].astype(jnp.bfloat16)


def whole(array):
    return pl.BlockSpec(array.shape, lambda i: (0,) * array.ndim)


def fused(kernel, name, tables, by_columns, by_rows, pieces):
    share, width = pieces[0].shape
    length = share * len(pieces)
    hidden = by_rows.shape[1]
    wide = min(WIDE, hidden)
    weights = list(by_columns) + [by_rows]
    flops = 2 * length * sum(w.size for w in weights)
    traffic = 2 * sum(w.size for w in weights) + 4 * length * width
    return pl.pallas_call(
        functools.partial(kernel, len(pieces)),
        out_shape=[jax.ShapeDtypeStruct((share, width), jnp.bfloat16) for _ in pieces],
        grid=(hidden // wide,),
        in_specs=[whole(t) for t in tables]
        + [pl.BlockSpec((1, width, wide), lambda i: (0, 0, i)) for _ in by_columns]
        + [pl.BlockSpec((1, wide, width), lambda i: (0, i, 0))]
        + [whole(p) for p in pieces],
        out_specs=[pl.BlockSpec((share, width), lambda i: (0, 0)) for _ in pieces],
        scratch_shapes=[
            pltpu.VMEM((length, width), jnp.bfloat16),
            pltpu.VMEM((length, width), jnp.float32),
        ],
        compiler_params=pltpu.CompilerParams(
            dimension_semantics=("arbitrary",), vmem_limit_bytes=VMEM_LIMIT
        ),
        cost_estimate=pl.CostEstimate(flops=flops, bytes_accessed=traffic, transcendentals=0),
        name=name,
    )(*tables, *weights, *pieces)


def distances(count):
    return [1 << bit for bit in range(count.bit_length() - 1)]


def swap(value, distance):
    count = lax.axis_size("tensor")
    return lax.ppermute(value, "tensor", [(z, z ^ distance) for z in range(count)])


def gather_rows(own):
    count = lax.axis_size("tensor")
    got = {0: own}
    for distance in reversed(distances(count)):
        for j in list(got):
            got[j ^ distance] = swap(got[j], distance)
    return [got[j] for j in range(count)]


def scatter_rows(partial):
    count = lax.axis_size("tensor")
    held = {j: piece for j, piece in enumerate(partial)}
    for distance in distances(count):
        for j in [j for j in held if j & distance][::-1]:
            part = swap(held.pop(j).astype(jnp.bfloat16), distance)
            base = held[j ^ distance].astype(jnp.float32)
            held[j ^ distance] = base + part.astype(jnp.float32)
    return held[0].astype(jnp.float32)


def body(
    ids_beam,
    beam_map,
    lengths,
    embed_table,
    gain_attn,
    w_query,
    w_key,
    w_value,
    w_out,
    gain_mlp,
    w_gate,
    w_up,
    w_down,
    final_gain,
    score_weight,
):
    section, tensor = lax.axis_index("section"), lax.axis_index("tensor")
    sections, tensors = lax.axis_size("section"), lax.axis_size("tensor")
    batch, batches = lax.axis_index("batch"), lax.axis_size("batch")
    per_device, length = ids_beam.shape
    share = length // tensors
    slots = jnp.arange(tensors, dtype=jnp.int32) ^ tensor

    owned = batch * per_device + jnp.arange(per_device, dtype=jnp.int32)
    beams_owned = jnp.take(beam_map, owned)
    lengths_owned = jnp.take(lengths, owned)
    blocks = [ids_beam]
    for steps in range(1, batches):
        blocks.append(
            lax.ppermute(ids_beam, "batch", [(b, (b + steps) % batches) for b in range(batches)])
        )
    blocks = jnp.concatenate(blocks, axis=0)
    holder = (batch - beams_owned // per_device) % batches
    tokens = blocks[holder * per_device + beams_owned % per_device]

    cosine, sine = rope_tables(length)
    by_slot = lambda t: jnp.asarray(t.reshape(tensors, share, -1))[slots].reshape(length, -1)
    cosine, sine = by_slot(cosine), by_slot(sine)
    positions = (slots[:, None] * share + jnp.arange(share, dtype=jnp.int32)).reshape(length)
    tables = (cosine, sine, positions[:, None], positions[None, :])

    hidden, first = [], []
    for c in range(per_device):
        looked = jnp.take(embed_table, tokens[c], axis=0)
        columns = []
        for source in range(sections):
            pieces = []
            for j in range(tensors):
                if source == 0 and j == 0:
                    pieces.append(looked)
                    continue
                links = [(source * tensors + z, z ^ j) for z in range(tensors)]
                pieces.append(lax.ppermute(looked, BOTH, links))
            pieces = jnp.stack(pieces)
            columns += [
                lax.dynamic_index_in_dim(pieces, z ^ tensor, 0, False) for z in range(tensors)
            ]
        embedded = jnp.concatenate(columns, axis=1)
        normed = rms_norm(embedded, gain_attn)
        first.append(
            [lax.dynamic_slice_in_dim(normed, slots[j] * share, share, 0) for j in range(tensors)]
        )
        hidden.append(lax.dynamic_slice_in_dim(embedded, tensor * share, share, 0))

    for layer in range(sections):
        for c in range(per_device):
            if layer == 0:
                pieces = first[c]
            else:
                links = [(layer - 1, layer)]
                hidden[c] = lax.ppermute(hidden[c], "section", links)
                pieces = gather_rows(rms_norm(hidden[c], gain_attn))
            partial = fused(
                attention_kernel, "attention", tables, (w_query, w_key, w_value), w_out, pieces
            )
            attn_sum = scatter_rows(partial)
            middle = (hidden[c].astype(jnp.float32) + attn_sum).astype(jnp.bfloat16)
            pieces = gather_rows(rms_norm(middle, gain_mlp))
            partial = fused(mlp_kernel, "mlp", (), (w_gate, w_up), w_down, pieces)
            mlp_sum = scatter_rows(partial)
            hidden[c] = (middle.astype(jnp.float32) + mlp_sum).astype(jnp.bfloat16)

    finals = jnp.stack(hidden)
    last = sections - 1
    half = finals.shape[2] // sections
    shown = lax.dynamic_slice_in_dim(finals, section * half, half, 2)
    for target in range(last):
        part = lax.ppermute(
            finals[:, :, target * half : (target + 1) * half], "section", [(last, target)]
        )
        shown = jnp.where(section == target, part, shown)

    at = lengths_owned - 1 - tensor * share
    owner = (at >= 0) & (at < share) & (section == last)
    row = jnp.take_along_axis(finals, jnp.clip(at, 0, share - 1)[:, None, None], axis=1)
    values = row[:, 0].astype(jnp.float32)
    inverse = lax.rsqrt(jnp.mean(values * values, axis=-1, keepdims=True) + EPSILON)
    score = jnp.sum(
        values * inverse * final_gain.astype(jnp.float32) * score_weight.astype(jnp.float32),
        axis=-1,
    )
    score = jnp.where(owner, score, 0.0)
    devices = sections * tensors
    total = score
    for steps in range(1, devices):
        total = total + lax.ppermute(
            score, BOTH, [(d, (d + steps) % devices) for d in range(devices)]
        )
    return (shown, total)


def solution(mesh):
    placed = (
        P("batch", None),
        P(),
        P(),
        P(None, ("section", "tensor")),
        P("section", None),
        P("section", None, "tensor"),
        P("section", None, "tensor"),
        P("section", None, "tensor"),
        P("section", "tensor", None),
        P("section", None),
        P("section", None, "tensor"),
        P("section", None, "tensor"),
        P("section", "tensor", None),
        P(),
        P(),
    )
    return jax.shard_map(
        body,
        mesh=mesh,
        in_specs=placed,
        out_specs=(P("batch", "tensor", "section"), P("batch")),
        check_vma=False,
    )
```

time: 961 us -> 737 us (0.77)
  waiting for transfers between devices: 690 us -> 390 us
  Pallas kernels: 0 us -> 186 us
  matrix products: 157 us -> 0 us
  starting transfers between devices: 11.4 us -> 97.9 us
  other arithmetic: 37.3 us -> 18 us
  local copies, waits for them, and re-layouts: 44.8 us -> 30.9 us
  between operations: 15.2 us -> 4.68 us
    psum x6 -> x0, waiting for transfers between devices: 513 us -> none  [tensor_total(): lax.psum(term_rows.astype(jnp.bfloat16), 'tensor').astype(jnp.float32)]
    ppermute x4 -> x69, waiting for transfers between devices: 100 us -> 390 us  [the longest x42 354 us: swap(): lax.ppermute(value, 'tensor', [(z, z ^ distance) for z in range(count)])]
    pallas_call x0 -> x8, Pallas kernels: none -> 186 us  [fused(): pl.pallas_call(functools.partial(kernel, len(pieces)), out_shape=[jax.Sha...]
    dot_general x24 -> x0, matrix products: 148 us -> none  [the longest x3 35.1 us: layer_whole(): jnp.dot(inner_act, w_down, preferred_element_type=jnp.float32)]
    ppermute x4 -> x69, starting transfers between devices: 10.2 us -> 97.9 us  [the longest x42 44.4 us: swap(): lax.ppermute(value, 'tensor', [(z, z ^ distance) for z in range(count)])]
    all_gather x2 -> x0, waiting for transfers between devices: 76.5 us -> none  [the longest x1 51.9 us: body(): embedded = lax.all_gather(picked, ('section', 'tensor'), axis=2, tiled=True)]
    dot_general x2 -> x0, local copies, waits for them, and re-layouts: 22.7 us -> none  [the longest x1 11.4 us: project_three(): jnp.dot(normed, w_query, preferred_element_type=jnp.float32)]
    gather x3 -> x9, local copies, waits for them, and re-layouts: 13.5 us -> 23.5 us  [the longest x2 18 us: body(): looked = jnp.take(embed_table, tokens[c], axis=0)]
  transfers between devices with their start and end apart: 12 -> 69, of which waited for: 11 -> 29; matrix products, arithmetic and copies ran while one was open for 3% -> 4% of each run, Pallas kernels for 0% -> 22%
where the time goes in v1:
time: 737 us; the launch traced here: 727 us
  waiting for transfers between devices  390 us (53%)
  Pallas kernels  186 us (25%)
  starting transfers between devices  97.9 us (13%)
  local copies, waits for them, and re-layouts  30.9 us (4%)
  other arithmetic  18 us (2%)
    ppermute x42, waiting for transfers between devices, swap(): lax.ppermute(value, 'tensor', [(z, z ^ distance) for z in range(count)])  354 us
    pallas_call x8, Pallas kernels, fused(): pl.pallas_call(functools.partial(kernel, len(pieces)), out_shape=[jax.Sha...  186 us
    ppermute x42, starting transfers between devices, swap(): lax.ppermute(value, 'tensor', [(z, z ^ distance) for z in range(count)])  44.4 us
    ppermute x14, starting transfers between devices, body(): pieces.append(lax.ppermute(looked, BOTH, links))  31.6 us
    ppermute x14, waiting for transfers between devices, body(): pieces.append(lax.ppermute(looked, BOTH, links))  24 us
    gather x2, local copies, waits for them, and re-layouts, body(): looked = jnp.take(embed_table, tokens[c], axis=0)  18 us
  transfers between devices with their start and end apart: 69, of which 29 were waited for; matrix products, arithmetic and copies ran while one was open for 4% of the time, Pallas kernels for 22%

profile of v1, /device:TPU:0, one launch (start us, length us, event | category | flops | bytes accessed | tf_op | source)
XLA Modules:
  0.0 727.4 jit_solution(9279443363131900295)
XLA Ops:
  14.4 9.0 %gather_fusion.5 = bf16[256,512]{1,0:T(8,128)(2,1)S(1)} fusion(bf16[16000,512]{1,0:T(8,128)(2,1)} %param.24, s32[1024]{0:T(1024)S(1)} %pad_clamp_fusion.2), kind=kCustom, calls=%fused_computation.1.clone | custom fusion | bytes 525312 | tf_op jit(solution)/shard_map/jit(_take)/gather | solution.py:222
  36.4 9.0 %gather_fusion.6 = bf16[256,512]{1,0:T(8,128)(2,1)S(1)} fusion(bf16[16000,512]{1,0:T(8,128)(2,1)} %param.24, s32[1024]{0:T(1024)S(1)} %pad_clamp_fusion), kind=kCustom, calls=%fused_computation.3.clone | custom fusion | bytes 525312 | tf_op jit(solution)/shard_map/jit(_take)/gather | solution.py:222
  67.5 11.2 %collective-permute-done.33 = bf16[256,512]{1,0:T(8,128)(2,1)S(1)} collective-permute-done((bf16[256,512]{1,0:T(8,128)(2,1)S(1)}, bf16[256,512]{1,0:T(8,128)(2,1)S(1)}, u32[]{:S(2)}, u32[]{:S(2)}) %collective-permute-start.33) | collective-permute-done | bytes 262176 | tf_op jit(solution)/shard_map/ppermute | solution.py:231
  80.9 9.0 %collective-permute-done.37 = bf16[256,512]{1,0:T(8,128)(2,1)S(1)} collective-permute-done((bf16[256,512]{1,0:T(8,128)(2,1)S(1)}, bf16[256,512]{1,0:T(8,128)(2,1)S(1)}, u32[]{:S(2)}, u32[]{:S(2)}) %collective-permute-start.37) | collective-permute-done | bytes 262176 | tf_op jit(solution)/shard_map/ppermute | solution.py:231
  93.5 22.3 %attention.4 = (bf16[64,4096]{1,0:T(8,128)(2,1)S(1)}, bf16[64,4096]{1,0:T(8,128)(2,1)S(1)}, bf16[64,4096]{1,0:T(8,128)(2,1)S(1)}, bf16[64,4096]{1,0:T(8,128)(2,1)S(1)}) custom-call(f32[256,128]{1,0:T(8,128)S(1)} %bitcast.69, f32[256,128]{1,0:T(8,128)S(1)} %bitcast.73, s32[256,1]{1,0:T(8,128)S(1)} %add.399.row_ref, s32[1,256]{1,0:T(1,128)S(1)} %add.335.col_ref, ...), custom_call_target="tpu_custom_call" | custom-call | flops 8589934592 | bytes 37748736 | tf_op jit(solution)/shard_map/attention/pallas_call | solution.py:128
  121.8 21.8 %attention.6 = (bf16[64,4096]{1,0:T(8,128)(2,1)S(1)}, bf16[64,4096]{1,0:T(8,128)(2,1)S(1)}, bf16[64,4096]{1,0:T(8,128)(2,1)S(1)}, bf16[64,4096]{1,0:T(8,128)(2,1)S(1)}) custom-call(f32[256,128]{1,0:T(8,128)S(1)} %bitcast.70, f32[256,128]{1,0:T(8,128)S(1)} %bitcast.74, s32[256,1]{1,0:T(8,128)S(1)} %add.399.row_ref, s32[1,256]{1,0:T(1,128)S(1)} %add.335.col_ref, ...), custom_call_target="tpu_custom_call" | custom-call | flops 8589934592 | bytes 37748736 | tf_op jit(solution)/shard_map/attention/pallas_call | solution.py:128
  149.1 21.1 %collective-permute-done.40 = bf16[64,4096]{1,0:T(8,128)(2,1)S(1)} collective-permute-done((bf16[64,4096]{1,0:T(8,128)(2,1)S(1)}, bf16[64,4096]{1,0:T(8,128)(2,1)S(1)}, u32[]{:S(2)}, u32[]{:S(2)}) %collective-permute-start.40) | collective-permute-done | bytes 524320 | tf_op jit(solution)/shard_map/ppermute | solution.py:155
  182.3 18.1 %collective-permute-done.41 = bf16[64,4096]{1,0:T(8,128)(2,1)} collective-permute-done((bf16[64,4096]{1,0:T(8,128)(2,1)}, bf16[64,4096]{1,0:T(8,128)(2,1)}, u32[]{:S(2)}, u32[]{:S(2)}) %collective-permute-start.41) | collective-permute-done | bytes 524320 | tf_op jit(solution)/shard_map/ppermute | solution.py:155
  205.4 31.4 %collective-permute-done.14.refs_2_ = bf16[64,4096]{1,0:T(8,128)(2,1)S(1)} collective-permute-done((bf16[64,4096]{1,0:T(8,128)(2,1)S(1)}, bf16[64,4096]{1,0:T(8,128)(2,1)S(1)}, u32[]{:S(2)}, u32[]{:S(2)}) %collective-permute-start.14) | collective-permute-done | bytes 524320 | tf_op jit(solution)/shard_map/ppermute | solution.py:155
  238.8 9.2 %collective-permute-done.43.refs_2_ = bf16[64,4096]{1,0:T(8,128)(2,1)S(1)} collective-permute-done((bf16[64,4096]{1,0:T(8,128)(2,1)S(1)}, bf16[64,4096]{1,0:T(8,128)(2,1)S(1)}, u32[]{:S(2)}, u32[]{:S(2)}) %collective-permute-start.43) | collective-permute-done | bytes 524320 | tf_op jit(solution)/shard_map/ppermute | solution.py:155
  248.0 11.2 %collective-permute-done.15.refs_3_ = bf16[64,4096]{1,0:T(8,128)(2,1)S(1)} collective-permute-done((bf16[64,4096]{1,0:T(8,128)(2,1)S(1)}, bf16[64,4096]{1,0:T(8,128)(2,1)S(1)}, u32[]{:S(2)}, u32[]{:S(2)}) %collective-permute-start.15) | collective-permute-done | bytes 524320 | tf_op jit(solution)/shard_map/ppermute | solution.py:155
  260.0 24.5 %mlp.4 = (bf16[64,4096]{1,0:T(8,128)(2,1)S(1)}, bf16[64,4096]{1,0:T(8,128)(2,1)S(1)}, bf16[64,4096]{1,0:T(8,128)(2,1)S(1)}, bf16[64,4096]{1,0:T(8,128)(2,1)S(1)}) custom-call(bf16[1,4096,2048]{2,1,0:T(8,128)(2,1)} %wg_ref.7, bf16[1,4096,2048]{2,1,0:T(8,128)(2,1)} %wu_ref.7, bf16[1,2048,4096]{2,1,0:T(8,128)(2,1)} %wd_ref.7, ...), custom_call_target="tpu_custom_call" | custom-call | flops 12884901888 | bytes 54525952 | tf_op jit(solution)/shard_map/mlp/pallas_call | solution.py:128
  287.4 24.3 %mlp.6 = (bf16[64,4096]{1,0:T(8,128)(2,1)S(1)}, bf16[64,4096]{1,0:T(8,128)(2,1)S(1)}, bf16[64,4096]{1,0:T(8,128)(2,1)S(1)}, bf16[64,4096]{1,0:T(8,128)(2,1)S(1)}) custom-call(bf16[1,4096,2048]{2,1,0:T(8,128)(2,1)} %wg_ref.7, bf16[1,4096,2048]{2,1,0:T(8,128)(2,1)} %wu_ref.7, bf16[1,2048,4096]{2,1,0:T(8,128)(2,1)} %wd_ref.7, ...), custom_call_target="tpu_custom_call" | custom-call | flops 12884901888 | bytes 54525952 | tf_op jit(solution)/shard_map/mlp/pallas_call | solution.py:128
  315.2 22.6 %collective-permute-done.46 = bf16[64,4096]{1,0:T(8,128)(2,1)S(1)} collective-permute-done((bf16[64,4096]{1,0:T(8,128)(2,1)S(1)}, bf16[64,4096]{1,0:T(8,128)(2,1)S(1)}, u32[]{:S(2)}, u32[]{:S(2)}) %collective-permute-start.46) | collective-permute-done | bytes 524320 | tf_op jit(solution)/shard_map/ppermute | solution.py:155
  338.7 7.9 %collective-permute-done.18 = bf16[64,4096]{1,0:T(8,128)(2,1)S(1)} collective-permute-done((bf16[64,4096]{1,0:T(8,128)(2,1)S(1)}, bf16[64,4096]{1,0:T(8,128)(2,1)S(1)}, u32[]{:S(2)}, u32[]{:S(2)}) %collective-permute-start.18) | collective-permute-done | bytes 524320 | tf_op jit(solution)/shard_map/ppermute | solution.py:155
  348.8 22.0 %collective-permute-done.47 = bf16[64,4096]{1,0:T(8,128)(2,1)S(1)} collective-permute-done((bf16[64,4096]{1,0:T(8,128)(2,1)S(1)}, bf16[64,4096]{1,0:T(8,128)(2,1)S(1)}, u32[]{:S(2)}, u32[]{:S(2)}) %collective-permute-start.47) | collective-permute-done | bytes 524320 | tf_op jit(solution)/shard_map/ppermute | solution.py:155
  372.5 11.3 %collective-permute-done.48 = bf16[64,4096]{1,0:T(8,128)(2,1)S(1)} collective-permute-done((bf16[64,4096]{1,0:T(8,128)(2,1)S(1)}, bf16[64,4096]{1,0:T(8,128)(2,1)S(1)}, u32[]{:S(2)}, u32[]{:S(2)}) %collective-permute-start.48) | collective-permute-done | bytes 524320 | tf_op jit(solution)/shard_map/ppermute | solution.py:249
  387.4 32.2 %collective-permute-done.21.refs_2_ = bf16[64,4096]{1,0:T(8,128)(2,1)S(1)} collective-permute-done((bf16[64,4096]{1,0:T(8,128)(2,1)S(1)}, bf16[64,4096]{1,0:T(8,128)(2,1)S(1)}, u32[]{:S(2)}, u32[]{:S(2)}) %collective-permute-start.21) | collective-permute-done | bytes 524320 | tf_op jit(solution)/shard_map/ppermute | solution.py:155
  421.6 9.2 %collective-permute-done.50.refs_2_ = bf16[64,4096]{1,0:T(8,128)(2,1)S(1)} collective-permute-done((bf16[64,4096]{1,0:T(8,128)(2,1)S(1)}, bf16[64,4096]{1,0:T(8,128)(2,1)S(1)}, u32[]{:S(2)}, u32[]{:S(2)}) %collective-permute-start.50) | collective-permute-done | bytes 524320 | tf_op jit(solution)/shard_map/ppermute | solution.py:155
  430.8 11.2 %collective-permute-done.22.refs_3_ = bf16[64,4096]{1,0:T(8,128)(2,1)S(1)} collective-permute-done((bf16[64,4096]{1,0:T(8,128)(2,1)S(1)}, bf16[64,4096]{1,0:T(8,128)(2,1)S(1)}, u32[]{:S(2)}, u32[]{:S(2)}) %collective-permute-start.22) | collective-permute-done | bytes 524320 | tf_op jit(solution)/shard_map/ppermute | solution.py:155
  442.8 22.0 %attention.5 = (bf16[64,4096]{1,0:T(8,128)(2,1)S(1)}, bf16[64,4096]{1,0:T(8,128)(2,1)S(1)}, bf16[64,4096]{1,0:T(8,128)(2,1)S(1)}, bf16[64,4096]{1,0:T(8,128)(2,1)S(1)}) custom-call(f32[256,128]{1,0:T(8,128)S(1)} %bitcast.71, f32[256,128]{1,0:T(8,128)S(1)} %bitcast.75, s32[256,1]{1,0:T(8,128)S(1)} %add.399.row_ref, s32[1,256]{1,0:T(1,128)S(1)} %add.335.col_ref, ...), custom_call_target="tpu_custom_call" | custom-call | flops 8589934592 | bytes 37748736 | tf_op jit(solution)/shard_map/attention/pallas_call | solution.py:128
  467.8 21.8 %attention.7 = (bf16[64,4096]{1,0:T(8,128)(2,1)S(1)}, bf16[64,4096]{1,0:T(8,128)(2,1)S(1)}, bf16[64,4096]{1,0:T(8,128)(2,1)S(1)}, bf16[64,4096]{1,0:T(8,128)(2,1)S(1)}) custom-call(f32[256,128]{1,0:T(8,128)S(1)} %bitcast.72, f32[256,128]{1,0:T(8,128)S(1)} %bitcast.76, s32[256,1]{1,0:T(8,128)S(1)} %add.399.row_ref, s32[1,256]{1,0:T(1,128)S(1)} %add.335.col_ref, ...), custom_call_target="tpu_custom_call" | custom-call | flops 8589934592 | bytes 37748736 | tf_op jit(solution)/shard_map/attention/pallas_call | solution.py:128
  493.2 22.6 %collective-permute-done.53 = bf16[64,4096]{1,0:T(8,128)(2,1)S(1)} collective-permute-done((bf16[64,4096]{1,0:T(8,128)(2,1)S(1)}, bf16[64,4096]{1,0:T(8,128)(2,1)S(1)}, u32[]{:S(2)}, u32[]{:S(2)}) %collective-permute-start.53) | collective-permute-done | bytes 524320 | tf_op jit(solution)/shard_map/ppermute | solution.py:155
  516.7 7.9 %collective-permute-done.25 = bf16[64,4096]{1,0:T(8,128)(2,1)S(1)} collective-permute-done((bf16[64,4096]{1,0:T(8,128)(2,1)S(1)}, bf16[64,4096]{1,0:T(8,128)(2,1)S(1)}, u32[]{:S(2)}, u32[]{:S(2)}) %collective-permute-start.25) | collective-permute-done | bytes 524320 | tf_op jit(solution)/shard_map/ppermute | solution.py:155
  525.6 23.1 %collective-permute-done.54 = bf16[64,4096]{1,0:T(8,128)(2,1)S(1)} collective-permute-done((bf16[64,4096]{1,0:T(8,128)(2,1)S(1)}, bf16[64,4096]{1,0:T(8,128)(2,1)S(1)}, u32[]{:S(2)}, u32[]{:S(2)}) %collective-permute-start.54) | collective-permute-done | bytes 524320 | tf_op jit(solution)/shard_map/ppermute | solution.py:155
  553.2 21.8 %collective-permute-done.56.refs_2_ = bf16[64,4096]{1,0:T(8,128)(2,1)S(1)} collective-permute-done((bf16[64,4096]{1,0:T(8,128)(2,1)S(1)}, bf16[64,4096]{1,0:T(8,128)(2,1)S(1)}, u32[]{:S(2)}, u32[]{:S(2)}) %collective-permute-start.56) | collective-permute-done | bytes 524320 | tf_op jit(solution)/shard_map/ppermute | solution.py:155
  577.4 19.4 %collective-permute-done.27.refs_2_ = bf16[64,4096]{1,0:T(8,128)(2,1)S(1)} collective-permute-done((bf16[64,4096]{1,0:T(8,128)(2,1)S(1)}, bf16[64,4096]{1,0:T(8,128)(2,1)S(1)}, u32[]{:S(2)}, u32[]{:S(2)}) %collective-permute-start.27) | collective-permute-done | bytes 524320 | tf_op jit(solution)/shard_map/ppermute | solution.py:155
  601.0 24.5 %mlp.7 = (bf16[64,4096]{1,0:T(8,128)(2,1)S(1)}, bf16[64,4096]{1,0:T(8,128)(2,1)S(1)}, bf16[64,4096]{1,0:T(8,128)(2,1)S(1)}, bf16[64,4096]{1,0:T(8,128)(2,1)S(1)}) custom-call(bf16[1,4096,2048]{2,1,0:T(8,128)(2,1)} %wg_ref.7, bf16[1,4096,2048]{2,1,0:T(8,128)(2,1)} %wu_ref.7, bf16[1,2048,4096]{2,1,0:T(8,128)(2,1)} %wd_ref.7, ...), custom_call_target="tpu_custom_call" | custom-call | flops 12884901888 | bytes 54525952 | tf_op jit(solution)/shard_map/mlp/pallas_call | solution.py:128
  628.5 24.3 %mlp.5 = (bf16[64,4096]{1,0:T(8,128)(2,1)S(1)}, bf16[64,4096]{1,0:T(8,128)(2,1)S(1)}, bf16[64,4096]{1,0:T(8,128)(2,1)S(1)}, bf16[64,4096]{1,0:T(8,128)(2,1)S(1)}) custom-call(bf16[1,4096,2048]{2,1,0:T(8,128)(2,1)} %wg_ref.7, bf16[1,4096,2048]{2,1,0:T(8,128)(2,1)} %wu_ref.7, bf16[1,2048,4096]{2,1,0:T(8,128)(2,1)} %wd_ref.7, ...), custom_call_target="tpu_custom_call" | custom-call | flops 12884901888 | bytes 54525952 | tf_op jit(solution)/shard_map/mlp/pallas_call | solution.py:128
  656.2 23.2 %collective-permute-done.30 = bf16[64,4096]{1,0:T(8,128)(2,1)S(1)} collective-permute-done((bf16[64,4096]{1,0:T(8,128)(2,1)S(1)}, bf16[64,4096]{1,0:T(8,128)(2,1)S(1)}, u32[]{:S(2)}, u32[]{:S(2)}) %collective-permute-start.30) | collective-permute-done | bytes 524320 | tf_op jit(solution)/shard_map/ppermute | solution.py:155
  679.7 8.2 %collective-permute-done.60 = bf16[64,4096]{1,0:T(8,128)(2,1)S(1)} collective-permute-done((bf16[64,4096]{1,0:T(8,128)(2,1)S(1)}, bf16[64,4096]{1,0:T(8,128)(2,1)S(1)}, u32[]{:S(2)}, u32[]{:S(2)}) %collective-permute-start.60) | collective-permute-done | bytes 524320 | tf_op jit(solution)/shard_map/ppermute | solution.py:155
  688.1 19.9 %collective-permute-done.31 = bf16[64,4096]{1,0:T(8,128)(2,1)S(1)} collective-permute-done((bf16[64,4096]{1,0:T(8,128)(2,1)S(1)}, bf16[64,4096]{1,0:T(8,128)(2,1)S(1)}, u32[]{:S(2)}, u32[]{:S(2)}) %collective-permute-start.31) | collective-permute-done | bytes 524320 | tf_op jit(solution)/shard_map/ppermute | solution.py:155
  (249 shorter events, 145.4 us)
Async XLA Ops:
  115.8 29.9 %collective-permute-start.11 = (bf16[64,4096]{1,0:T(8,128)(2,1)S(1)}, bf16[64,4096]{1,0:T(8,128)(2,1)S(1)}, u32[]{:S(2)}, u32[]{:S(2)}) collective-permute-start(bf16[64,4096]{1,0:T(8,128)(2,1)S(1)} %get-tuple-element.39), channel_id=1, source_target_pairs={{0,1},{1,0},{2,3},{3,2},{4,5},{5,4},{6,7},{7,6},{8,9},{9,8},{10,11... | collective-permute-start | bytes 1572872 | tf_op jit(solution)/shard_map/ppermute | solution.py:155
  120.7 53.5 %collective-permute-start.10 = (bf16[64,4096]{1,0:T(8,128)(2,1)S(1)}, bf16[64,4096]{1,0:T(8,128)(2,1)S(1)}, u32[]{:S(2)}, u32[]{:S(2)}) collective-permute-start(bf16[64,4096]{1,0:T(8,128)(2,1)S(1)} %get-tuple-element.37), channel_id=1, source_target_pairs={{0,1},{1,0},{2,3},{3,2},{4,5},{5,4},{6,7},{7,6},{8,9},{9,8},{10,11... | collective-permute-start | bytes 1572872 | tf_op jit(solution)/shard_map/ppermute | solution.py:155
  145.6 36.7 %collective-permute-start.39 = (bf16[64,4096]{1,0:T(8,128)(2,1)S(1)}, bf16[64,4096]{1,0:T(8,128)(2,1)S(1)}, u32[]{:S(2)}, u32[]{:S(2)}) collective-permute-start(bf16[64,4096]{1,0:T(8,128)(2,1)S(1)} %get-tuple-element.53), channel_id=1, source_target_pairs={{0,1},{1,0},{2,3},{3,2},{4,5},{5,4},{6,7},{7,6},{8,9},{9,8},{10,11... | collective-permute-start | bytes 1572872 | tf_op jit(solution)/shard_map/ppermute | solution.py:155
  146.6 34.0 %collective-permute-start.12 = (bf16[64,4096]{1,0:T(8,128)(2,1)}, bf16[64,4096]{1,0:T(8,128)(2,1)}, u32[]{:S(2)}, u32[]{:S(2)}) collective-permute-start(bf16[64,4096]{1,0:T(8,128)(2,1)} %add_convert_fusion.9), channel_id=1, source_target_pairs={{0,2},{1,3},{2,0},{3,1},{4,6},{5,7},{6,4},{7,5},{8,10},{9,11},{10,... | collective-permute-start | bytes 1572872 | tf_op jit(solution)/shard_map/ppermute | solution.py:155
  171.1 29.3 %collective-permute-start.41 = (bf16[64,4096]{1,0:T(8,128)(2,1)}, bf16[64,4096]{1,0:T(8,128)(2,1)}, u32[]{:S(2)}, u32[]{:S(2)}) collective-permute-start(bf16[64,4096]{1,0:T(8,128)(2,1)} %add_convert_fusion.4), channel_id=1, source_target_pairs={{0,2},{1,3},{2,0},{3,1},{4,6},{5,7},{6,4},{7,5},{8,10},{9,11},{10,... | collective-permute-start | bytes 1572872 | tf_op jit(solution)/shard_map/ppermute | solution.py:155
  202.4 34.4 %collective-permute-start.14 = (bf16[64,4096]{1,0:T(8,128)(2,1)S(1)}, bf16[64,4096]{1,0:T(8,128)(2,1)S(1)}, u32[]{:S(2)}, u32[]{:S(2)}) collective-permute-start(bf16[64,4096]{1,0:T(8,128)(2,1)S(1)} %get-tuple-element.93.refs_0_), channel_id=1, source_target_pairs={{0,2},{1,3},{2,0},{3,1},{4,6},{5,7},{6,4},{7,5},{8,10},{9,11},{10,... | collective-permute-start | bytes 1572872 | tf_op jit(solution)/shard_map/ppermute | solution.py:155
  202.4 45.5 %collective-permute-start.43 = (bf16[64,4096]{1,0:T(8,128)(2,1)S(1)}, bf16[64,4096]{1,0:T(8,128)(2,1)S(1)}, u32[]{:S(2)}, u32[]{:S(2)}) collective-permute-start(bf16[64,4096]{1,0:T(8,128)(2,1)S(1)} %get-tuple-element.92.refs_0_), channel_id=1, source_target_pairs={{0,2},{1,3},{2,0},{3,1},{4,6},{5,7},{6,4},{7,5},{8,10},{9,11},{10,... | collective-permute-start | bytes 1572872 | tf_op jit(solution)/shard_map/ppermute | solution.py:155
  205.4 42.6 %collective-permute-start.13 = (bf16[64,4096]{1,0:T(8,128)(2,1)S(1)}, bf16[64,4096]{1,0:T(8,128)(2,1)S(1)}, u32[]{:S(2)}, u32[]{:S(2)}) collective-permute-start(bf16[64,4096]{1,0:T(8,128)(2,1)S(1)} %get-tuple-element.93.refs_0_), channel_id=1, source_target_pairs={{0,1},{1,0},{2,3},{3,2},{4,5},{5,4},{6,7},{7,6},{8,9},{9,8},{10,11... | collective-permute-start | bytes 1572872 | tf_op jit(solution)/shard_map/ppermute | solution.py:155
  237.0 49.6 %collective-permute-start.42 = (bf16[64,4096]{1,0:T(8,128)(2,1)S(1)}, bf16[64,4096]{1,0:T(8,128)(2,1)S(1)}, u32[]{:S(2)}, u32[]{:S(2)}) collective-permute-start(bf16[64,4096]{1,0:T(8,128)(2,1)S(1)} %get-tuple-element.92.refs_0_), channel_id=1, source_target_pairs={{0,1},{1,0},{2,3},{3,2},{4,5},{5,4},{6,7},{7,6},{8,9},{9,8},{10,11... | collective-permute-start | bytes 1572872 | tf_op jit(solution)/shard_map/ppermute | solution.py:155
  248.0 38.6 %collective-permute-start.44 = (bf16[64,4096]{1,0:T(8,128)(2,1)S(1)}, bf16[64,4096]{1,0:T(8,128)(2,1)S(1)}, u32[]{:S(2)}, u32[]{:S(2)}) collective-permute-start(bf16[64,4096]{1,0:T(8,128)(2,1)S(1)} %collective-permute-done.43.refs_2_), channel_id=1, source_target_pairs={{0,1},{1,0},{2,3},{3,2},{4,5},{5,4},{6,7},{7,6},{8,9},{9,8},{10,11... | collective-permute-start | bytes 1572872 | tf_op jit(solution)/shard_map/ppermute | solution.py:155
  284.5 29.3 %collective-permute-start.17 = (bf16[64,4096]{1,0:T(8,128)(2,1)S(1)}, bf16[64,4096]{1,0:T(8,128)(2,1)S(1)}, u32[]{:S(2)}, u32[]{:S(2)}) collective-permute-start(bf16[64,4096]{1,0:T(8,128)(2,1)S(1)} %get-tuple-element.43), channel_id=1, source_target_pairs={{0,1},{1,0},{2,3},{3,2},{4,5},{5,4},{6,7},{7,6},{8,9},{9,8},{10,11... | collective-permute-start | bytes 1572872 | tf_op jit(solution)/shard_map/ppermute | solution.py:155
  284.5 54.2 %collective-permute-start.16 = (bf16[64,4096]{1,0:T(8,128)(2,1)S(1)}, bf16[64,4096]{1,0:T(8,128)(2,1)S(1)}, u32[]{:S(2)}, u32[]{:S(2)}) collective-permute-start(bf16[64,4096]{1,0:T(8,128)(2,1)S(1)} %get-tuple-element.41), channel_id=1, source_target_pairs={{0,1},{1,0},{2,3},{3,2},{4,5},{5,4},{6,7},{7,6},{8,9},{9,8},{10,11... | collective-permute-start | bytes 1572872 | tf_op jit(solution)/shard_map/ppermute | solution.py:155
  311.8 37.0 %collective-permute-start.45 = (bf16[64,4096]{1,0:T(8,128)(2,1)S(1)}, bf16[64,4096]{1,0:T(8,128)(2,1)S(1)}, u32[]{:S(2)}, u32[]{:S(2)}) collective-permute-start(bf16[64,4096]{1,0:T(8,128)(2,1)S(1)} %get-tuple-element.57), channel_id=1, source_target_pairs={{0,1},{1,0},{2,3},{3,2},{4,5},{5,4},{6,7},{7,6},{8,9},{9,8},{10,11... | collective-permute-start | bytes 1572872 | tf_op jit(solution)/shard_map/ppermute | solution.py:155
  313.9 32.8 %collective-permute-start.18 = (bf16[64,4096]{1,0:T(8,128)(2,1)S(1)}, bf16[64,4096]{1,0:T(8,128)(2,1)S(1)}, u32[]{:S(2)}, u32[]{:S(2)}) collective-permute-start(bf16[64,4096]{1,0:T(8,128)(2,1)S(1)} %add_convert_fusion.7), channel_id=1, source_target_pairs={{0,2},{1,3},{2,0},{3,1},{4,6},{5,7},{6,4},{7,5},{8,10},{9,11},{10,... | collective-permute-start | bytes 1572872 | tf_op jit(solution)/shard_map/ppermute | solution.py:155
  338.0 32.8 %collective-permute-start.47 = (bf16[64,4096]{1,0:T(8,128)(2,1)S(1)}, bf16[64,4096]{1,0:T(8,128)(2,1)S(1)}, u32[]{:S(2)}, u32[]{:S(2)}) collective-permute-start(bf16[64,4096]{1,0:T(8,128)(2,1)S(1)} %add_convert_fusion.2), channel_id=1, source_target_pairs={{0,2},{1,3},{2,0},{3,1},{4,6},{5,7},{6,4},{7,5},{8,10},{9,11},{10,... | collective-permute-start | bytes 1572872 | tf_op jit(solution)/shard_map/ppermute | solution.py:155
  384.4 35.2 %collective-permute-start.21 = (bf16[64,4096]{1,0:T(8,128)(2,1)S(1)}, bf16[64,4096]{1,0:T(8,128)(2,1)S(1)}, u32[]{:S(2)}, u32[]{:S(2)}) collective-permute-start(bf16[64,4096]{1,0:T(8,128)(2,1)S(1)} %get-tuple-element.91.refs_0_), channel_id=1, source_target_pairs={{0,2},{1,3},{2,0},{3,1},{4,6},{5,7},{6,4},{7,5},{8,10},{9,11},{10,... | collective-permute-start | bytes 1572872 | tf_op jit(solution)/shard_map/ppermute | solution.py:155
  384.4 46.4 %collective-permute-start.50 = (bf16[64,4096]{1,0:T(8,128)(2,1)S(1)}, bf16[64,4096]{1,0:T(8,128)(2,1)S(1)}, u32[]{:S(2)}, u32[]{:S(2)}) collective-permute-start(bf16[64,4096]{1,0:T(8,128)(2,1)S(1)} %get-tuple-element.90.refs_0_), channel_id=1, source_target_pairs={{0,2},{1,3},{2,0},{3,1},{4,6},{5,7},{6,4},{7,5},{8,10},{9,11},{10,... | collective-permute-start | bytes 1572872 | tf_op jit(solution)/shard_map/ppermute | solution.py:155
  387.4 43.5 %collective-permute-start.20 = (bf16[64,4096]{1,0:T(8,128)(2,1)S(1)}, bf16[64,4096]{1,0:T(8,128)(2,1)S(1)}, u32[]{:S(2)}, u32[]{:S(2)}) collective-permute-start(bf16[64,4096]{1,0:T(8,128)(2,1)S(1)} %get-tuple-element.91.refs_0_), channel_id=1, source_target_pairs={{0,1},{1,0},{2,3},{3,2},{4,5},{5,4},{6,7},{7,6},{8,9},{9,8},{10,11... | collective-permute-start | bytes 1572872 | tf_op jit(solution)/shard_map/ppermute | solution.py:155
  419.6 47.4 %collective-permute-start.49 = (bf16[64,4096]{1,0:T(8,128)(2,1)S(1)}, bf16[64,4096]{1,0:T(8,128)(2,1)S(1)}, u32[]{:S(2)}, u32[]{:S(2)}) collective-permute-start(bf16[64,4096]{1,0:T(8,128)(2,1)S(1)} %get-tuple-element.90.refs_0_), channel_id=1, source_target_pairs={{0,1},{1,0},{2,3},{3,2},{4,5},{5,4},{6,7},{7,6},{8,9},{9,8},{10,11... | collective-permute-start | bytes 1572872 | tf_op jit(solution)/shard_map/ppermute | solution.py:155
  430.8 36.2 %collective-permute-start.51 = (bf16[64,4096]{1,0:T(8,128)(2,1)S(1)}, bf16[64,4096]{1,0:T(8,128)(2,1)S(1)}, u32[]{:S(2)}, u32[]{:S(2)}) collective-permute-start(bf16[64,4096]{1,0:T(8,128)(2,1)S(1)} %collective-permute-done.50.refs_2_), channel_id=1, source_target_pairs={{0,1},{1,0},{2,3},{3,2},{4,5},{5,4},{6,7},{7,6},{8,9},{9,8},{10,11... | collective-permute-start | bytes 1572872 | tf_op jit(solution)/shard_map/ppermute | solution.py:155
  465.0 51.7 %collective-permute-start.23 = (bf16[64,4096]{1,0:T(8,128)(2,1)S(1)}, bf16[64,4096]{1,0:T(8,128)(2,1)S(1)}, u32[]{:S(2)}, u32[]{:S(2)}) collective-permute-start(bf16[64,4096]{1,0:T(8,128)(2,1)S(1)} %get-tuple-element.45), channel_id=1, source_target_pairs={{0,1},{1,0},{2,3},{3,2},{4,5},{5,4},{6,7},{7,6},{8,9},{9,8},{10,11... | collective-permute-start | bytes 1572872 | tf_op jit(solution)/shard_map/ppermute | solution.py:155
  489.8 35.8 %collective-permute-start.52 = (bf16[64,4096]{1,0:T(8,128)(2,1)S(1)}, bf16[64,4096]{1,0:T(8,128)(2,1)S(1)}, u32[]{:S(2)}, u32[]{:S(2)}) collective-permute-start(bf16[64,4096]{1,0:T(8,128)(2,1)S(1)} %get-tuple-element.61), channel_id=1, source_target_pairs={{0,1},{1,0},{2,3},{3,2},{4,5},{5,4},{6,7},{7,6},{8,9},{9,8},{10,11... | collective-permute-start | bytes 1572872 | tf_op jit(solution)/shard_map/ppermute | solution.py:155
  491.9 32.8 %collective-permute-start.25 = (bf16[64,4096]{1,0:T(8,128)(2,1)S(1)}, bf16[64,4096]{1,0:T(8,128)(2,1)S(1)}, u32[]{:S(2)}, u32[]{:S(2)}) collective-permute-start(bf16[64,4096]{1,0:T(8,128)(2,1)S(1)} %add_convert_fusion.6), channel_id=1, source_target_pairs={{0,2},{1,3},{2,0},{3,1},{4,6},{5,7},{6,4},{7,5},{8,10},{9,11},{10,... | collective-permute-start | bytes 1572872 | tf_op jit(solution)/shard_map/ppermute | solution.py:155
  515.9 32.8 %collective-permute-start.54 = (bf16[64,4096]{1,0:T(8,128)(2,1)S(1)}, bf16[64,4096]{1,0:T(8,128)(2,1)S(1)}, u32[]{:S(2)}, u32[]{:S(2)}) collective-permute-start(bf16[64,4096]{1,0:T(8,128)(2,1)S(1)} %add_convert_fusion.1), channel_id=1, source_target_pairs={{0,2},{1,3},{2,0},{3,1},{4,6},{5,7},{6,4},{7,5},{8,10},{9,11},{10,... | collective-permute-start | bytes 1572872 | tf_op jit(solution)/shard_map/ppermute | solution.py:155
  550.2 46.6 %collective-permute-start.55 = (bf16[64,4096]{1,0:T(8,128)(2,1)S(1)}, bf16[64,4096]{1,0:T(8,128)(2,1)S(1)}, u32[]{:S(2)}, u32[]{:S(2)}) collective-permute-start(bf16[64,4096]{1,0:T(8,128)(2,1)S(1)} %get-tuple-element.88.refs_0_), channel_id=1, source_target_pairs={{0,1},{1,0},{2,3},{3,2},{4,5},{5,4},{6,7},{7,6},{8,9},{9,8},{10,11... | collective-permute-start | bytes 1572872 | tf_op jit(solution)/shard_map/ppermute | solution.py:155
  552.0 44.8 %collective-permute-start.27 = (bf16[64,4096]{1,0:T(8,128)(2,1)S(1)}, bf16[64,4096]{1,0:T(8,128)(2,1)S(1)}, u32[]{:S(2)}, u32[]{:S(2)}) collective-permute-start(bf16[64,4096]{1,0:T(8,128)(2,1)S(1)} %get-tuple-element.89.refs_0_), channel_id=1, source_target_pairs={{0,2},{1,3},{2,0},{3,1},{4,6},{5,7},{6,4},{7,5},{8,10},{9,11},{10,... | collective-permute-start | bytes 1572872 | tf_op jit(solution)/shard_map/ppermute | solution.py:155
  575.3 52.3 %collective-permute-start.26 = (bf16[64,4096]{1,0:T(8,128)(2,1)S(1)}, bf16[64,4096]{1,0:T(8,128)(2,1)S(1)}, u32[]{:S(2)}, u32[]{:S(2)}) collective-permute-start(bf16[64,4096]{1,0:T(8,128)(2,1)S(1)} %get-tuple-element.89.refs_0_), channel_id=1, source_target_pairs={{0,1},{1,0},{2,3},{3,2},{4,5},{5,4},{6,7},{7,6},{8,9},{9,8},{10,11... | collective-permute-start | bytes 1572872 | tf_op jit(solution)/shard_map/ppermute | solution.py:155
  596.8 30.9 %collective-permute-start.28 = (bf16[64,4096]{1,0:T(8,128)(2,1)S(1)}, bf16[64,4096]{1,0:T(8,128)(2,1)S(1)}, u32[]{:S(2)}, u32[]{:S(2)}) collective-permute-start(bf16[64,4096]{1,0:T(8,128)(2,1)S(1)} %collective-permute-done.27.refs_2_), channel_id=1, source_target_pairs={{0,1},{1,0},{2,3},{3,2},{4,5},{5,4},{6,7},{7,6},{8,9},{9,8},{10,11... | collective-permute-start | bytes 1572872 | tf_op jit(solution)/shard_map/ppermute | solution.py:155
  625.6 29.3 %collective-permute-start.59 = (bf16[64,4096]{1,0:T(8,128)(2,1)S(1)}, bf16[64,4096]{1,0:T(8,128)(2,1)S(1)}, u32[]{:S(2)}, u32[]{:S(2)}) collective-permute-start(bf16[64,4096]{1,0:T(8,128)(2,1)S(1)} %get-tuple-element.67), channel_id=1, source_target_pairs={{0,1},{1,0},{2,3},{3,2},{4,5},{5,4},{6,7},{7,6},{8,9},{9,8},{10,11... | collective-permute-start | bytes 1572872 | tf_op jit(solution)/shard_map/ppermute | solution.py:155
  625.6 54.0 %collective-permute-start.58 = (bf16[64,4096]{1,0:T(8,128)(2,1)S(1)}, bf16[64,4096]{1,0:T(8,128)(2,1)S(1)}, u32[]{:S(2)}, u32[]{:S(2)}) collective-permute-start(bf16[64,4096]{1,0:T(8,128)(2,1)S(1)} %get-tuple-element.65), channel_id=1, source_target_pairs={{0,1},{1,0},{2,3},{3,2},{4,5},{5,4},{6,7},{7,6},{8,9},{9,8},{10,11... | collective-permute-start | bytes 1572872 | tf_op jit(solution)/shard_map/ppermute | solution.py:155
  652.9 35.2 %collective-permute-start.29 = (bf16[64,4096]{1,0:T(8,128)(2,1)S(1)}, bf16[64,4096]{1,0:T(8,128)(2,1)S(1)}, u32[]{:S(2)}, u32[]{:S(2)}) collective-permute-start(bf16[64,4096]{1,0:T(8,128)(2,1)S(1)} %get-tuple-element.49), channel_id=1, source_target_pairs={{0,1},{1,0},{2,3},{3,2},{4,5},{5,4},{6,7},{7,6},{8,9},{9,8},{10,11... | collective-permute-start | bytes 1572872 | tf_op jit(solution)/shard_map/ppermute | solution.py:155
  655.0 32.8 %collective-permute-start.60 = (bf16[64,4096]{1,0:T(8,128)(2,1)S(1)}, bf16[64,4096]{1,0:T(8,128)(2,1)S(1)}, u32[]{:S(2)}, u32[]{:S(2)}) collective-permute-start(bf16[64,4096]{1,0:T(8,128)(2,1)S(1)} %add_convert_fusion), channel_id=1, source_target_pairs={{0,2},{1,3},{2,0},{3,1},{4,6},{5,7},{6,4},{7,5},{8,10},{9,11},{10,... | collective-permute-start | bytes 1572872 | tf_op jit(solution)/shard_map/ppermute | solution.py:155
  (54 other events, 948.1 us)

commit v2 on v1

v2 whole, which is shorter than its diff:
```python
import functools

import jax
import jax.numpy as jnp
import numpy as np
from jax import lax
from jax.experimental import pallas as pl
from jax.experimental.pallas import tpu as pltpu
from jax.sharding import PartitionSpec as P

HEAD_DIM = 128
EPSILON = 1e-05
ROTARY_FREQ_BASE = 10000.0
BOTH = ("section", "tensor")
WIDE = 256
VMEM_LIMIT = 50 * 2**20


def rms_norm(hidden, scale_gain):
    values = hidden.astype(jnp.float32)
    inverse = lax.rsqrt(jnp.mean(values * values, axis=-1, keepdims=True) + EPSILON)
    return (values * inverse * scale_gain.astype(jnp.float32)).astype(jnp.bfloat16)


def rope_tables(length):
    half_dim = HEAD_DIM // 2
    frequency = ROTARY_FREQ_BASE ** (-(np.arange(half_dim, dtype=np.float64) / half_dim))
    angles = np.arange(length, dtype=np.float64)[:, None] * frequency[None, :]
    cosine, sine = np.cos(angles), np.sin(angles)
    cosine = np.concatenate([cosine, cosine], axis=1).astype(np.float32)
    sine = np.concatenate([-sine, sine], axis=1).astype(np.float32)
    return cosine, sine


def dot(left, right):
    return jnp.dot(left, right, preferred_element_type=jnp.float32)


def load_rows(x_refs, x_all):
    start = 0
    for ref in x_refs:
        x_all[start : start + ref.shape[0], :] = ref[...]
        start += ref.shape[0]


def add_part(part, total, out_refs):
    step = pl.program_id(0)

    @pl.when(step == 0)
    def _():
        total[...] = part

    @pl.when(step > 0)
    def _():
        total[...] += part

    @pl.when(step == pl.num_programs(0) - 1)
    def _():
        start = 0
        for ref in out_refs:
            ref[...] = total[start : start + ref.shape[0], :].astype(jnp.bfloat16)
            start += ref.shape[0]


def attention_kernel(count, cos_ref, sin_ref, row_ref, col_ref, wq_ref, wk_ref, wv_ref, wo_ref, *refs):
    x_refs, out_refs, (x_all, total) = refs[:count], refs[count:-2], refs[-2:]
    pl.when(pl.program_id(0) == 0)(lambda: load_rows(x_refs, x_all))
    x = x_all[...]
    cosine, sine = cos_ref[...], sin_ref[...]
    visible = row_ref[...] >= col_ref[...]
    query, key, value = dot(x, wq_ref[0]), dot(x, wk_ref[0]), dot(x, wv_ref[0])
    value = value.astype(jnp.bfloat16)
    outs = []
    for head in range(query.shape[1] // HEAD_DIM):
        cut = slice(head * HEAD_DIM, (head + 1) * HEAD_DIM)
        q, k, v = query[:, cut], key[:, cut], value[:, cut]
        q = (q * cosine + pltpu.roll(q, HEAD_DIM // 2, 1) * sine).astype(jnp.bfloat16)
        k = (k * cosine + pltpu.roll(k, HEAD_DIM // 2, 1) * sine).astype(jnp.bfloat16)
        scores = lax.dot_general(
            q, k, (((1,), (1,)), ((), ())), preferred_element_type=jnp.float32
        ) * HEAD_DIM ** (-0.5)
        scores = jnp.where(visible, scores, -jnp.inf)
        scores = jnp.exp(scores - jnp.max(scores, axis=-1, keepdims=True))
        probs = scores / jnp.sum(scores, axis=-1, keepdims=True)
        outs.append(dot(probs.astype(jnp.bfloat16), v).astype(jnp.bfloat16))
    add_part(dot(jnp.concatenate(outs, axis=1), wo_ref[0]), total, out_refs)


def mlp_kernel(count, wg_ref, wu_ref, wd_ref, *refs):
    x_refs, out_refs, (x_all, total) = refs[:count], refs[count:-2], refs[-2:]
    pl.when(pl.program_id(0) == 0)(lambda: load_rows(x_refs, x_all))
    x = x_all[...]
    gate, up = dot(x, wg_ref[0]), dot(x, wu_ref[0])
    inner = (gate / (1.0 + jnp.exp(-gate)) * up).astype(jnp.bfloat16)
    add_part(dot(inner, wd_ref[0]), total, out_refs)


def whole(array):
    return pl.BlockSpec(array.shape, lambda i: (0,) * array.ndim)


def fused(kernel, name, tables, by_columns, by_rows, pieces, cuts):
    width = pieces[0].shape[1]
    length = sum(piece.shape[0] for piece in pieces)
    hidden = by_rows.shape[1]
    wide = min(WIDE, hidden)
    weights = list(by_columns) + [by_rows]
    flops = 2 * length * sum(w.size for w in weights)
    traffic = 2 * sum(w.size for w in weights) + 4 * length * width
    return pl.pallas_call(
        functools.partial(kernel, len(pieces)),
        out_shape=[jax.ShapeDtypeStruct((rows, width), jnp.bfloat16) for rows in cuts],
        grid=(hidden // wide,),
        in_specs=[whole(t) for t in tables]
        + [pl.BlockSpec((1, width, wide), lambda i: (0, 0, i)) for _ in by_columns]
        + [pl.BlockSpec((1, wide, width), lambda i: (0, i, 0))]
        + [whole(p) for p in pieces],
        out_specs=[pl.BlockSpec((rows, width), lambda i: (0, 0)) for rows in cuts],
        scratch_shapes=[
            pltpu.VMEM((length, width), jnp.bfloat16),
            pltpu.VMEM((length, width), jnp.float32),
        ],
        compiler_params=pltpu.CompilerParams(
            dimension_semantics=("arbitrary",), vmem_limit_bytes=VMEM_LIMIT
        ),
        cost_estimate=pl.CostEstimate(flops=flops, bytes_accessed=traffic, transcendentals=0),
        name=name,
    )(*tables, *weights, *pieces)


def send(value, source, target, distance):
    count = lax.axis_size("tensor")
    links = [(source * count + z, target * count + (z ^ distance)) for z in range(count)]
    return lax.ppermute(value, BOTH, links)


def relayed(j):
    return j & (j - 1) != 0


def row_cuts(length):
    sections, tensors = lax.axis_size("section"), lax.axis_size("tensor")
    share = length // tensors
    cuts = []
    for j in range(tensors):
        cuts += [share] if relayed(j) else [share // sections] * sections
    return cuts


def gather_rows(own, layer):
    pieces = []
    for j in range(lax.axis_size("tensor")):
        for source in range(lax.axis_size("section")):
            local = j == 0 and source == layer
            pieces.append(own if local else send(own, source, layer, j))
    return pieces


def scatter_rows(partial, layer):
    sections, tensors = lax.axis_size("section"), lax.axis_size("tensor")
    partial = list(partial)
    held = {}
    for j in range(tensors):
        if relayed(j):
            held[j] = partial.pop(0)
        else:
            held[j] = [partial.pop(0) for _ in range(sections)]
    sums = jnp.where(lax.axis_index("section") == layer, held[0][layer], 0).astype(jnp.float32)
    arrived = []
    for bit in range(tensors.bit_length() - 1):
        distance = 1 << bit
        for j in [j for j in range(tensors - 1, 0, -1) if j in held and j & distance]:
            piece = held.pop(j)
            if relayed(j):
                part = send(piece.astype(jnp.bfloat16), layer, layer, distance)
                part = part.astype(jnp.float32)
                into = held[j ^ distance]
                if relayed(j ^ distance):
                    held[j ^ distance] = into.astype(jnp.float32) + part
                else:
                    rows = into[0].shape[0]
                    held[j ^ distance] = [
                        p.astype(jnp.float32) + part[h * rows : (h + 1) * rows]
                        for h, p in enumerate(into)
                    ]
            else:
                arrived += [
                    send(p.astype(jnp.bfloat16), layer, h, distance) for h, p in enumerate(piece)
                ]
    arrived += [send(held[0][h], layer, h, 0) for h in range(sections) if h != layer]
    for part in arrived:
        sums = sums + part.astype(jnp.float32)
    return sums


def layer_gains(gain):
    sections, section = lax.axis_size("section"), lax.axis_index("section")
    held = [gain]
    for steps in range(1, sections):
        links = [(h, (h + steps) % sections) for h in range(sections)]
        held.append(lax.ppermute(gain, "section", links))
    held = jnp.concatenate(held, axis=0)
    return [held[(section - layer) % sections] for layer in range(sections)]


def body(
    ids_beam,
    beam_map,
    lengths,
    embed_table,
    gain_attn,
    w_query,
    w_key,
    w_value,
    w_out,
    gain_mlp,
    w_gate,
    w_up,
    w_down,
    final_gain,
    score_weight,
):
    section, tensor = lax.axis_index("section"), lax.axis_index("tensor")
    sections, tensors = lax.axis_size("section"), lax.axis_size("tensor")
    batch, batches = lax.axis_index("batch"), lax.axis_size("batch")
    per_device, length = ids_beam.shape
    share = length // tensors
    slots = jnp.arange(tensors, dtype=jnp.int32) ^ tensor

    owned = batch * per_device + jnp.arange(per_device, dtype=jnp.int32)
    beams_owned = jnp.take(beam_map, owned)
    lengths_owned = jnp.take(lengths, owned)
    blocks = [ids_beam]
    for steps in range(1, batches):
        blocks.append(
            lax.ppermute(ids_beam, "batch", [(b, (b + steps) % batches) for b in range(batches)])
        )
    blocks = jnp.concatenate(blocks, axis=0)
    holder = (batch - beams_owned // per_device) % batches
    tokens = blocks[holder * per_device + beams_owned % per_device]

    cosine, sine = rope_tables(length)
    by_slot = lambda t: jnp.asarray(t.reshape(tensors, share, -1))[slots].reshape(length, -1)
    cosine, sine = by_slot(cosine), by_slot(sine)
    positions = (slots[:, None] * share + jnp.arange(share, dtype=jnp.int32)).reshape(length)
    tables = (cosine, sine, positions[:, None], positions[None, :])

    rows = share // sections
    cuts = row_cuts(length)
    gains_attn, gains_mlp = layer_gains(gain_attn), layer_gains(gain_mlp)
    hidden, first = [], []
    embedded = None
    for c in range(per_device):
        looked = jnp.take(embed_table, tokens[c], axis=0)
        if embedded is not None:
            looked, first[-1][0] = lax.optimization_barrier((looked, first[-1][0]))
        columns = []
        for source in range(sections):
            pieces = jnp.stack(
                [
                    looked if source == 0 and j == 0 else send(looked, source, 0, j)
                    for j in range(tensors)
                ]
            )
            columns += [
                lax.dynamic_index_in_dim(pieces, z ^ tensor, 0, False) for z in range(tensors)
            ]
        embedded = jnp.concatenate(columns, axis=1)
        normed = rms_norm(embedded, gains_attn[0])
        first.append(
            [lax.dynamic_slice_in_dim(normed, slots[j] * share, share, 0) for j in range(tensors)]
        )
        own = [
            lax.dynamic_slice_in_dim(embedded, tensor * share + h * rows, rows, 0)
            for h in range(sections)
        ]
        mine = own[0]
        for h in range(1, sections):
            mine = jnp.where(section == h, send(own[h], 0, h, 0), mine)
        hidden.append(mine)

    for layer in range(sections):
        for c in range(per_device):
            pieces = first[c] if layer == 0 else gather_rows(rms_norm(hidden[c], gains_attn[layer]), layer)
            partial = fused(
                attention_kernel,
                "attention",
                tables,
                (w_query, w_key, w_value),
                w_out,
                pieces,
                cuts,
            )
            attn_sum = scatter_rows(partial, layer)
            middle = (hidden[c].astype(jnp.float32) + attn_sum).astype(jnp.bfloat16)
            pieces = gather_rows(rms_norm(middle, gains_mlp[layer]), layer)
            partial = fused(mlp_kernel, "mlp", (), (w_gate, w_up), w_down, pieces, cuts)
            mlp_sum = scatter_rows(partial, layer)
            hidden[c] = (middle.astype(jnp.float32) + mlp_sum).astype(jnp.bfloat16)

    finals = jnp.stack(hidden)
    half = finals.shape[2] // sections
    shown = [lax.dynamic_slice_in_dim(finals, section * half, half, 2)]
    for steps in range(1, sections):
        part = lax.dynamic_slice_in_dim(finals, (section + steps) % sections * half, half, 2)
        links = [(h, (h + steps) % sections) for h in range(sections)]
        shown.append(lax.ppermute(part, "section", links))
    shown = jnp.stack([shown[k] for k in range(sections)])
    shown = jnp.concatenate(
        [
            lax.dynamic_index_in_dim(shown, (section - h) % sections, 0, False)
            for h in range(sections)
        ],
        axis=1,
    )

    at = lengths_owned - 1 - tensor * share - section * rows
    owner = (at >= 0) & (at < rows)
    row = jnp.take_along_axis(finals, jnp.clip(at, 0, rows - 1)[:, None, None], axis=1)
    values = row[:, 0].astype(jnp.float32)
    inverse = lax.rsqrt(jnp.mean(values * values, axis=-1, keepdims=True) + EPSILON)
    score = jnp.sum(
        values * inverse * final_gain.astype(jnp.float32) * score_weight.astype(jnp.float32),
        axis=-1,
    )
    score = jnp.where(owner, score, 0.0)
    devices = sections * tensors
    total = score
    for steps in range(1, devices):
        total = total + lax.ppermute(
            score, BOTH, [(d, (d + steps) % devices) for d in range(devices)]
        )
    return (shown, total)


def solution(mesh):
    placed = (
        P("batch", None),
        P(),
        P(),
        P(None, ("section", "tensor")),
        P("section", None),
        P("section", None, "tensor"),
        P("section", None, "tensor"),
        P("section", None, "tensor"),
        P("section", "tensor", None),
        P("section", None),
        P("section", None, "tensor"),
        P("section", None, "tensor"),
        P("section", "tensor", None),
        P(),
        P(),
    )
    return jax.shard_map(
        body,
        mesh=mesh,
        in_specs=placed,
        out_specs=(P("batch", "tensor", "section"), P("batch")),
        check_vma=False,
    )
```

time: 737 us -> 701 us (0.951)
  waiting for transfers between devices: 390 us -> 203 us
  starting transfers between devices: 97.9 us -> 257 us
    ppermute x59 -> x109, waiting for transfers between devices: 389 us -> 200 us  [the longest x106 200 us: send(): return lax.ppermute(value, BOTH, links)]
    ppermute x59 -> x109, starting transfers between devices: 80.4 us -> 242 us  [the longest x106 237 us: send(): return lax.ppermute(value, BOTH, links)]
  transfers between devices with their start and end apart: 69 -> 119, of which waited for: 29 -> 32; matrix products, arithmetic and copies ran while one was open for 4% -> 5% of each run, Pallas kernels for 22% -> 27%
where the time goes in v2:
time: 701 us; the launch traced here: 689 us
  starting transfers between devices  257 us (37%)
  waiting for transfers between devices  203 us (29%)
  Pallas kernels  185 us (26%)
  local copies, waits for them, and re-layouts  27 us (4%)
  other arithmetic  11.5 us (2%)
    ppermute x106, starting transfers between devices, send(): return lax.ppermute(value, BOTH, links)  237 us
    ppermute x106, waiting for transfers between devices, send(): return lax.ppermute(value, BOTH, links)  200 us
    pallas_call x8, Pallas kernels, fused(): pl.pallas_call(functools.partial(kernel, len(pieces)), out_shape=[jax.Sha...  185 us
    gather x2, local copies, waits for them, and re-layouts, body(): looked = jnp.take(embed_table, tokens[c], axis=0)  18 us
  transfers between devices with their start and end apart: 119, of which 32 were waited for; matrix products, arithmetic and copies ran while one was open for 5% of the time, Pallas kernels for 27%

profile of v2, /device:TPU:0, one launch (start us, length us, event | category | flops | bytes accessed | tf_op | source)
XLA Modules:
  0.0 688.6 jit_solution(3869355022011952878)
XLA Ops:
  15.6 9.0 %gather_fusion.5 = bf16[256,512]{1,0:T(8,128)(2,1)S(1)} fusion(bf16[16000,512]{1,0:T(8,128)(2,1)} %param.24, s32[1024]{0:T(1024)S(1)} %pad_clamp_fusion.2), kind=kCustom, calls=%fused_computation.1.clone | custom fusion | bytes 525312 | tf_op jit(solution)/shard_map/jit(_take)/gather | solution.py:254
  35.0 9.0 %gather_fusion.6 = bf16[256,512]{1,0:T(8,128)(2,1)S(1)} fusion(bf16[16000,512]{1,0:T(8,128)(2,1)} %param.24, s32[1024]{0:T(1024)S(1)} %pad_clamp_fusion), kind=kCustom, calls=%fused_computation.3.clone | custom fusion | bytes 525312 | tf_op jit(solution)/shard_map/jit(_take)/gather | solution.py:254
  55.9 13.2 %collective-permute-done.8 = bf16[256,512]{1,0:T(8,128)(2,1)S(1)} collective-permute-done((bf16[256,512]{1,0:T(8,128)(2,1)S(1)}, bf16[256,512]{1,0:T(8,128)(2,1)S(1)}, u32[]{:S(2)}, u32[]{:S(2)}) %collective-permute-start.8) | collective-permute-done | bytes 262176 | tf_op jit(solution)/shard_map/ppermute | solution.py:134
  75.2 5.5 collective-permute-start.58
  87.3 21.9 %attention.4 = (bf16[32,4096]{1,0:T(8,128)(2,1)S(1)}, bf16[32,4096]{1,0:T(8,128)(2,1)S(1)}, bf16[32,4096]{1,0:T(8,128)(2,1)S(1)}, bf16[32,4096]{1,0:T(8,128)(2,1...) custom-call(f32[256,128]{1,0:T(8,128)S(1)} %bitcast.77, ...), custom_call_target="tpu_custom_call" | custom-call | flops 8589934592 | bytes 37748736 | tf_op jit(solution)/shard_map/attention/pallas_call | solution.py:110
  119.4 11.3 %collective-permute-done.63 = bf16[256,512]{1,0:T(8,128)(2,1)S(1)} collective-permute-done((bf16[256,512]{1,0:T(8,128)(2,1)S(1)}, bf16[256,512]{1,0:T(8,128)(2,1)S(1)}, u32[]{:S(2)}, u32[]{:S(2)}) %collective-permute-start.63) | collective-permute-done | bytes 262176 | tf_op jit(solution)/shard_map/ppermute | solution.py:134
  135.8 21.8 %attention.6 = (bf16[32,4096]{1,0:T(8,128)(2,1)S(1)}, bf16[32,4096]{1,0:T(8,128)(2,1)S(1)}, bf16[32,4096]{1,0:T(8,128)(2,1)S(1)}, bf16[32,4096]{1,0:T(8,128)(2,1...) custom-call(f32[256,128]{1,0:T(8,128)S(1)} %bitcast.78, ...), custom_call_target="tpu_custom_call" | custom-call | flops 8589934592 | bytes 37748736 | tf_op jit(solution)/shard_map/attention/pallas_call | solution.py:110
  157.7 6.3 collective-permute-start.68
  164.2 11.6 %collective-permute-done.68 = bf16[64,4096]{1,0:T(8,128)(2,1)S(1)} collective-permute-done((bf16[64,4096]{1,0:T(8,128)(2,1)S(1)}, bf16[64,4096]{1,0:T(8,128)(2,1)S(1)}, u32[]{:S(2)}, u32[]{:S(2)}) %collective-permute-start.68) | collective-permute-done | bytes 524320 | tf_op jit(solution)/shard_map/ppermute | solution.py:134
  190.9 11.6 %collective-permute-done.15 = bf16[32,4096]{1,0:T(8,128)(2,1)S(1)} collective-permute-done((bf16[32,4096]{1,0:T(8,128)(2,1)S(1)}, bf16[32,4096]{1,0:T(8,128)(2,1)S(1)}, u32[]{:S(2)}, u32[]{:S(2)}) %collective-permute-start.15) | collective-permute-done | bytes 262176 | tf_op jit(solution)/shard_map/ppermute | solution.py:134
  206.8 18.2 %collective-permute-done.69 = bf16[32,4096]{1,0:T(8,128)(2,1)S(1)} collective-permute-done((bf16[32,4096]{1,0:T(8,128)(2,1)S(1)}, bf16[32,4096]{1,0:T(8,128)(2,1)S(1)}, u32[]{:S(2)}, u32[]{:S(2)}) %collective-permute-start.69) | collective-permute-done | bytes 262176 | tf_op jit(solution)/shard_map/ppermute | solution.py:134
  237.3 11.6 %collective-permute-done.19.refs_1_ = bf16[32,4096]{1,0:T(8,128)(2,1)S(1)} collective-permute-done((bf16[32,4096]{1,0:T(8,128)(2,1)S(1)}, bf16[32,4096]{1,0:T(8,128)(2,1)S(1)}, u32[]{:S(2)}, u32[]{:S(2)}) %collective-permute-start.19) | collective-permute-done | bytes 262176 | tf_op jit(solution)/shard_map/ppermute | solution.py:134
  264.5 9.4 %collective-permute-done.72.refs_1_ = bf16[32,4096]{1,0:T(8,128)(2,1)S(1)} collective-permute-done((bf16[32,4096]{1,0:T(8,128)(2,1)S(1)}, bf16[32,4096]{1,0:T(8,128)(2,1)S(1)}, u32[]{:S(2)}, u32[]{:S(2)}) %collective-permute-start.72) | collective-permute-done | bytes 262176 | tf_op jit(solution)/shard_map/ppermute | solution.py:134
  279.1 24.4 %mlp.4 = (bf16[32,4096]{1,0:T(8,128)(2,1)S(1)}, bf16[32,4096]{1,0:T(8,128)(2,1)S(1)}, bf16[32,4096]{1,0:T(8,128)(2,1)S(1)}, bf16[32,4096]{1,0:T(8,128)(2,1)S(1)}...) custom-call(bf16[1,4096,2048]{2,1,0:T(8,128)(2,1)} %wg_ref.7, ...), custom_call_target="tpu_custom_call" | custom-call | flops 12884901888 | bytes 54525952 | tf_op jit(solution)/shard_map/mlp/pallas_call | solution.py:110
  312.2 24.4 %mlp.6 = (bf16[32,4096]{1,0:T(8,128)(2,1)S(1)}, bf16[32,4096]{1,0:T(8,128)(2,1)S(1)}, bf16[32,4096]{1,0:T(8,128)(2,1)S(1)}, bf16[32,4096]{1,0:T(8,128)(2,1)S(1)}...) custom-call(bf16[1,4096,2048]{2,1,0:T(8,128)(2,1)} %wg_ref.7, ...), custom_call_target="tpu_custom_call" | custom-call | flops 12884901888 | bytes 54525952 | tf_op jit(solution)/shard_map/mlp/pallas_call | solution.py:110
  343.2 13.0 %collective-permute-done.81 = bf16[64,4096]{1,0:T(8,128)(2,1)S(1)} collective-permute-done((bf16[64,4096]{1,0:T(8,128)(2,1)}, bf16[64,4096]{1,0:T(8,128)(2,1)S(1)}, u32[]{:S(2)}, u32[]{:S(2)}) %collective-permute-start.81) | collective-permute-done | bytes 524320 | tf_op jit(solution)/shard_map/ppermute | solution.py:134
  368.9 7.0 %collective-permute-done.84 = bf16[32,4096]{1,0:T(8,128)(2,1)S(1)} collective-permute-done((bf16[32,4096]{1,0:T(8,128)(2,1)S(1)}, bf16[32,4096]{1,0:T(8,128)(2,1)S(1)}, u32[]{:S(2)}, u32[]{:S(2)}) %collective-permute-start.84) | collective-permute-done | bytes 262176 | tf_op jit(solution)/shard_map/ppermute | solution.py:134
  378.9 13.8 %collective-permute-start.32 = (bf16[32,4096]{1,0:T(8,128)(2,1)S(1)}, bf16[32,4096]{1,0:T(8,128)(2,1)S(1)}, u32[]{:S(2)}, u32[]{:S(2)}) collective-permute-start(bf16[32,4096]{1,0:T(8,128)(2,1)S(1)} %get-tuple-element.171.refs_1_), channel_id=1, source_target_pairs={{0,16},{1,17},{2,18},{3,19},{4,20},{5,21},{6,22},{7,23},{8,24},{9,... | collective-permute-start | bytes 786440 | tf_op jit(solution)/shard_map/ppermute | solution.py:134
  403.5 5.8 collective-permute-start.37
  415.1 11.5 %collective-permute-start.88 = (bf16[32,4096]{1,0:T(8,128)(2,1)S(1)}, bf16[32,4096]{1,0:T(8,128)(2,1)S(1)}, u32[]{:S(2)}, u32[]{:S(2)}) collective-permute-start(bf16[32,4096]{1,0:T(8,128)(2,1)S(1)} %get-tuple-element.170.refs_1_), channel_id=1, source_target_pairs={{0,18},{1,19},{2,16},{3,17},{4,22},{5,23},{6,20},{7,21},{8,26},{9,... | collective-permute-start | bytes 786440 | tf_op jit(solution)/shard_map/ppermute | solution.py:134
  432.6 22.0 %attention.5 = (bf16[32,4096]{1,0:T(8,128)(2,1)S(1)}, bf16[32,4096]{1,0:T(8,128)(2,1)S(1)}, bf16[32,4096]{1,0:T(8,128)(2,1)S(1)}, bf16[32,4096]{1,0:T(8,128)(2,1...) custom-call(f32[256,128]{1,0:T(8,128)S(1)} %bitcast.79, ...), custom_call_target="tpu_custom_call" | custom-call | flops 8589934592 | bytes 37748736 | tf_op jit(solution)/shard_map/attention/pallas_call | solution.py:110
  458.6 22.0 %attention.7 = (bf16[32,4096]{1,0:T(8,128)(2,1)S(1)}, bf16[32,4096]{1,0:T(8,128)(2,1)S(1)}, bf16[32,4096]{1,0:T(8,128)(2,1)S(1)}, bf16[32,4096]{1,0:T(8,128)(2,1...) custom-call(f32[256,128]{1,0:T(8,128)S(1)} %bitcast.80, ...), custom_call_target="tpu_custom_call" | custom-call | flops 8589934592 | bytes 37748736 | tf_op jit(solution)/shard_map/attention/pallas_call | solution.py:110
  486.9 12.5 %collective-permute-done.42 = bf16[32,4096]{1,0:T(8,128)(2,1)S(1)} collective-permute-done((bf16[32,4096]{1,0:T(8,128)(2,1)S(1)}, bf16[32,4096]{1,0:T(8,128)(2,1)S(1)}, u32[]{:S(2)}, u32[]{:S(2)}) %collective-permute-start.42) | collective-permute-done | bytes 262176 | tf_op jit(solution)/shard_map/ppermute | solution.py:134
  501.9 10.8 %collective-permute-done.92 = bf16[32,4096]{1,0:T(8,128)(2,1)S(1)} collective-permute-done((bf16[32,4096]{1,0:T(8,128)(2,1)S(1)}, bf16[32,4096]{1,0:T(8,128)(2,1)S(1)}, u32[]{:S(2)}, u32[]{:S(2)}) %collective-permute-start.92) | collective-permute-done | bytes 262176 | tf_op jit(solution)/shard_map/ppermute | solution.py:134
  516.5 13.5 %collective-permute-done.95 = bf16[32,4096]{1,0:T(8,128)(2,1)S(1)} collective-permute-done((bf16[32,4096]{1,0:T(8,128)(2,1)S(1)}, bf16[32,4096]{1,0:T(8,128)(2,1)S(1)}, u32[]{:S(2)}, u32[]{:S(2)}) %collective-permute-start.95) | collective-permute-done | bytes 262176 | tf_op jit(solution)/shard_map/ppermute | solution.py:134
  531.3 11.6 %collective-permute-start.101 = (bf16[32,4096]{1,0:T(8,128)(2,1)S(1)}, bf16[32,4096]{1,0:T(8,128)(2,1)S(1)}, u32[]{:S(2)}, u32[]{:S(2)}) collective-permute-start(bf16[32,4096]{1,0:T(8,128)(2,1)S(1)} %get-tuple-element.168.refs_1_), channel_id=1, source_target_pairs={{0,18},{1,19},{2,16},{3,17},{4,22},{5,23},{6,20},{7,21},{8,26},{9,... | collective-permute-start | bytes 786440 | tf_op jit(solution)/shard_map/ppermute | solution.py:134
  553.9 7.0 %collective-permute-start.45 = (bf16[32,4096]{1,0:T(8,128)(2,1)S(1)}, bf16[32,4096]{1,0:T(8,128)(2,1)S(1)}, u32[]{:S(2)}, u32[]{:S(2)}) collective-permute-start(bf16[32,4096]{1,0:T(8,128)(2,1)S(1)} %get-tuple-element.169.refs_1_), channel_id=1, source_target_pairs={{0,16},{1,17},{2,18},{3,19},{4,20},{5,21},{6,22},{7,23},{8,24},{9,... | collective-permute-start | bytes 786440 | tf_op jit(solution)/shard_map/ppermute | solution.py:134
  570.0 5.7 collective-permute-start.50
  576.6 24.4 %mlp.7 = (bf16[32,4096]{1,0:T(8,128)(2,1)S(1)}, bf16[32,4096]{1,0:T(8,128)(2,1)S(1)}, bf16[32,4096]{1,0:T(8,128)(2,1)S(1)}, bf16[32,4096]{1,0:T(8,128)(2,1)S(1)}...) custom-call(bf16[1,4096,2048]{2,1,0:T(8,128)(2,1)} %wg_ref.7, ...), custom_call_target="tpu_custom_call" | custom-call | flops 12884901888 | bytes 54525952 | tf_op jit(solution)/shard_map/mlp/pallas_call | solution.py:110
  605.1 24.5 %mlp.5 = (bf16[32,4096]{1,0:T(8,128)(2,1)S(1)}, bf16[32,4096]{1,0:T(8,128)(2,1)S(1)}, bf16[32,4096]{1,0:T(8,128)(2,1)S(1)}, bf16[32,4096]{1,0:T(8,128)(2,1)S(1)}...) custom-call(bf16[1,4096,2048]{2,1,0:T(8,128)(2,1)} %wg_ref.7, ...), custom_call_target="tpu_custom_call" | custom-call | flops 12884901888 | bytes 54525952 | tf_op jit(solution)/shard_map/mlp/pallas_call | solution.py:110
  635.9 9.1 %collective-permute-done.108 = bf16[32,4096]{1,0:T(8,128)(2,1)S(1)} collective-permute-done((bf16[32,4096]{1,0:T(8,128)(2,1)S(1)}, bf16[32,4096]{1,0:T(8,128)(2,1)S(1)}, u32[]{:S(2)}, u32[]{:S(2)}) %collective-permute-start.108) | collective-permute-done | bytes 262176 | tf_op jit(solution)/shard_map/ppermute | solution.py:134
  647.3 16.1 %collective-permute-done.52 = bf16[32,4096]{1,0:T(8,128)(2,1)S(1)} collective-permute-done((bf16[32,4096]{1,0:T(8,128)(2,1)S(1)}, bf16[32,4096]{1,0:T(8,128)(2,1)S(1)}, u32[]{:S(2)}, u32[]{:S(2)}) %collective-permute-start.52) | collective-permute-done | bytes 262176 | tf_op jit(solution)/shard_map/ppermute | solution.py:134
  (337 shorter events, 243.4 us)
Async XLA Ops:
  5.1 39.0 %collective-permute-start.11 = (bf16[1,4096]{1,0:T(2,128)(2,1)}, bf16[1,4096]{1,0:T(2,128)(2,1)S(1)}, u32[]{:S(2)}, u32[]{:S(2)}) collective-permute-start(bf16[1,4096]{1,0:T(2,128)(2,1)} %param.25), channel_id=1, source_target_pairs={{0,16},{16,0},{1,17},{17,1},{2,18},{18,2},{3,19},{19,3},{4,20},{20... | collective-permute-start | bytes 24584 | tf_op jit(solution)/shard_map/ppermute | solution.py:201
  6.6 38.7 %collective-permute-start.18 = (bf16[1,4096]{1,0:T(2,128)(2,1)}, bf16[1,4096]{1,0:T(2,128)(2,1)S(1)}, u32[]{:S(2)}, u32[]{:S(2)}) collective-permute-start(bf16[1,4096]{1,0:T(2,128)(2,1)} %param.30), channel_id=1, source_target_pairs={{0,16},{16,0},{1,17},{17,1},{2,18},{18,2},{3,19},{19,3},{4,20},{20... | collective-permute-start | bytes 24584 | tf_op jit(solution)/shard_map/ppermute | solution.py:201
  72.6 42.6 %collective-permute-start.61 = (bf16[256,512]{1,0:T(8,128)(2,1)S(1)}, bf16[256,512]{1,0:T(8,128)(2,1)S(1)}, u32[]{:S(2)}, u32[]{:S(2)}) collective-permute-start(bf16[256,512]{1,0:T(8,128)(2,1)S(1)} %broadcast_select_fusion), channel_id=1, source_target_pairs={{16,0},{17,1},{18,2},{19,3},{20,4},{21,5},{22,6},{23,7},{24,8},{25... | collective-permute-start | bytes 786440 | tf_op jit(solution)/shard_map/ppermute | solution.py:134
  73.9 44.2 %collective-permute-start.62 = (bf16[256,512]{1,0:T(8,128)(2,1)S(1)}, bf16[256,512]{1,0:T(8,128)(2,1)S(1)}, u32[]{:S(2)}, u32[]{:S(2)}) collective-permute-start(bf16[256,512]{1,0:T(8,128)(2,1)S(1)} %broadcast_select_fusion), channel_id=1, source_target_pairs={{16,1},{17,0},{18,3},{19,2},{20,5},{21,4},{22,7},{23,6},{24,9},{25... | collective-permute-start | bytes 786440 | tf_op jit(solution)/shard_map/ppermute | solution.py:134
  75.2 34.1 %collective-permute-start.58 = (bf16[256,512]{1,0:T(8,128)(2,1)S(1)}, bf16[256,512]{1,0:T(8,128)(2,1)S(1)}, u32[]{:S(2)}, u32[]{:S(2)}) collective-permute-start(bf16[256,512]{1,0:T(8,128)(2,1)S(1)} %broadcast_select_fusion), channel_id=1, source_target_pairs={{0,1},{1,0},{2,3},{3,2},{4,5},{5,4},{6,7},{7,6},{8,9},{9,8},{10,11... | collective-permute-start | bytes 786440 | tf_op jit(solution)/shard_map/ppermute | solution.py:134
  111.9 45.8 %collective-permute-start.14 = (bf16[64,4096]{1,0:T(8,128)(2,1)S(1)}, bf16[64,4096]{1,0:T(8,128)(2,1)S(1)}, u32[]{:S(2)}, u32[]{:S(2)}) collective-permute-start(bf16[64,4096]{1,0:T(8,128)(2,1)S(1)} %get-tuple-element.67), channel_id=1, source_target_pairs={{0,1},{1,0},{2,3},{3,2},{4,5},{5,4},{6,7},{7,6},{8,9},{9,8},{10,11... | collective-permute-start | bytes 1572872 | tf_op jit(solution)/shard_map/ppermute | solution.py:134
  115.2 64.3 %collective-permute-start.12 = (bf16[32,4096]{1,0:T(8,128)(2,1)S(1)}, bf16[32,4096]{1,0:T(8,128)(2,1)S(1)}, u32[]{:S(2)}, u32[]{:S(2)}) collective-permute-start(bf16[32,4096]{1,0:T(8,128)(2,1)S(1)} %get-tuple-element.64), channel_id=1, source_target_pairs={{0,1},{1,0},{2,3},{3,2},{4,5},{5,4},{6,7},{7,6},{8,9},{9,8},{10,11... | collective-permute-start | bytes 786440 | tf_op jit(solution)/shard_map/ppermute | solution.py:134
  118.0 64.6 %collective-permute-start.13 = (bf16[32,4096]{1,0:T(8,128)(2,1)S(1)}, bf16[32,4096]{1,0:T(8,128)(2,1)S(1)}, u32[]{:S(2)}, u32[]{:S(2)}) collective-permute-start(bf16[32,4096]{1,0:T(8,128)(2,1)S(1)} %get-tuple-element.65), channel_id=1, source_target_pairs={{0,17},{1,16},{2,19},{3,18},{4,21},{5,20},{6,23},{7,22},{8,25},{9,... | collective-permute-start | bytes 786440 | tf_op jit(solution)/shard_map/ppermute | solution.py:134
  130.7 53.4 %collective-permute-start.17 = (bf16[32,4096]{1,0:T(8,128)(2,1)S(1)}, bf16[32,4096]{1,0:T(8,128)(2,1)S(1)}, u32[]{:S(2)}, u32[]{:S(2)}) collective-permute-start(bf16[32,4096]{1,0:T(8,128)(2,1)S(1)} %get-tuple-element.69), channel_id=1, source_target_pairs={{0,16},{1,17},{2,18},{3,19},{4,20},{5,21},{6,22},{7,23},{8,24},{9,... | collective-permute-start | bytes 786440 | tf_op jit(solution)/shard_map/ppermute | solution.py:134
  132.0 53.4 %collective-permute-start.10 = (bf16[32,4096]{1,0:T(8,128)(2,1)S(1)}, bf16[32,4096]{1,0:T(8,128)(2,1)S(1)}, u32[]{:S(2)}, u32[]{:S(2)}) collective-permute-start(bf16[32,4096]{1,0:T(8,128)(2,1)S(1)} %constant_dynamic-slice_fusion.9), channel_id=1, source_target_pairs={{0,16},{1,17},{2,18},{3,19},{4,20},{5,21},{6,22},{7,23},{8,24},{9,... | collective-permute-start | bytes 786440 | tf_op jit(solution)/shard_map/ppermute | solution.py:134
  255.5 48.1 %collective-permute-start.74 = (bf16[32,4096]{1,0:T(8,128)(2,1)S(1)}, bf16[32,4096]{1,0:T(8,128)(2,1)S(1)}, u32[]{:S(2)}, u32[]{:S(2)}) collective-permute-start(bf16[32,4096]{1,0:T(8,128)(2,1)S(1)} %get-tuple-element.172.refs_0_), channel_id=1, source_target_pairs={{16,1},{17,0},{18,3},{19,2},{20,5},{21,4},{22,7},{23,6},{24,9},{25... | collective-permute-start | bytes 786440 | tf_op jit(solution)/shard_map/ppermute | solution.py:134
  260.2 45.3 %collective-permute-start.75 = (bf16[32,4096]{1,0:T(8,128)(2,1)S(1)}, bf16[32,4096]{1,0:T(8,128)(2,1)S(1)}, u32[]{:S(2)}, u32[]{:S(2)}) collective-permute-start(bf16[32,4096]{1,0:T(8,128)(2,1)S(1)} %get-tuple-element.172.refs_0_), channel_id=1, source_target_pairs={{0,2},{1,3},{2,0},{3,1},{4,6},{5,7},{6,4},{7,5},{8,10},{9,11},{10,... | collective-permute-start | bytes 786440 | tf_op jit(solution)/shard_map/ppermute | solution.py:134
  263.2 46.2 %collective-permute-start.76 = (bf16[32,4096]{1,0:T(8,128)(2,1)S(1)}, bf16[32,4096]{1,0:T(8,128)(2,1)S(1)}, u32[]{:S(2)}, u32[]{:S(2)}) collective-permute-start(bf16[32,4096]{1,0:T(8,128)(2,1)S(1)} %get-tuple-element.172.refs_0_), channel_id=1, source_target_pairs={{16,2},{17,3},{18,0},{19,1},{20,6},{21,7},{22,4},{23,5},{24,10},{2... | collective-permute-start | bytes 786440 | tf_op jit(solution)/shard_map/ppermute | solution.py:134
  273.9 36.8 %collective-permute-start.77 = (bf16[32,4096]{1,0:T(8,128)(2,1)S(1)}, bf16[32,4096]{1,0:T(8,128)(2,1)S(1)}, u32[]{:S(2)}, u32[]{:S(2)}) collective-permute-start(bf16[32,4096]{1,0:T(8,128)(2,1)S(1)} %get-tuple-element.172.refs_0_), channel_id=1, source_target_pairs={{0,3},{1,2},{2,1},{3,0},{4,7},{5,6},{6,5},{7,4},{8,11},{9,10},{10,... | collective-permute-start | bytes 786440 | tf_op jit(solution)/shard_map/ppermute | solution.py:134
  277.8 34.3 %collective-permute-start.78 = (bf16[32,4096]{1,0:T(8,128)(2,1)S(1)}, bf16[32,4096]{1,0:T(8,128)(2,1)S(1)}, u32[]{:S(2)}, u32[]{:S(2)}) collective-permute-start(bf16[32,4096]{1,0:T(8,128)(2,1)S(1)} %get-tuple-element.172.refs_0_), channel_id=1, source_target_pairs={{16,3},{17,2},{18,1},{19,0},{20,7},{21,6},{22,5},{23,4},{24,11},{2... | collective-permute-start | bytes 786440 | tf_op jit(solution)/shard_map/ppermute | solution.py:134
  303.6 36.4 %collective-permute-start.28 = (bf16[64,4096]{1,0:T(8,128)(2,1)}, bf16[64,4096]{1,0:T(8,128)(2,1)S(1)}, u32[]{:S(2)}, u32[]{:S(2)}) collective-permute-start(bf16[64,4096]{1,0:T(8,128)(2,1)} %get-tuple-element.74), channel_id=1, source_target_pairs={{0,1},{1,0},{2,3},{3,2},{4,5},{5,4},{6,7},{7,6},{8,9},{9,8},{10,11... | collective-permute-start | bytes 1572872 | tf_op jit(solution)/shard_map/ppermute | solution.py:134
  305.5 52.1 %collective-permute-start.26 = (bf16[32,4096]{1,0:T(8,128)(2,1)S(1)}, bf16[32,4096]{1,0:T(8,128)(2,1)S(1)}, u32[]{:S(2)}, u32[]{:S(2)}) collective-permute-start(bf16[32,4096]{1,0:T(8,128)(2,1)S(1)} %get-tuple-element.71), channel_id=1, source_target_pairs={{0,1},{1,0},{2,3},{3,2},{4,5},{5,4},{6,7},{7,6},{8,9},{9,8},{10,11... | collective-permute-start | bytes 786440 | tf_op jit(solution)/shard_map/ppermute | solution.py:134
  309.4 50.1 %collective-permute-start.27 = (bf16[32,4096]{1,0:T(8,128)(2,1)S(1)}, bf16[32,4096]{1,0:T(8,128)(2,1)S(1)}, u32[]{:S(2)}, u32[]{:S(2)}) collective-permute-start(bf16[32,4096]{1,0:T(8,128)(2,1)S(1)} %get-tuple-element.72), channel_id=1, source_target_pairs={{0,17},{1,16},{2,19},{3,18},{4,21},{5,20},{6,23},{7,22},{8,25},{9,... | collective-permute-start | bytes 786440 | tf_op jit(solution)/shard_map/ppermute | solution.py:134
  310.8 50.1 %collective-permute-start.31 = (bf16[32,4096]{1,0:T(8,128)(2,1)S(1)}, bf16[32,4096]{1,0:T(8,128)(2,1)S(1)}, u32[]{:S(2)}, u32[]{:S(2)}) collective-permute-start(bf16[32,4096]{1,0:T(8,128)(2,1)S(1)} %get-tuple-element.76), channel_id=1, source_target_pairs={{0,16},{1,17},{2,18},{3,19},{4,20},{5,21},{6,22},{7,23},{8,24},{9,... | collective-permute-start | bytes 786440 | tf_op jit(solution)/shard_map/ppermute | solution.py:134
  414.4 40.1 %collective-permute-start.87 = (bf16[32,4096]{1,0:T(8,128)(2,1)S(1)}, bf16[32,4096]{1,0:T(8,128)(2,1)S(1)}, u32[]{:S(2)}, u32[]{:S(2)}) collective-permute-start(bf16[32,4096]{1,0:T(8,128)(2,1)S(1)} %get-tuple-element.170.refs_1_), channel_id=1, source_target_pairs={{16,17},{17,16},{18,19},{19,18},{20,21},{21,20},{22,23},{23,22},{2... | collective-permute-start | bytes 786440 | tf_op jit(solution)/shard_map/ppermute | solution.py:134
  415.1 40.1 %collective-permute-start.88 = (bf16[32,4096]{1,0:T(8,128)(2,1)S(1)}, bf16[32,4096]{1,0:T(8,128)(2,1)S(1)}, u32[]{:S(2)}, u32[]{:S(2)}) collective-permute-start(bf16[32,4096]{1,0:T(8,128)(2,1)S(1)} %get-tuple-element.170.refs_1_), channel_id=1, source_target_pairs={{0,18},{1,19},{2,16},{3,17},{4,22},{5,23},{6,20},{7,21},{8,26},{9,... | collective-permute-start | bytes 786440 | tf_op jit(solution)/shard_map/ppermute | solution.py:134
  485.6 30.9 %collective-permute-start.97 = (bf16[32,4096]{1,0:T(8,128)(2,1)S(1)}, bf16[32,4096]{1,0:T(8,128)(2,1)S(1)}, u32[]{:S(2)}, u32[]{:S(2)}) collective-permute-start(bf16[32,4096]{1,0:T(8,128)(2,1)S(1)} %get-tuple-element.112), channel_id=1, source_target_pairs={{16,0},{17,1},{18,2},{19,3},{20,4},{21,5},{22,6},{23,7},{24,8},{25... | collective-permute-start | bytes 786440 | tf_op jit(solution)/shard_map/ppermute | solution.py:134
  499.5 30.6 %collective-permute-start.95 = (bf16[32,4096]{1,0:T(8,128)(2,1)S(1)}, bf16[32,4096]{1,0:T(8,128)(2,1)S(1)}, u32[]{:S(2)}, u32[]{:S(2)}) collective-permute-start(bf16[32,4096]{1,0:T(8,128)(2,1)S(1)} %get-tuple-element.146), channel_id=1, source_target_pairs={{16,2},{17,3},{18,0},{19,1},{20,6},{21,7},{22,4},{23,5},{24,10},{2... | collective-permute-start | bytes 786440 | tf_op jit(solution)/shard_map/ppermute | solution.py:134
  565.3 35.8 %collective-permute-start.47 = (bf16[32,4096]{1,0:T(8,128)(2,1)S(1)}, bf16[32,4096]{1,0:T(8,128)(2,1)S(1)}, u32[]{:S(2)}, u32[]{:S(2)}) collective-permute-start(bf16[32,4096]{1,0:T(8,128)(2,1)S(1)} %get-tuple-element.169.refs_1_), channel_id=1, source_target_pairs={{16,17},{17,16},{18,19},{19,18},{20,21},{21,20},{22,23},{23,22},{2... | collective-permute-start | bytes 786440 | tf_op jit(solution)/shard_map/ppermute | solution.py:134
  566.0 35.8 %collective-permute-start.48 = (bf16[32,4096]{1,0:T(8,128)(2,1)S(1)}, bf16[32,4096]{1,0:T(8,128)(2,1)S(1)}, u32[]{:S(2)}, u32[]{:S(2)}) collective-permute-start(bf16[32,4096]{1,0:T(8,128)(2,1)S(1)} %get-tuple-element.169.refs_1_), channel_id=1, source_target_pairs={{0,18},{1,19},{2,16},{3,17},{4,22},{5,23},{6,20},{7,21},{8,26},{9,... | collective-permute-start | bytes 786440 | tf_op jit(solution)/shard_map/ppermute | solution.py:134
  569.0 34.1 %collective-permute-start.49 = (bf16[32,4096]{1,0:T(8,128)(2,1)S(1)}, bf16[32,4096]{1,0:T(8,128)(2,1)S(1)}, u32[]{:S(2)}, u32[]{:S(2)}) collective-permute-start(bf16[32,4096]{1,0:T(8,128)(2,1)S(1)} %get-tuple-element.169.refs_1_), channel_id=1, source_target_pairs={{16,18},{17,19},{18,16},{19,17},{20,22},{21,23},{22,20},{23,21},{2... | collective-permute-start | bytes 786440 | tf_op jit(solution)/shard_map/ppermute | solution.py:134
  570.0 33.8 %collective-permute-start.50 = (bf16[32,4096]{1,0:T(8,128)(2,1)S(1)}, bf16[32,4096]{1,0:T(8,128)(2,1)S(1)}, u32[]{:S(2)}, u32[]{:S(2)}) collective-permute-start(bf16[32,4096]{1,0:T(8,128)(2,1)S(1)} %get-tuple-element.169.refs_1_), channel_id=1, source_target_pairs={{0,19},{1,18},{2,17},{3,16},{4,23},{5,22},{6,21},{7,20},{8,27},{9,... | collective-permute-start | bytes 786440 | tf_op jit(solution)/shard_map/ppermute | solution.py:134
  601.8 30.8 %collective-permute-start.105 = (bf16[32,4096]{1,0:T(8,128)(2,1)S(1)}, bf16[32,4096]{1,0:T(8,128)(2,1)S(1)}, u32[]{:S(2)}, u32[]{:S(2)}) collective-permute-start(bf16[32,4096]{1,0:T(8,128)(2,1)S(1)} %get-tuple-element.114), channel_id=1, source_target_pairs={{16,1},{17,0},{18,3},{19,2},{20,5},{21,4},{22,7},{23,6},{24,9},{25... | collective-permute-start | bytes 786440 | tf_op jit(solution)/shard_map/ppermute | solution.py:134
  603.1 30.8 %collective-permute-start.106 = (bf16[32,4096]{1,0:T(8,128)(2,1)S(1)}, bf16[32,4096]{1,0:T(8,128)(2,1)S(1)}, u32[]{:S(2)}, u32[]{:S(2)}) collective-permute-start(bf16[32,4096]{1,0:T(8,128)(2,1)S(1)} %get-tuple-element.115), channel_id=1, source_target_pairs={{16,17},{17,16},{18,19},{19,18},{20,21},{21,20},{22,23},{23,22},{2... | collective-permute-start | bytes 786440 | tf_op jit(solution)/shard_map/ppermute | solution.py:134
  603.8 30.8 %collective-permute-start.110 = (bf16[32,4096]{1,0:T(8,128)(2,1)S(1)}, bf16[32,4096]{1,0:T(8,128)(2,1)S(1)}, u32[]{:S(2)}, u32[]{:S(2)}) collective-permute-start(bf16[32,4096]{1,0:T(8,128)(2,1)S(1)} %get-tuple-element.119), channel_id=1, source_target_pairs={{16,0},{17,1},{18,2},{19,3},{20,4},{21,5},{22,6},{23,7},{24,8},{25... | collective-permute-start | bytes 786440 | tf_op jit(solution)/shard_map/ppermute | solution.py:134
  632.6 30.8 %collective-permute-start.52 = (bf16[32,4096]{1,0:T(8,128)(2,1)S(1)}, bf16[32,4096]{1,0:T(8,128)(2,1)S(1)}, u32[]{:S(2)}, u32[]{:S(2)}) collective-permute-start(bf16[32,4096]{1,0:T(8,128)(2,1)S(1)} %get-tuple-element.85), channel_id=1, source_target_pairs={{16,1},{17,0},{18,3},{19,2},{20,5},{21,4},{22,7},{23,6},{24,9},{25... | collective-permute-start | bytes 786440 | tf_op jit(solution)/shard_map/ppermute | solution.py:134
  634.6 31.5 %collective-permute-start.57 = (bf16[32,4096]{1,0:T(8,128)(2,1)S(1)}, bf16[32,4096]{1,0:T(8,128)(2,1)S(1)}, u32[]{:S(2)}, u32[]{:S(2)}) collective-permute-start(bf16[32,4096]{1,0:T(8,128)(2,1)S(1)} %get-tuple-element.90), channel_id=1, source_target_pairs={{16,0},{17,1},{18,2},{19,3},{20,4},{21,5},{22,6},{23,7},{24,8},{25... | collective-permute-start | bytes 786440 | tf_op jit(solution)/shard_map/ppermute | solution.py:134
  (94 other events, 1841.5 us)

commit v3 on v2

--- a/solution.py
+++ b/solution.py
@@ -134,63 +134,78 @@
     return lax.ppermute(value, BOTH, links)
 
 
-def relayed(j):
-    return j & (j - 1) != 0
+def slot_order(count):
+    bits = [1 << bit for bit in range(count.bit_length() - 1)]
+    groups, left = [], list(range(count))
+    for bit in bits[:-1]:
+        groups.append([j for j in left if j & bit])
+        left = [j for j in left if not j & bit]
+    return groups, left
 
 
 def row_cuts(length):
     sections, tensors = lax.axis_size("section"), lax.axis_size("tensor")
     share = length // tensors
-    cuts = []
-    for j in range(tensors):
-        cuts += [share] if relayed(j) else [share // sections] * sections
-    return cuts
+    groups, left = slot_order(tensors)
+    return [len(g) * share for g in groups] + [share // sections] * (sections * len(left))
 
 
 def gather_rows(own, layer):
+    groups, left = slot_order(lax.axis_size("tensor"))
     pieces = []
-    for j in range(lax.axis_size("tensor")):
+    for j in sum(groups, []) + left:
         for source in range(lax.axis_size("section")):
             local = j == 0 and source == layer
             pieces.append(own if local else send(own, source, layer, j))
     return pieces
 
 
-def scatter_rows(partial, layer):
+def sum_nearby(partial, layer):
     sections, tensors = lax.axis_size("section"), lax.axis_size("tensor")
-    partial = list(partial)
+    groups, left = slot_order(tensors)
+    rows = partial[-1].shape[0]
     held = {}
-    for j in range(tensors):
-        if relayed(j):
-            held[j] = partial.pop(0)
-        else:
-            held[j] = [partial.pop(0) for _ in range(sections)]
-    sums = jnp.where(lax.axis_index("section") == layer, held[0][layer], 0).astype(jnp.float32)
-    arrived = []
-    for bit in range(tensors.bit_length() - 1):
-        distance = 1 << bit
-        for j in [j for j in range(tensors - 1, 0, -1) if j in held and j & distance]:
-            piece = held.pop(j)
-            if relayed(j):
-                part = send(piece.astype(jnp.bfloat16), layer, layer, distance)
-                part = part.astype(jnp.float32)
-                into = held[j ^ distance]
-                if relayed(j ^ distance):
-                    held[j ^ distance] = into.astype(jnp.float32) + part
-                else:
-                    rows = into[0].shape[0]
-                    held[j ^ distance] = [
-                        p.astype(jnp.float32) + part[h * rows : (h + 1) * rows]
-                        for h, p in enumerate(into)
-                    ]
-            else:
-                arrived += [
-                    send(p.astype(jnp.bfloat16), layer, h, distance) for h, p in enumerate(piece)
-                ]
-    arrived += [send(held[0][h], layer, h, 0) for h in range(sections) if h != layer]
+    for group, array in zip(groups, partial):
+        for k, j in enumerate(group):
+            for h in range(sections):
+                start = (k * sections + h) * rows
+                held[j, h] = (array, start)
+    for k, j in enumerate(left):
+        for h in range(sections):
+            held[j, h] = (partial[len(groups) + k * sections + h], 0)
+    value = lambda entry: entry[0][entry[1] : entry[1] + rows].astype(jnp.float32)
+    for step, group in enumerate(groups):
+        whole_group = held[group[0], 0][0]
+        if whole_group.shape[0] != rows * sections * len(group):
+            whole_group = jnp.concatenate(
+                [value(held[j, h]) for j in group for h in range(sections)]
+            ).astype(jnp.bfloat16)
+        arrived = send(whole_group, layer, layer, 1 << step)
+        for k, j in enumerate(group):
+            for h in range(sections):
+                start = (k * sections + h) * rows
+                to = (j ^ (1 << step), h)
+                held[to] = (value(held[to]) + value((arrived, start)), 0)
+    return [[value(held[j, h]).astype(jnp.bfloat16) for h in range(sections)] for j in left]
+
+
+def send_to_owners(nearby, layer):
+    sections, tensors = lax.axis_size("section"), lax.axis_size("tensor")
+    near, far = nearby if len(nearby) == 2 else (nearby[0], [])
+    arrived = [send(piece, layer, h, tensors // 2) for h, piece in enumerate(far)]
+    return arrived + [send(near[h], layer, h, 0) for h in range(sections) if h != layer]
+
+
+def sum_arrived(nearby, arrived, layer):
+    sums = jnp.where(lax.axis_index("section") == layer, nearby[0][layer], 0)
+    sums = sums.astype(jnp.float32)
     for part in arrived:
         sums = sums + part.astype(jnp.float32)
     return sums
+
+
+def after(values, *others):
+    return lax.optimization_barrier((values, others))[0]
 
 
 def layer_gains(gain):
@@ -225,7 +240,6 @@
     batch, batches = lax.axis_index("batch"), lax.axis_size("batch")
     per_device, length = ids_beam.shape
     share = length // tensors
-    slots = jnp.arange(tensors, dtype=jnp.int32) ^ tensor
 
     owned = batch * per_device + jnp.arange(per_device, dtype=jnp.int32)
     beams_owned = jnp.take(beam_map, owned)
@@ -239,6 +253,8 @@
     holder = (batch - beams_owned // per_device) % batches
     tokens = blocks[holder * per_device + beams_owned % per_device]
 
+    groups, left = slot_order(tensors)
+    slots = jnp.asarray(sum(groups, []) + left, jnp.int32) ^ tensor
     cosine, sine = rope_tables(length)
     by_slot = lambda t: jnp.asarray(t.reshape(tensors, share, -1))[slots].reshape(length, -1)
     cosine, sine = by_slot(cosine), by_slot(sine)
@@ -248,12 +264,8 @@
     rows = share // sections
     cuts = row_cuts(length)
     gains_attn, gains_mlp = layer_gains(gain_attn), layer_gains(gain_mlp)
-    hidden, first = [], []
-    embedded = None
-    for c in range(per_device):
-        looked = jnp.take(embed_table, tokens[c], axis=0)
-        if embedded is not None:
-            looked, first[-1][0] = lax.optimization_barrier((looked, first[-1][0]))
+
+    def embed(looked):
         columns = []
         for source in range(sections):
             pieces = jnp.stack(
@@ -267,9 +279,9 @@
             ]
         embedded = jnp.concatenate(columns, axis=1)
         normed = rms_norm(embedded, gains_attn[0])
-        first.append(
-            [lax.dynamic_slice_in_dim(normed, slots[j] * share, share, 0) for j in range(tensors)]
-        )
+        pieces = [
+            lax.dynamic_slice_in_dim(normed, slots[j] * share, share, 0) for j in range(tensors)
+        ]
         own = [
             lax.dynamic_slice_in_dim(embedded, tensor * share + h * rows, rows, 0)
             for h in range(sections)
@@ -277,26 +289,42 @@
         mine = own[0]
         for h in range(1, sections):
             mine = jnp.where(section == h, send(own[h], 0, h, 0), mine)
-        hidden.append(mine)
-
-    for layer in range(sections):
+        return pieces, mine
+
+    def compute(half, pieces):
+        if half % 2:
+            return fused(mlp_kernel, "mlp", (), (w_gate, w_up), w_down, pieces, cuts)
+        weights = (w_query, w_key, w_value)
+        return fused(attention_kernel, "attention", tables, weights, w_out, pieces, cuts)
+
+    def add(base, sums):
+        return (base.astype(jnp.float32) + sums).astype(jnp.bfloat16)
+
+    halves = 2 * sections
+    gains = [gains_attn[half // 2] if half % 2 == 0 else gains_mlp[half // 2] for half in range(halves)]
+    looked = [jnp.take(embed_table, tokens[c], axis=0) for c in range(per_device)]
+    hidden = [None] * per_device
+    nearby = [None] * per_device
+    arrived = [None] * per_device
+    for half in range(halves):
         for c in range(per_device):
-            pieces = first[c] if layer == 0 else gather_rows(rms_norm(hidden[c], gains_attn[layer]), layer)
-            partial = fused(
-                attention_kernel,
-                "attention",
-                tables,
-                (w_query, w_key, w_value),
-                w_out,
-                pieces,
-                cuts,
-            )
-            attn_sum = scatter_rows(partial, layer)
-            middle = (hidden[c].astype(jnp.float32) + attn_sum).astype(jnp.bfloat16)
-            pieces = gather_rows(rms_norm(middle, gains_mlp[layer]), layer)
-            partial = fused(mlp_kernel, "mlp", (), (w_gate, w_up), w_down, pieces, cuts)
-            mlp_sum = scatter_rows(partial, layer)
-            hidden[c] = (middle.astype(jnp.float32) + mlp_sum).astype(jnp.bfloat16)
+            if half == 0:
+                if c:
+                    looked[c] = after(looked[c], partial[-1])
+                pieces, hidden[c] = embed(looked[c])
+            else:
+                if c or half > 1 or per_device > 1:
+                    arrived[c] = after(arrived[c], partial[-1])
+                hidden[c] = add(hidden[c], sum_arrived(nearby[c], arrived[c], (half - 1) // 2))
+                pieces = gather_rows(rms_norm(hidden[c], gains[half]), half // 2)
+            if half or c:
+                before = (c - 1) % per_device
+                pieces = after(pieces, nearby[before])
+            partial = compute(half, pieces)
+            nearby[c] = sum_nearby(partial, half // 2)
+            arrived[c] = send_to_owners(nearby[c], half // 2)
+    for c in range(per_device):
+        hidden[c] = add(hidden[c], sum_arrived(nearby[c], arrived[c], sections - 1))
 
     finals = jnp.stack(hidden)
     half = finals.shape[2] // sections

time: 701 us -> 793 us (1.13)
  starting transfers between devices: 257 us -> 328 us
  waiting for transfers between devices: 203 us -> 227 us
    ppermute x106 -> x90, starting transfers between devices: 237 us -> 312 us  [send(): return lax.ppermute(value, BOTH, links)]
    ppermute x106 -> x90, waiting for transfers between devices: 200 us -> 222 us  [send(): return lax.ppermute(value, BOTH, links)]
  transfers between devices with their start and end apart: 119 -> 103, of which waited for: 32 -> 23; matrix products, arithmetic and copies ran while one was open for 5% -> 4% of each run, Pallas kernels for 27% -> 18%
where the time goes in v3:
time: 793 us; the launch traced here: 785 us
  starting transfers between devices  328 us (41%)
  waiting for transfers between devices  227 us (29%)
  Pallas kernels  187 us (24%)
  local copies, waits for them, and re-layouts  25.4 us (3%)
  other arithmetic  12.5 us (2%)
    ppermute x90, starting transfers between devices, send(): return lax.ppermute(value, BOTH, links)  312 us
    ppermute x90, waiting for transfers between devices, send(): return lax.ppermute(value, BOTH, links)  222 us
    pallas_call x8, Pallas kernels, fused(): pl.pallas_call(functools.partial(kernel, len(pieces)), out_shape=[jax.Sha...  187 us
    gather x2, local copies, waits for them, and re-layouts, body(): jnp.take(embed_table, tokens[c], axis=0)  18 us
  transfers between devices with their start and end apart: 103, of which 23 were waited for; matrix products, arithmetic and copies ran while one was open for 4% of the time, Pallas kernels for 18%

profile of v3, /device:TPU:0, one launch (start us, length us, event | category | flops | bytes accessed | tf_op | source)
XLA Modules:
  0.0 785.2 jit_solution(2707169119332530662)
XLA Ops:
  15.2 9.0 %gather_fusion.5 = bf16[256,512]{1,0:T(8,128)(2,1)S(1)} fusion(bf16[16000,512]{1,0:T(8,128)(2,1)} %param.25, s32[1024]{0:T(1024)S(1)} %pad_clamp_fusion.2), kind=kCustom, calls=%fused_computation.1.clone | custom fusion | bytes 525312 | tf_op jit(solution)/shard_map/jit(_take)/gather | solution.py:305
  24.3 5.5 collective-permute-start.5
  34.5 9.0 %gather_fusion.6 = bf16[256,512]{1,0:T(8,128)(2,1)S(1)} fusion(bf16[16000,512]{1,0:T(8,128)(2,1)} %param.25, s32[1024]{0:T(1024)S(1)} %pad_clamp_fusion), kind=kCustom, calls=%fused_computation.3.clone | custom fusion | bytes 525312 | tf_op jit(solution)/shard_map/jit(_take)/gather | solution.py:305
  57.5 17.1 %collective-permute-done.8 = bf16[256,512]{1,0:T(8,128)(2,1)S(1)} collective-permute-done((bf16[256,512]{1,0:T(8,128)(2,1)S(1)}, bf16[256,512]{1,0:T(8,128)(2,1)S(1)}, u32[]{:S(2)}, u32[]{:S(2)}) %collective-permute-start.8) | collective-permute-done | bytes 262176 | tf_op jit(solution)/shard_map/ppermute | solution.py:134
  76.3 22.2 %attention.4 = (bf16[128,4096]{1,0:T(8,128)(2,1)}, bf16[32,4096]{1,0:T(8,128)(2,1)S(1)}, bf16[32,4096]{1,0:T(8,128)(2,1)S(1)}, bf16[32,4096]{1,0:T(8,128)(2,1)S(1)}, bf16[32,4096]{1,0:T(8,128)(2,1)S(1)}) custom-call(f32[256,128]{1,0:T(8,128)S(1)} %bitcast.75, f32[256,128]{1,0:T(8,128)S(1)} %bitcast.79, s32[256,1]{1,0:T(8,128)S(1)} %add.571.row_ref, ...), custom_call_target="tpu_custom_call" | custom-call | flops 8589934592 | bytes 37748736 | tf_op jit(solution)/shard_map/attention/pallas_call | solution.py:110
  98.5 6.2 collective-permute-start.18
  113.3 14.1 %collective-permute-done.17 = bf16[256,512]{1,0:T(8,128)(2,1)S(1)} collective-permute-done((bf16[256,512]{1,0:T(8,128)(2,1)S(1)}, bf16[256,512]{1,0:T(8,128)(2,1)S(1)}, u32[]{:S(2)}, u32[]{:S(2)}) %collective-permute-start.17) | collective-permute-done | bytes 262176 | tf_op jit(solution)/shard_map/ppermute | solution.py:134
  144.9 11.1 %collective-permute-done.12 = bf16[128,4096]{1,0:T(8,128)(2,1)S(1)} collective-permute-done((bf16[128,4096]{1,0:T(8,128)(2,1)}, bf16[128,4096]{1,0:T(8,128)(2,1)S(1)}, u32[]{:S(2)}, u32[]{:S(2)}) %collective-permute-start.12) | collective-permute-done | bytes 1048608 | tf_op jit(solution)/shard_map/ppermute | solution.py:134
  160.9 22.2 %attention.5 = (bf16[128,4096]{1,0:T(8,128)(2,1)}, bf16[32,4096]{1,0:T(8,128)(2,1)S(1)}, bf16[32,4096]{1,0:T(8,128)(2,1)S(1)}, bf16[32,4096]{1,0:T(8,128)(2,1)S(1)}, bf16[32,4096]{1,0:T(8,128)(2,1)S(1)}) custom-call(f32[256,128]{1,0:T(8,128)S(1)} %bitcast.76, f32[256,128]{1,0:T(8,128)S(1)} %bitcast.80, s32[256,1]{1,0:T(8,128)S(1)} %add.571.row_ref, ...), custom_call_target="tpu_custom_call" | custom-call | flops 8589934592 | bytes 37748736 | tf_op jit(solution)/shard_map/attention/pallas_call | solution.py:110
  196.7 18.9 %collective-permute-done.24.refs_0_ = bf16[32,4096]{1,0:T(8,128)(2,1)S(1)} collective-permute-done((bf16[32,4096]{1,0:T(8,128)(2,1)S(1)}, bf16[32,4096]{1,0:T(8,128)(2,1)S(1)}, u32[]{:S(2)}, u32[]{:S(2)}) %collective-permute-start.24) | collective-permute-done | bytes 262176 | tf_op jit(solution)/shard_map/ppermute | solution.py:134
  216.9 6.2 collective-permute-start.29
  234.8 10.5 %collective-permute-done.29.refs_6_ = bf16[32,4096]{1,0:T(8,128)(2,1)S(1)} collective-permute-done((bf16[32,4096]{1,0:T(8,128)(2,1)S(1)}, bf16[32,4096]{1,0:T(8,128)(2,1)S(1)}, u32[]{:S(2)}, u32[]{:S(2)}) %collective-permute-start.29) | collective-permute-done | bytes 262176 | tf_op jit(solution)/shard_map/ppermute | solution.py:134
  246.6 24.6 %mlp.4 = (bf16[128,4096]{1,0:T(8,128)(2,1)}, bf16[32,4096]{1,0:T(8,128)(2,1)S(1)}, bf16[32,4096]{1,0:T(8,128)(2,1)S(1)}, bf16[32,4096]{1,0:T(8,128)(2,1)S(1)}, bf16[32,4096]{1,0:T(8,128)(2,1)S(1)}) custom-call(bf16[1,4096,2048]{2,1,0:T(8,128)(2,1)} %wg_ref.7, bf16[1,4096,2048]{2,1,0:T(8,128)(2,1)} %wu_ref.7, bf16[1,2048,4096]{2,1,0:T(8,128)(2,1)} %wd_ref.7, ...), custom_call_target="tpu_custom_call" | custom-call | flops 12884901888 | bytes 54525952 | tf_op jit(solution)/shard_map/mlp/pallas_call | solution.py:110
  284.0 25.5 %collective-permute-done.40.refs_0_ = bf16[32,4096]{1,0:T(8,128)(2,1)S(1)} collective-permute-done((bf16[32,4096]{1,0:T(8,128)(2,1)S(1)}, bf16[32,4096]{1,0:T(8,128)(2,1)S(1)}, u32[]{:S(2)}, u32[]{:S(2)}) %collective-permute-start.40) | collective-permute-done | bytes 262176 | tf_op jit(solution)/shard_map/ppermute | solution.py:134
  323.5 10.1 %collective-permute-done.45.refs_6_ = bf16[32,4096]{1,0:T(8,128)(2,1)S(1)} collective-permute-done((bf16[32,4096]{1,0:T(8,128)(2,1)S(1)}, bf16[32,4096]{1,0:T(8,128)(2,1)S(1)}, u32[]{:S(2)}, u32[]{:S(2)}) %collective-permute-start.45) | collective-permute-done | bytes 262176 | tf_op jit(solution)/shard_map/ppermute | solution.py:134
  333.6 24.6 %mlp.5 = (bf16[128,4096]{1,0:T(8,128)(2,1)}, bf16[32,4096]{1,0:T(8,128)(2,1)S(1)}, bf16[32,4096]{1,0:T(8,128)(2,1)S(1)}, bf16[32,4096]{1,0:T(8,128)(2,1)S(1)}, bf16[32,4096]{1,0:T(8,128)(2,1)S(1)}) custom-call(bf16[1,4096,2048]{2,1,0:T(8,128)(2,1)} %wg_ref.7, bf16[1,4096,2048]{2,1,0:T(8,128)(2,1)} %wu_ref.7, bf16[1,2048,4096]{2,1,0:T(8,128)(2,1)} %wd_ref.7, ...), custom_call_target="tpu_custom_call" | custom-call | flops 12884901888 | bytes 54525952 | tf_op jit(solution)/shard_map/mlp/pallas_call | solution.py:110
  364.6 24.9 %collective-permute-done.47.refs_0_ = bf16[32,4096]{1,0:T(8,128)(2,1)S(1)} collective-permute-done((bf16[32,4096]{1,0:T(8,128)(2,1)S(1)}, bf16[32,4096]{1,0:T(8,128)(2,1)S(1)}, u32[]{:S(2)}, u32[]{:S(2)}) %collective-permute-start.47) | collective-permute-done | bytes 262176 | tf_op jit(solution)/shard_map/ppermute | solution.py:134
  389.5 8.6 %collective-permute-start.51 = (bf16[32,4096]{1,0:T(8,128)(2,1)S(1)}, bf16[32,4096]{1,0:T(8,128)(2,1)S(1)}, u32[]{:S(2)}, u32[]{:S(2)}) collective-permute-start(bf16[32,4096]{1,0:T(8,128)(2,1)S(1)} %fusion.16.refs_5_), channel_id=1, source_target_pairs={{0,16},{1,17},{2,18},{3,19},{4,20},{5,21},{6,22},{7,23},{8,24},{9,... | collective-permute-start | bytes 786440 | tf_op jit(solution)/shard_map/ppermute | solution.py:134
  407.3 22.2 %attention.6 = (bf16[128,4096]{1,0:T(8,128)(2,1)}, bf16[32,4096]{1,0:T(8,128)(2,1)S(1)}, bf16[32,4096]{1,0:T(8,128)(2,1)S(1)}, bf16[32,4096]{1,0:T(8,128)(2,1)S(1)}, bf16[32,4096]{1,0:T(8,128)(2,1)S(1)}) custom-call(f32[256,128]{1,0:T(8,128)S(1)} %bitcast.77, f32[256,128]{1,0:T(8,128)S(1)} %bitcast.81, s32[256,1]{1,0:T(8,128)S(1)} %add.571.row_ref, ...), custom_call_target="tpu_custom_call" | custom-call | flops 8589934592 | bytes 37748736 | tf_op jit(solution)/shard_map/attention/pallas_call | solution.py:110
  430.8 15.4 %collective-permute-start.62 = (bf16[32,4096]{1,0:T(8,128)(2,1)S(1)}, bf16[32,4096]{1,0:T(8,128)(2,1)S(1)}, u32[]{:S(2)}, u32[]{:S(2)}) collective-permute-start(bf16[32,4096]{1,0:T(8,128)(2,1)S(1)} %fusion.20.refs_5_), channel_id=1, source_target_pairs={{0,17},{1,16},{2,19},{3,18},{4,21},{5,20},{6,23},{7,22},{8,25},{9,... | collective-permute-start | bytes 786440 | tf_op jit(solution)/shard_map/ppermute | solution.py:134
  446.8 6.2 collective-permute-start.64
  456.9 20.6 %collective-permute-start.67 = (bf16[32,4096]{1,0:T(8,128)(2,1)S(1)}, bf16[32,4096]{1,0:T(8,128)(2,1)S(1)}, u32[]{:S(2)}, u32[]{:S(2)}) collective-permute-start(bf16[32,4096]{1,0:T(8,128)(2,1)S(1)} %fusion.20.refs_5_), channel_id=1, source_target_pairs={{0,18},{1,19},{2,16},{3,17},{4,22},{5,23},{6,20},{7,21},{8,26},{9,... | collective-permute-start | bytes 786440 | tf_op jit(solution)/shard_map/ppermute | solution.py:134
  482.0 22.2 %attention.7 = (bf16[128,4096]{1,0:T(8,128)(2,1)}, bf16[32,4096]{1,0:T(8,128)(2,1)S(1)}, bf16[32,4096]{1,0:T(8,128)(2,1)S(1)}, bf16[32,4096]{1,0:T(8,128)(2,1)S(1)}, bf16[32,4096]{1,0:T(8,128)(2,1)S(1)}) custom-call(f32[256,128]{1,0:T(8,128)S(1)} %bitcast.78, f32[256,128]{1,0:T(8,128)S(1)} %bitcast.82, s32[256,1]{1,0:T(8,128)S(1)} %add.571.row_ref, ...), custom_call_target="tpu_custom_call" | custom-call | flops 8589934592 | bytes 37748736 | tf_op jit(solution)/shard_map/attention/pallas_call | solution.py:110
  506.4 22.4 %collective-permute-start.69 = (bf16[32,4096]{1,0:T(8,128)(2,1)S(1)}, bf16[32,4096]{1,0:T(8,128)(2,1)S(1)}, u32[]{:S(2)}, u32[]{:S(2)}) collective-permute-start(bf16[32,4096]{1,0:T(8,128)(2,1)S(1)} %fusion.24.refs_5_), channel_id=1, source_target_pairs={{0,17},{1,16},{2,19},{3,18},{4,21},{5,20},{6,23},{7,22},{8,25},{9,... | collective-permute-start | bytes 786440 | tf_op jit(solution)/shard_map/ppermute | solution.py:134
  538.4 20.9 %collective-permute-start.74 = (bf16[32,4096]{1,0:T(8,128)(2,1)S(1)}, bf16[32,4096]{1,0:T(8,128)(2,1)S(1)}, u32[]{:S(2)}, u32[]{:S(2)}) collective-permute-start(bf16[32,4096]{1,0:T(8,128)(2,1)S(1)} %fusion.24.refs_5_), channel_id=1, source_target_pairs={{0,18},{1,19},{2,16},{3,17},{4,22},{5,23},{6,20},{7,21},{8,26},{9,... | collective-permute-start | bytes 786440 | tf_op jit(solution)/shard_map/ppermute | solution.py:134
  563.6 24.6 %mlp.6 = (bf16[128,4096]{1,0:T(8,128)(2,1)}, bf16[32,4096]{1,0:T(8,128)(2,1)S(1)}, bf16[32,4096]{1,0:T(8,128)(2,1)S(1)}, bf16[32,4096]{1,0:T(8,128)(2,1)S(1)}, bf16[32,4096]{1,0:T(8,128)(2,1)S(1)}) custom-call(bf16[1,4096,2048]{2,1,0:T(8,128)(2,1)} %wg_ref.7, bf16[1,4096,2048]{2,1,0:T(8,128)(2,1)} %wu_ref.7, bf16[1,2048,4096]{2,1,0:T(8,128)(2,1)} %wd_ref.7, ...), custom_call_target="tpu_custom_call" | custom-call | flops 12884901888 | bytes 54525952 | tf_op jit(solution)/shard_map/mlp/pallas_call | solution.py:110
  590.5 24.9 %collective-permute-start.84 = (bf16[32,4096]{1,0:T(8,128)(2,1)S(1)}, bf16[32,4096]{1,0:T(8,128)(2,1)S(1)}, u32[]{:S(2)}, u32[]{:S(2)}) collective-permute-start(bf16[32,4096]{1,0:T(8,128)(2,1)S(1)} %fusion.28.refs_5_), channel_id=1, source_target_pairs={{0,17},{1,16},{2,19},{3,18},{4,21},{5,20},{6,23},{7,22},{8,25},{9,... | collective-permute-start | bytes 786440 | tf_op jit(solution)/shard_map/ppermute | solution.py:134
  620.7 25.4 %collective-permute-start.86 = (bf16[32,4096]{1,0:T(8,128)(2,1)S(1)}, bf16[32,4096]{1,0:T(8,128)(2,1)S(1)}, u32[]{:S(2)}, u32[]{:S(2)}) collective-permute-start(bf16[32,4096]{1,0:T(8,128)(2,1)S(1)} %fusion.28.refs_5_), channel_id=1, source_target_pairs={{0,19},{1,18},{2,17},{3,16},{4,23},{5,22},{6,21},{7,20},{8,27},{9,... | collective-permute-start | bytes 786440 | tf_op jit(solution)/shard_map/ppermute | solution.py:134
  650.0 16.1 %collective-permute-start.89 = (bf16[32,4096]{1,0:T(8,128)(2,1)S(1)}, bf16[32,4096]{1,0:T(8,128)(2,1)S(1)}, u32[]{:S(2)}, u32[]{:S(2)}) collective-permute-start(bf16[32,4096]{1,0:T(8,128)(2,1)S(1)} %fusion.28.refs_5_), channel_id=1, source_target_pairs={{0,18},{1,19},{2,16},{3,17},{4,22},{5,23},{6,20},{7,21},{8,26},{9,... | collective-permute-start | bytes 786440 | tf_op jit(solution)/shard_map/ppermute | solution.py:134
  671.7 24.6 %mlp.7 = (bf16[128,4096]{1,0:T(8,128)(2,1)}, bf16[32,4096]{1,0:T(8,128)(2,1)S(1)}, bf16[32,4096]{1,0:T(8,128)(2,1)S(1)}, bf16[32,4096]{1,0:T(8,128)(2,1)S(1)}, bf16[32,4096]{1,0:T(8,128)(2,1)S(1)}) custom-call(bf16[1,4096,2048]{2,1,0:T(8,128)(2,1)} %wg_ref.7, bf16[1,4096,2048]{2,1,0:T(8,128)(2,1)} %wu_ref.7, bf16[1,2048,4096]{2,1,0:T(8,128)(2,1)} %wd_ref.7, ...), custom_call_target="tpu_custom_call" | custom-call | flops 12884901888 | bytes 54525952 | tf_op jit(solution)/shard_map/mlp/pallas_call | solution.py:110
  701.7 44.8 %collective-permute-done.94 = bf16[32,4096]{1,0:T(8,128)(2,1)S(1)} collective-permute-done((bf16[32,4096]{1,0:T(8,128)(2,1)S(1)}, bf16[32,4096]{1,0:T(8,128)(2,1)S(1)}, u32[]{:S(2)}, u32[]{:S(2)}) %collective-permute-start.94) | collective-permute-done | bytes 262176 | tf_op jit(solution)/shard_map/ppermute | solution.py:134
  746.5 20.9 %collective-permute-done.92 = bf16[32,4096]{1,0:T(8,128)(2,1)S(1)} collective-permute-done((bf16[32,4096]{1,0:T(8,128)(2,1)S(1)}, bf16[32,4096]{1,0:T(8,128)(2,1)S(1)}, u32[]{:S(2)}, u32[]{:S(2)}) %collective-permute-start.92) | collective-permute-done | bytes 262176 | tf_op jit(solution)/shard_map/ppermute | solution.py:134
  (299 shorter events, 198.2 us)
Async XLA Ops:
  3.9 39.8 %collective-permute-start.23 = (bf16[1,4096]{1,0:T(2,128)(2,1)}, bf16[1,4096]{1,0:T(2,128)(2,1)S(1)}, u32[]{:S(2)}, u32[]{:S(2)}) collective-permute-start(bf16[1,4096]{1,0:T(2,128)(2,1)} %param.31), channel_id=1, source_target_pairs={{0,16},{16,0},{1,17},{17,1},{2,18},{18,2},{3,19},{19,3},{4,20},{20... | collective-permute-start | bytes 24584 | tf_op jit(solution)/shard_map/ppermute | solution.py:216
  5.4 39.6 %collective-permute-start.11 = (bf16[1,4096]{1,0:T(2,128)(2,1)}, bf16[1,4096]{1,0:T(2,128)(2,1)S(1)}, u32[]{:S(2)}, u32[]{:S(2)}) collective-permute-start(bf16[1,4096]{1,0:T(2,128)(2,1)} %param.26), channel_id=1, source_target_pairs={{0,16},{16,0},{1,17},{17,1},{2,18},{18,2},{3,19},{19,3},{4,20},{20... | collective-permute-start | bytes 24584 | tf_op jit(solution)/shard_map/ppermute | solution.py:216
  131.0 55.2 %collective-permute-start.10 = (bf16[32,4096]{1,0:T(8,128)(2,1)S(1)}, bf16[32,4096]{1,0:T(8,128)(2,1)S(1)}, u32[]{:S(2)}, u32[]{:S(2)}) collective-permute-start(bf16[32,4096]{1,0:T(8,128)(2,1)S(1)} %constant_dynamic-slice_fusion.9), channel_id=1, source_target_pairs={{0,16},{1,17},{2,18},{3,19},{4,20},{5,21},{6,22},{7,23},{8,24},{9,... | collective-permute-start | bytes 786440 | tf_op jit(solution)/shard_map/ppermute | solution.py:134
  183.1 39.9 %collective-permute-start.31 = (bf16[128,4096]{1,0:T(8,128)(2,1)}, bf16[128,4096]{1,0:T(8,128)(2,1)S(1)}, u32[]{:S(2)}, u32[]{:S(2)}) collective-permute-start(bf16[128,4096]{1,0:T(8,128)(2,1)} %get-tuple-element.130), channel_id=1, source_target_pairs={{0,1},{1,0},{2,3},{3,2},{4,5},{5,4},{6,7},{7,6},{8,9},{9,8},{10,11... | collective-permute-start | bytes 3145736 | tf_op jit(solution)/shard_map/ppermute | solution.py:134
  190.8 33.8 %collective-permute-start.26 = (bf16[32,4096]{1,0:T(8,128)(2,1)S(1)}, bf16[32,4096]{1,0:T(8,128)(2,1)S(1)}, u32[]{:S(2)}, u32[]{:S(2)}) collective-permute-start(bf16[32,4096]{1,0:T(8,128)(2,1)S(1)} %fusion.8.refs_4_), channel_id=1, source_target_pairs={{0,3},{1,2},{2,1},{3,0},{4,7},{5,6},{6,5},{7,4},{8,11},{9,10},{10,... | collective-permute-start | bytes 786440 | tf_op jit(solution)/shard_map/ppermute | solution.py:134
  195.4 33.3 %collective-permute-start.27 = (bf16[32,4096]{1,0:T(8,128)(2,1)S(1)}, bf16[32,4096]{1,0:T(8,128)(2,1)S(1)}, u32[]{:S(2)}, u32[]{:S(2)}) collective-permute-start(bf16[32,4096]{1,0:T(8,128)(2,1)S(1)} %fusion.8.refs_4_), channel_id=1, source_target_pairs={{16,3},{17,2},{18,1},{19,0},{20,7},{21,6},{22,5},{23,4},{24,11},{2... | collective-permute-start | bytes 786440 | tf_op jit(solution)/shard_map/ppermute | solution.py:134
  224.6 48.6 %collective-permute-start.36 = (bf16[32,4096]{1,0:T(8,128)(2,1)S(1)}, bf16[32,4096]{1,0:T(8,128)(2,1)S(1)}, u32[]{:S(2)}, u32[]{:S(2)}) collective-permute-start(bf16[32,4096]{1,0:T(8,128)(2,1)S(1)} %constant_dynamic-slice_fusion), channel_id=1, source_target_pairs={{0,16},{1,17},{2,18},{3,19},{4,20},{5,21},{6,22},{7,23},{8,24},{9,... | collective-permute-start | bytes 786440 | tf_op jit(solution)/shard_map/ppermute | solution.py:134
  228.7 44.5 %collective-permute-start.37 = (bf16[32,4096]{1,0:T(8,128)(2,1)S(1)}, bf16[32,4096]{1,0:T(8,128)(2,1)S(1)}, u32[]{:S(2)}, u32[]{:S(2)}) collective-permute-start(bf16[32,4096]{1,0:T(8,128)(2,1)S(1)} %get-tuple-element.275), channel_id=1, source_target_pairs={{0,2},{1,3},{2,0},{3,1},{4,6},{5,7},{6,4},{7,5},{8,10},{9,11},{10,... | collective-permute-start | bytes 786440 | tf_op jit(solution)/shard_map/ppermute | solution.py:134
  233.5 39.7 %collective-permute-start.38 = (bf16[32,4096]{1,0:T(8,128)(2,1)S(1)}, bf16[32,4096]{1,0:T(8,128)(2,1)S(1)}, u32[]{:S(2)}, u32[]{:S(2)}) collective-permute-start(bf16[32,4096]{1,0:T(8,128)(2,1)S(1)} %get-tuple-element.274), channel_id=1, source_target_pairs={{0,18},{1,19},{2,16},{3,17},{4,22},{5,23},{6,20},{7,21},{8,26},{9,... | collective-permute-start | bytes 786440 | tf_op jit(solution)/shard_map/ppermute | solution.py:134
  271.3 41.5 %collective-permute-start.32 = (bf16[128,4096]{1,0:T(8,128)(2,1)}, bf16[128,4096]{1,0:T(8,128)(2,1)S(1)}, u32[]{:S(2)}, u32[]{:S(2)}) collective-permute-start(bf16[128,4096]{1,0:T(8,128)(2,1)} %get-tuple-element.142), channel_id=1, source_target_pairs={{0,1},{1,0},{2,3},{3,2},{4,5},{5,4},{6,7},{7,6},{8,9},{9,8},{10,11... | collective-permute-start | bytes 3145736 | tf_op jit(solution)/shard_map/ppermute | solution.py:134
  273.7 35.8 %collective-permute-start.40 = (bf16[32,4096]{1,0:T(8,128)(2,1)S(1)}, bf16[32,4096]{1,0:T(8,128)(2,1)S(1)}, u32[]{:S(2)}, u32[]{:S(2)}) collective-permute-start(bf16[32,4096]{1,0:T(8,128)(2,1)S(1)} %fusion.12.refs_4_), channel_id=1, source_target_pairs={{0,1},{1,0},{2,3},{3,2},{4,5},{5,4},{6,7},{7,6},{8,9},{9,8},{10,11... | collective-permute-start | bytes 786440 | tf_op jit(solution)/shard_map/ppermute | solution.py:134
  277.7 33.2 %collective-permute-start.41 = (bf16[32,4096]{1,0:T(8,128)(2,1)S(1)}, bf16[32,4096]{1,0:T(8,128)(2,1)S(1)}, u32[]{:S(2)}, u32[]{:S(2)}) collective-permute-start(bf16[32,4096]{1,0:T(8,128)(2,1)S(1)} %fusion.12.refs_4_), channel_id=1, source_target_pairs={{16,1},{17,0},{18,3},{19,2},{20,5},{21,4},{22,7},{23,6},{24,9},{25... | collective-permute-start | bytes 786440 | tf_op jit(solution)/shard_map/ppermute | solution.py:134
  279.0 35.4 %collective-permute-start.42 = (bf16[32,4096]{1,0:T(8,128)(2,1)S(1)}, bf16[32,4096]{1,0:T(8,128)(2,1)S(1)}, u32[]{:S(2)}, u32[]{:S(2)}) collective-permute-start(bf16[32,4096]{1,0:T(8,128)(2,1)S(1)} %fusion.12.refs_4_), channel_id=1, source_target_pairs={{0,3},{1,2},{2,1},{3,0},{4,7},{5,6},{6,5},{7,4},{8,11},{9,10},{10,... | collective-permute-start | bytes 786440 | tf_op jit(solution)/shard_map/ppermute | solution.py:134
  282.7 36.5 %collective-permute-start.43 = (bf16[32,4096]{1,0:T(8,128)(2,1)S(1)}, bf16[32,4096]{1,0:T(8,128)(2,1)S(1)}, u32[]{:S(2)}, u32[]{:S(2)}) collective-permute-start(bf16[32,4096]{1,0:T(8,128)(2,1)S(1)} %fusion.12.refs_4_), channel_id=1, source_target_pairs={{16,3},{17,2},{18,1},{19,0},{20,7},{21,6},{22,5},{23,4},{24,11},{2... | collective-permute-start | bytes 786440 | tf_op jit(solution)/shard_map/ppermute | solution.py:134
  314.4 45.7 %collective-permute-start.33 = (bf16[32,4096]{1,0:T(8,128)(2,1)S(1)}, bf16[32,4096]{1,0:T(8,128)(2,1)S(1)}, u32[]{:S(2)}, u32[]{:S(2)}) collective-permute-start(bf16[32,4096]{1,0:T(8,128)(2,1)S(1)} %get-tuple-element.273), channel_id=1, source_target_pairs={{0,2},{1,3},{2,0},{3,1},{4,6},{5,7},{6,4},{7,5},{8,10},{9,11},{10,... | collective-permute-start | bytes 786440 | tf_op jit(solution)/shard_map/ppermute | solution.py:134
  319.2 40.9 %collective-permute-start.34 = (bf16[32,4096]{1,0:T(8,128)(2,1)S(1)}, bf16[32,4096]{1,0:T(8,128)(2,1)S(1)}, u32[]{:S(2)}, u32[]{:S(2)}) collective-permute-start(bf16[32,4096]{1,0:T(8,128)(2,1)S(1)} %get-tuple-element.272), channel_id=1, source_target_pairs={{0,18},{1,19},{2,16},{3,17},{4,22},{5,23},{6,20},{7,21},{8,26},{9,... | collective-permute-start | bytes 786440 | tf_op jit(solution)/shard_map/ppermute | solution.py:134
  321.5 38.7 %collective-permute-start.35 = (bf16[32,4096]{1,0:T(8,128)(2,1)S(1)}, bf16[32,4096]{1,0:T(8,128)(2,1)S(1)}, u32[]{:S(2)}, u32[]{:S(2)}) collective-permute-start(bf16[32,4096]{1,0:T(8,128)(2,1)S(1)} %get-tuple-element.271), channel_id=1, source_target_pairs={{0,16},{1,17},{2,18},{3,19},{4,20},{5,21},{6,22},{7,23},{8,24},{9,... | collective-permute-start | bytes 786440 | tf_op jit(solution)/shard_map/ppermute | solution.py:134
  358.2 41.2 %collective-permute-start.54 = (bf16[128,4096]{1,0:T(8,128)(2,1)}, bf16[128,4096]{1,0:T(8,128)(2,1)S(1)}, u32[]{:S(2)}, u32[]{:S(2)}) collective-permute-start(bf16[128,4096]{1,0:T(8,128)(2,1)} %get-tuple-element.162), channel_id=1, source_target_pairs={{0,1},{1,0},{2,3},{3,2},{4,5},{5,4},{6,7},{7,6},{8,9},{9,8},{10,11... | collective-permute-start | bytes 3145736 | tf_op jit(solution)/shard_map/ppermute | solution.py:134
  361.9 36.2 %collective-permute-start.48 = (bf16[32,4096]{1,0:T(8,128)(2,1)S(1)}, bf16[32,4096]{1,0:T(8,128)(2,1)S(1)}, u32[]{:S(2)}, u32[]{:S(2)}) collective-permute-start(bf16[32,4096]{1,0:T(8,128)(2,1)S(1)} %fusion.16.refs_5_), channel_id=1, source_target_pairs={{16,17},{17,16},{18,19},{19,18},{20,21},{21,20},{22,23},{23,22},{2... | collective-permute-start | bytes 786440 | tf_op jit(solution)/shard_map/ppermute | solution.py:134
  362.6 37.8 %collective-permute-start.49 = (bf16[32,4096]{1,0:T(8,128)(2,1)S(1)}, bf16[32,4096]{1,0:T(8,128)(2,1)S(1)}, u32[]{:S(2)}, u32[]{:S(2)}) collective-permute-start(bf16[32,4096]{1,0:T(8,128)(2,1)S(1)} %fusion.16.refs_5_), channel_id=1, source_target_pairs={{0,19},{1,18},{2,17},{3,16},{4,23},{5,22},{6,21},{7,20},{8,27},{9,... | collective-permute-start | bytes 786440 | tf_op jit(solution)/shard_map/ppermute | solution.py:134
  363.9 40.7 %collective-permute-start.50 = (bf16[32,4096]{1,0:T(8,128)(2,1)S(1)}, bf16[32,4096]{1,0:T(8,128)(2,1)S(1)}, u32[]{:S(2)}, u32[]{:S(2)}) collective-permute-start(bf16[32,4096]{1,0:T(8,128)(2,1)S(1)} %fusion.16.refs_5_), channel_id=1, source_target_pairs={{16,19},{17,18},{18,17},{19,16},{20,23},{21,22},{22,21},{23,20},{2... | collective-permute-start | bytes 786440 | tf_op jit(solution)/shard_map/ppermute | solution.py:134
  429.5 47.9 %collective-permute-start.55 = (bf16[128,4096]{1,0:T(8,128)(2,1)}, bf16[128,4096]{1,0:T(8,128)(2,1)S(1)}, u32[]{:S(2)}, u32[]{:S(2)}) collective-permute-start(bf16[128,4096]{1,0:T(8,128)(2,1)} %get-tuple-element.174), channel_id=1, source_target_pairs={{16,17},{17,16},{18,19},{19,18},{20,21},{21,20},{22,23},{23,22},{2... | collective-permute-start | bytes 3145736 | tf_op jit(solution)/shard_map/ppermute | solution.py:134
  446.8 31.6 %collective-permute-start.64 = (bf16[32,4096]{1,0:T(8,128)(2,1)S(1)}, bf16[32,4096]{1,0:T(8,128)(2,1)S(1)}, u32[]{:S(2)}, u32[]{:S(2)}) collective-permute-start(bf16[32,4096]{1,0:T(8,128)(2,1)S(1)} %fusion.20.refs_5_), channel_id=1, source_target_pairs={{0,19},{1,18},{2,17},{3,16},{4,23},{5,22},{6,21},{7,20},{8,27},{9,... | collective-permute-start | bytes 786440 | tf_op jit(solution)/shard_map/ppermute | solution.py:134
  504.2 55.1 %collective-permute-start.76 = (bf16[128,4096]{1,0:T(8,128)(2,1)}, bf16[128,4096]{1,0:T(8,128)(2,1)S(1)}, u32[]{:S(2)}, u32[]{:S(2)}) collective-permute-start(bf16[128,4096]{1,0:T(8,128)(2,1)} %get-tuple-element.194), channel_id=1, source_target_pairs={{16,17},{17,16},{18,19},{19,18},{20,21},{21,20},{22,23},{23,22},{2... | collective-permute-start | bytes 3145736 | tf_op jit(solution)/shard_map/ppermute | solution.py:134
  529.5 30.7 %collective-permute-start.71 = (bf16[32,4096]{1,0:T(8,128)(2,1)S(1)}, bf16[32,4096]{1,0:T(8,128)(2,1)S(1)}, u32[]{:S(2)}, u32[]{:S(2)}) collective-permute-start(bf16[32,4096]{1,0:T(8,128)(2,1)S(1)} %fusion.24.refs_5_), channel_id=1, source_target_pairs={{0,19},{1,18},{2,17},{3,16},{4,23},{5,22},{6,21},{7,20},{8,27},{9,... | collective-permute-start | bytes 786440 | tf_op jit(solution)/shard_map/ppermute | solution.py:134
  615.4 30.8 %collective-permute-start.85 = (bf16[32,4096]{1,0:T(8,128)(2,1)S(1)}, bf16[32,4096]{1,0:T(8,128)(2,1)S(1)}, u32[]{:S(2)}, u32[]{:S(2)}) collective-permute-start(bf16[32,4096]{1,0:T(8,128)(2,1)S(1)} %fusion.28.refs_5_), channel_id=1, source_target_pairs={{16,17},{17,16},{18,19},{19,18},{20,21},{21,20},{22,23},{23,22},{2... | collective-permute-start | bytes 786440 | tf_op jit(solution)/shard_map/ppermute | solution.py:134
  617.6 32.4 %collective-permute-start.79 = (bf16[32,4096]{1,0:T(8,128)(2,1)S(1)}, bf16[32,4096]{1,0:T(8,128)(2,1)S(1)}, u32[]{:S(2)}, u32[]{:S(2)}) collective-permute-start(bf16[32,4096]{1,0:T(8,128)(2,1)S(1)} %get-tuple-element.257), channel_id=1, source_target_pairs={{16,18},{17,19},{18,16},{19,17},{20,22},{21,23},{22,20},{23,21},{2... | collective-permute-start | bytes 786440 | tf_op jit(solution)/shard_map/ppermute | solution.py:134
  618.3 52.0 %collective-permute-start.78 = (bf16[32,4096]{1,0:T(8,128)(2,1)S(1)}, bf16[32,4096]{1,0:T(8,128)(2,1)S(1)}, u32[]{:S(2)}, u32[]{:S(2)}) collective-permute-start(bf16[32,4096]{1,0:T(8,128)(2,1)S(1)} %get-tuple-element.255), channel_id=1, source_target_pairs={{16,2},{17,3},{18,0},{19,1},{20,6},{21,7},{22,4},{23,5},{24,10},{2... | collective-permute-start | bytes 786440 | tf_op jit(solution)/shard_map/ppermute | solution.py:134
  620.7 50.8 %collective-permute-start.86 = (bf16[32,4096]{1,0:T(8,128)(2,1)S(1)}, bf16[32,4096]{1,0:T(8,128)(2,1)S(1)}, u32[]{:S(2)}, u32[]{:S(2)}) collective-permute-start(bf16[32,4096]{1,0:T(8,128)(2,1)S(1)} %fusion.28.refs_5_), channel_id=1, source_target_pairs={{0,19},{1,18},{2,17},{3,16},{4,23},{5,22},{6,21},{7,20},{8,27},{9,... | collective-permute-start | bytes 786440 | tf_op jit(solution)/shard_map/ppermute | solution.py:134
  698.1 48.4 %collective-permute-start.94 = (bf16[32,4096]{1,0:T(8,128)(2,1)S(1)}, bf16[32,4096]{1,0:T(8,128)(2,1)S(1)}, u32[]{:S(2)}, u32[]{:S(2)}) collective-permute-start(bf16[32,4096]{1,0:T(8,128)(2,1)S(1)} %get-tuple-element.253), channel_id=1, source_target_pairs={{16,0},{17,1},{18,2},{19,3},{20,4},{21,5},{22,6},{23,7},{24,8},{25... | collective-permute-start | bytes 786440 | tf_op jit(solution)/shard_map/ppermute | solution.py:134
  699.4 47.1 %collective-permute-start.93 = (bf16[32,4096]{1,0:T(8,128)(2,1)S(1)}, bf16[32,4096]{1,0:T(8,128)(2,1)S(1)}, u32[]{:S(2)}, u32[]{:S(2)}) collective-permute-start(bf16[32,4096]{1,0:T(8,128)(2,1)S(1)} %get-tuple-element.254), channel_id=1, source_target_pairs={{16,18},{17,19},{18,16},{19,17},{20,22},{21,23},{22,20},{23,21},{2... | collective-permute-start | bytes 786440 | tf_op jit(solution)/shard_map/ppermute | solution.py:134
  700.1 67.3 %collective-permute-start.92 = (bf16[32,4096]{1,0:T(8,128)(2,1)S(1)}, bf16[32,4096]{1,0:T(8,128)(2,1)S(1)}, u32[]{:S(2)}, u32[]{:S(2)}) collective-permute-start(bf16[32,4096]{1,0:T(8,128)(2,1)S(1)} %get-tuple-element.252), channel_id=1, source_target_pairs={{16,2},{17,3},{18,0},{19,1},{20,6},{21,7},{22,4},{23,5},{24,10},{2... | collective-permute-start | bytes 786440 | tf_op jit(solution)/shard_map/ppermute | solution.py:134
  (78 other events, 1537.7 us)

commit v4 on v3

--- a/solution.py
+++ b/solution.py
@@ -13,6 +13,7 @@
 ROTARY_FREQ_BASE = 10000.0
 BOTH = ("section", "tensor")
 WIDE = 256
+OUT_WIDE = 1024
 VMEM_LIMIT = 50 * 2**20
 
 
@@ -43,34 +44,14 @@
         start += ref.shape[0]
 
 
-def add_part(part, total, out_refs):
-    step = pl.program_id(0)
-
-    @pl.when(step == 0)
-    def _():
-        total[...] = part
-
-    @pl.when(step > 0)
-    def _():
-        total[...] += part
-
-    @pl.when(step == pl.num_programs(0) - 1)
-    def _():
-        start = 0
-        for ref in out_refs:
-            ref[...] = total[start : start + ref.shape[0], :].astype(jnp.bfloat16)
-            start += ref.shape[0]
-
-
-def attention_kernel(count, cos_ref, sin_ref, row_ref, col_ref, wq_ref, wk_ref, wv_ref, wo_ref, *refs):
-    x_refs, out_refs, (x_all, total) = refs[:count], refs[count:-2], refs[-2:]
+def attention_kernel(count, cos_ref, sin_ref, row_ref, col_ref, wq_ref, wk_ref, wv_ref, *refs):
+    x_refs, (out_ref, x_all) = refs[:count], refs[count:]
     pl.when(pl.program_id(0) == 0)(lambda: load_rows(x_refs, x_all))
     x = x_all[...]
     cosine, sine = cos_ref[...], sin_ref[...]
     visible = row_ref[...] >= col_ref[...]
     query, key, value = dot(x, wq_ref[0]), dot(x, wk_ref[0]), dot(x, wv_ref[0])
     value = value.astype(jnp.bfloat16)
-    outs = []
     for head in range(query.shape[1] // HEAD_DIM):
         cut = slice(head * HEAD_DIM, (head + 1) * HEAD_DIM)
         q, k, v = query[:, cut], key[:, cut], value[:, cut]
@@ -82,50 +63,77 @@
         scores = jnp.where(visible, scores, -jnp.inf)
         scores = jnp.exp(scores - jnp.max(scores, axis=-1, keepdims=True))
         probs = scores / jnp.sum(scores, axis=-1, keepdims=True)
-        outs.append(dot(probs.astype(jnp.bfloat16), v).astype(jnp.bfloat16))
-    add_part(dot(jnp.concatenate(outs, axis=1), wo_ref[0]), total, out_refs)
-
-
-def mlp_kernel(count, wg_ref, wu_ref, wd_ref, *refs):
-    x_refs, out_refs, (x_all, total) = refs[:count], refs[count:-2], refs[-2:]
+        out_ref[:, cut] = dot(probs.astype(jnp.bfloat16), v).astype(jnp.bfloat16)
+
+
+def gate_kernel(count, wg_ref, wu_ref, *refs):
+    x_refs, (out_ref, x_all) = refs[:count], refs[count:]
     pl.when(pl.program_id(0) == 0)(lambda: load_rows(x_refs, x_all))
     x = x_all[...]
     gate, up = dot(x, wg_ref[0]), dot(x, wu_ref[0])
-    inner = (gate / (1.0 + jnp.exp(-gate)) * up).astype(jnp.bfloat16)
-    add_part(dot(inner, wd_ref[0]), total, out_refs)
+    out_ref[...] = (gate / (1.0 + jnp.exp(-gate)) * up).astype(jnp.bfloat16)
+
+
+def down_kernel(x_ref, w_ref, *out_refs):
+    part = dot(x_ref[...], w_ref[0]).astype(jnp.bfloat16)
+    start = 0
+    for ref in out_refs:
+        ref[...] = part[start : start + ref.shape[0], :]
+        start += ref.shape[0]
 
 
 def whole(array):
     return pl.BlockSpec(array.shape, lambda i: (0,) * array.ndim)
 
 
-def fused(kernel, name, tables, by_columns, by_rows, pieces, cuts):
+def cost(length, weights, other):
+    return pl.CostEstimate(
+        flops=2 * length * sum(w.size for w in weights),
+        bytes_accessed=2 * sum(w.size for w in weights) + other,
+        transcendentals=0,
+    )
+
+
+def params():
+    return pltpu.CompilerParams(
+        dimension_semantics=("arbitrary",), vmem_limit_bytes=VMEM_LIMIT
+    )
+
+
+def inward(kernel, name, tables, weights, pieces):
     width = pieces[0].shape[1]
     length = sum(piece.shape[0] for piece in pieces)
-    hidden = by_rows.shape[1]
+    hidden = weights[0].shape[2]
     wide = min(WIDE, hidden)
-    weights = list(by_columns) + [by_rows]
-    flops = 2 * length * sum(w.size for w in weights)
-    traffic = 2 * sum(w.size for w in weights) + 4 * length * width
     return pl.pallas_call(
         functools.partial(kernel, len(pieces)),
-        out_shape=[jax.ShapeDtypeStruct((rows, width), jnp.bfloat16) for rows in cuts],
+        out_shape=jax.ShapeDtypeStruct((length, hidden), jnp.bfloat16),
         grid=(hidden // wide,),
         in_specs=[whole(t) for t in tables]
-        + [pl.BlockSpec((1, width, wide), lambda i: (0, 0, i)) for _ in by_columns]
-        + [pl.BlockSpec((1, wide, width), lambda i: (0, i, 0))]
+        + [pl.BlockSpec((1, width, wide), lambda i: (0, 0, i)) for _ in weights]
         + [whole(p) for p in pieces],
-        out_specs=[pl.BlockSpec((rows, width), lambda i: (0, 0)) for rows in cuts],
-        scratch_shapes=[
-            pltpu.VMEM((length, width), jnp.bfloat16),
-            pltpu.VMEM((length, width), jnp.float32),
-        ],
-        compiler_params=pltpu.CompilerParams(
-            dimension_semantics=("arbitrary",), vmem_limit_bytes=VMEM_LIMIT
-        ),
-        cost_estimate=pl.CostEstimate(flops=flops, bytes_accessed=traffic, transcendentals=0),
+        out_specs=pl.BlockSpec((length, wide), lambda i: (0, i)),
+        scratch_shapes=[pltpu.VMEM((length, width), jnp.bfloat16)],
+        compiler_params=params(),
+        cost_estimate=cost(length, weights, 4 * length * width),
         name=name,
     )(*tables, *weights, *pieces)
+
+
+def outward(name, inner, weight, cuts):
+    length, hidden = inner.shape
+    width = weight.shape[2]
+    wide = min(OUT_WIDE, width)
+    return pl.pallas_call(
+        down_kernel,
+        out_shape=[jax.ShapeDtypeStruct((rows, width), jnp.bfloat16) for rows in cuts],
+        grid=(width // wide,),
+        in_specs=[whole(inner), pl.BlockSpec((1, hidden, wide), lambda i: (0, 0, i))],
+        out_specs=[pl.BlockSpec((rows, wide), lambda i: (0, i)) for rows in cuts],
+        compiler_params=params(),
+        cost_estimate=cost(length, [weight], 4 * length * width),
+        name=name,
+    )(inner, weight)
 
 
 def send(value, source, target, distance):
@@ -293,9 +301,11 @@
 
     def compute(half, pieces):
         if half % 2:
-            return fused(mlp_kernel, "mlp", (), (w_gate, w_up), w_down, pieces, cuts)
+            inner = inward(gate_kernel, "gate", (), (w_gate, w_up), pieces)
+            return outward("down", inner, w_down, cuts)
         weights = (w_query, w_key, w_value)
-        return fused(attention_kernel, "attention", tables, weights, w_out, pieces, cuts)
+        inner = inward(attention_kernel, "attention", tables, weights, pieces)
+        return outward("out", inner, w_out, cuts)
 
     def add(base, sums):
         return (base.astype(jnp.float32) + sums).astype(jnp.bfloat16)
@@ -310,16 +320,14 @@
         for c in range(per_device):
             if half == 0:
                 if c:
-                    looked[c] = after(looked[c], partial[-1])
+                    looked[c] = after(looked[c], pieces)
                 pieces, hidden[c] = embed(looked[c])
             else:
-                if c or half > 1 or per_device > 1:
-                    arrived[c] = after(arrived[c], partial[-1])
+                if c:
+                    arrived[c] = after(arrived[c], normed)
                 hidden[c] = add(hidden[c], sum_arrived(nearby[c], arrived[c], (half - 1) // 2))
-                pieces = gather_rows(rms_norm(hidden[c], gains[half]), half // 2)
-            if half or c:
-                before = (c - 1) % per_device
-                pieces = after(pieces, nearby[before])
+                normed = rms_norm(hidden[c], gains[half])
+                pieces = gather_rows(normed, half // 2)
             partial = compute(half, pieces)
             nearby[c] = sum_nearby(partial, half // 2)
             arrived[c] = send_to_owners(nearby[c], half // 2)

time: 793 us -> 683 us (0.86)
  starting transfers between devices: 328 us -> 254 us
  waiting for transfers between devices: 227 us -> 192 us
  Pallas kernels: 187 us -> 177 us
    ppermute x90, starting transfers between devices: 312 us -> 239 us  [send(): return lax.ppermute(value, BOTH, links)]
    ppermute x90, waiting for transfers between devices: 222 us -> 187 us  [send(): return lax.ppermute(value, BOTH, links)]
    pallas_call x8 -> x16, Pallas kernels: 187 us -> 177 us  [the longest x8 120 us: inward(): pl.pallas_call(functools.partial(kernel, len(pieces)), out_shape=jax.Shap...]
  transfers between devices with their start and end apart: 103 -> 103, of which waited for: 23 -> 24; matrix products, arithmetic and copies ran while one was open for 4% -> 6% of each run, Pallas kernels for 18% -> 26%
where the time goes in v4:
time: 683 us; the launch traced here: 674 us
  starting transfers between devices  254 us (37%)
  waiting for transfers between devices  192 us (28%)
  Pallas kernels  177 us (26%)
  local copies, waits for them, and re-layouts  26 us (4%)
  other arithmetic  18.5 us (3%)
    ppermute x90, starting transfers between devices, send(): return lax.ppermute(value, BOTH, links)  239 us
    ppermute x90, waiting for transfers between devices, send(): return lax.ppermute(value, BOTH, links)  187 us
    pallas_call x8, Pallas kernels, inward(): pl.pallas_call(functools.partial(kernel, len(pieces)), out_shape=jax.Shap...  120 us
    pallas_call x8, Pallas kernels, outward(): pl.pallas_call(down_kernel, out_shape=[jax.ShapeDtypeStruct((rows, width)...  56.9 us
    gather x2, local copies, waits for them, and re-layouts, body(): jnp.take(embed_table, tokens[c], axis=0)  18 us
  transfers between devices with their start and end apart: 103, of which 24 were waited for; matrix products, arithmetic and copies ran while one was open for 6% of the time, Pallas kernels for 26%

profile of v4, /device:TPU:0, one launch (start us, length us, event | category | flops | bytes accessed | tf_op | source)
XLA Modules:
  0.0 673.7 jit_solution(5920552455152660058)
XLA Ops:
  15.2 9.0 %gather_fusion.5 = bf16[256,512]{1,0:T(8,128)(2,1)S(1)} fusion(bf16[16000,512]{1,0:T(8,128)(2,1)} %param.25, s32[1024]{0:T(1024)S(1)} %pad_clamp_fusion.2), kind=kCustom, calls=%fused_computation.1.clone | custom fusion | bytes 525312 | tf_op jit(solution)/shard_map/jit(_take)/gather | solution.py:315
  35.2 9.0 %gather_fusion.6 = bf16[256,512]{1,0:T(8,128)(2,1)S(1)} fusion(bf16[16000,512]{1,0:T(8,128)(2,1)} %param.25, s32[1024]{0:T(1024)S(1)} %pad_clamp_fusion), kind=kCustom, calls=%fused_computation.3.clone | custom fusion | bytes 525312 | tf_op jit(solution)/shard_map/jit(_take)/gather | solution.py:315
  58.4 17.1 %collective-permute-done.8 = bf16[256,512]{1,0:T(8,128)(2,1)S(1)} collective-permute-done((bf16[256,512]{1,0:T(8,128)(2,1)}, bf16[256,512]{1,0:T(8,128)(2,1)S(1)}, u32[]{:S(2)}, u32[]{:S(2)}) %collective-permute-start.8) | collective-permute-done | bytes 262176 | tf_op jit(solution)/shard_map/ppermute | solution.py:142
  90.8 13.9 %attention.4.x_ref = bf16[256,1024]{1,0:T(8,128)(2,1)S(1)} custom-call(f32[256,128]{1,0:T(8,128)S(1)} %bitcast.75, f32[256,128]{1,0:T(8,128)S(1)} %bitcast.79, s32[256,1]{1,0:T(8,128)S(1)} %add.571.row_ref, s32[1,256]{1,0:T(1,128)S(1)} %add.468.col_ref, bf16[1,4096,1024]{2,1,0:T(8,128)(2,1)} %wq_ref.7, bf16[1,4096,1024]{2,1,0:T(8,128)(2,1)} %wk_ref.7, ...), custom_call_target="tpu_custom_call" | custom-call | flops 6442450944 | bytes 29360128 | tf_op jit(solution)/shard_map/attention/pallas_call | solution.py:108
  129.4 13.9 %attention.6.x_ref = bf16[256,1024]{1,0:T(8,128)(2,1)S(1)} custom-call(f32[256,128]{1,0:T(8,128)S(1)} %bitcast.76, f32[256,128]{1,0:T(8,128)S(1)} %bitcast.80, s32[256,1]{1,0:T(8,128)S(1)} %add.571.row_ref, s32[1,256]{1,0:T(1,128)S(1)} %add.468.col_ref, bf16[1,4096,1024]{2,1,0:T(8,128)(2,1)} %wq_ref.7, bf16[1,4096,1024]{2,1,0:T(8,128)(2,1)} %wk_ref.7, ...), custom_call_target="tpu_custom_call" | custom-call | flops 6442450944 | bytes 29360128 | tf_op jit(solution)/shard_map/attention/pallas_call | solution.py:108
  159.0 7.1 %collective-permute-done.15 = bf16[32,4096]{1,0:T(8,128)(2,1)S(1)} collective-permute-done((bf16[32,4096]{1,0:T(8,128)(2,1)S(1)}, bf16[32,4096]{1,0:T(8,128)(2,1)S(1)}, u32[]{:S(2)}, u32[]{:S(2)}) %collective-permute-start.15) | collective-permute-done | bytes 262176 | tf_op jit(solution)/shard_map/ppermute | solution.py:142
  166.2 15.3 %collective-permute-done.14 = bf16[32,4096]{1,0:T(8,128)(2,1)S(1)} collective-permute-done((bf16[32,4096]{1,0:T(8,128)(2,1)S(1)}, bf16[32,4096]{1,0:T(8,128)(2,1)S(1)}, u32[]{:S(2)}, u32[]{:S(2)}) %collective-permute-start.14) | collective-permute-done | bytes 262176 | tf_op jit(solution)/shard_map/ppermute | solution.py:142
  196.8 13.0 %collective-permute-done.59 = bf16[32,4096]{1,0:T(8,128)(2,1)S(1)} collective-permute-done((bf16[32,4096]{1,0:T(8,128)(2,1)S(1)}, bf16[32,4096]{1,0:T(8,128)(2,1)S(1)}, u32[]{:S(2)}, u32[]{:S(2)}) %collective-permute-start.59) | collective-permute-done | bytes 262176 | tf_op jit(solution)/shard_map/ppermute | solution.py:142
  223.5 11.7 %collective-permute-start.62 = (bf16[32,4096]{1,0:T(8,128)(2,1)S(1)}, bf16[32,4096]{1,0:T(8,128)(2,1)S(1)}, u32[]{:S(2)}, u32[]{:S(2)}) collective-permute-start(bf16[32,4096]{1,0:T(8,128)(2,1)S(1)} %fusion.20.refs_4_), channel_id=1, source_target_pairs={{0,1},{1,0},{2,3},{3,2},{4,5},{5,4},{6,7},{7,6},{8,9},{9,8},{10,11... | collective-permute-start | bytes 786440 | tf_op jit(solution)/shard_map/ppermute | solution.py:142
  242.9 16.1 %gate.4.x_ref = bf16[256,2048]{1,0:T(8,128)(2,1)S(1)} custom-call(bf16[1,4096,2048]{2,1,0:T(8,128)(2,1)} %wg_ref.7, bf16[1,4096,2048]{2,1,0:T(8,128)(2,1)} %wu_ref.7, bf16[32,4096]{1,0:T(8,128)(2,1)S(1)} %collective-permute-done.17.refs_0_, bf16[32,4096]{1,0:T(8,128)(2,1)S(1)} %collective-permute-done.18.refs_1_, ...), custom_call_target="tpu_custom_call" | custom-call | flops 8589934592 | bytes 37748736 | tf_op jit(solution)/shard_map/gate/pallas_call | solution.py:108
  264.0 8.5 %down.4 = (bf16[128,4096]{1,0:T(8,128)(2,1)S(1)}, bf16[32,4096]{1,0:T(8,128)(2,1)S(1)}, bf16[32,4096]{1,0:T(8,128)(2,1)S(1)}, bf16[32,4096]{1,0:T(8,128)(2,1)S(1)}, bf16[32,4096]{1,0:T(8,128)(2,1)S(1)}) custom-call(bf16[256,2048]{1,0:T(8,128)(2,1)S(1)} %gate.4.x_ref, bf16[1,2048,4096]{2,1,0:T(8,128)(2,1)} %w_ref.15), custom_call_target="tpu_custom_call" | custom-call | flops 4294967296 | bytes 20971520 | tf_op jit(solution)/shard_map/down/pallas_call | solution.py:127
  278.6 16.0 %gate.6.x_ref = bf16[256,2048]{1,0:T(8,128)(2,1)S(1)} custom-call(bf16[1,4096,2048]{2,1,0:T(8,128)(2,1)} %wg_ref.7, bf16[1,4096,2048]{2,1,0:T(8,128)(2,1)} %wu_ref.7, bf16[32,4096]{1,0:T(8,128)(2,1)S(1)} %collective-permute-done.62.refs_0_, bf16[32,4096]{1,0:T(8,128)(2,1)S(1)} %collective-permute-done.63.refs_1_, ...), custom_call_target="tpu_custom_call" | custom-call | flops 8589934592 | bytes 37748736 | tf_op jit(solution)/shard_map/gate/pallas_call | solution.py:108
  294.6 8.5 %down.6 = (bf16[128,4096]{1,0:T(8,128)(2,1)S(1)}, bf16[32,4096]{1,0:T(8,128)(2,1)S(1)}, bf16[32,4096]{1,0:T(8,128)(2,1)S(1)}, bf16[32,4096]{1,0:T(8,128)(2,1)S(1)}, bf16[32,4096]{1,0:T(8,128)(2,1)S(1)}) custom-call(bf16[256,2048]{1,0:T(8,128)(2,1)S(1)} %gate.6.x_ref, bf16[1,2048,4096]{2,1,0:T(8,128)(2,1)} %w_ref.15), custom_call_target="tpu_custom_call" | custom-call | flops 4294967296 | bytes 20971520 | tf_op jit(solution)/shard_map/down/pallas_call | solution.py:127
  312.7 26.9 %collective-permute-done.69 = bf16[128,4096]{1,0:T(8,128)(2,1)S(1)} collective-permute-done((bf16[128,4096]{1,0:T(8,128)(2,1)S(1)}, bf16[128,4096]{1,0:T(8,128)(2,1)S(1)}, u32[]{:S(2)}, u32[]{:S(2)}) %collective-permute-start.69) | collective-permute-done | bytes 1048608 | tf_op jit(solution)/shard_map/ppermute | solution.py:142
  349.5 13.2 %collective-permute-done.70 = bf16[32,4096]{1,0:T(8,128)(2,1)S(1)} collective-permute-done((bf16[32,4096]{1,0:T(8,128)(2,1)S(1)}, bf16[32,4096]{1,0:T(8,128)(2,1)S(1)}, u32[]{:S(2)}, u32[]{:S(2)}) %collective-permute-start.70) | collective-permute-done | bytes 262176 | tf_op jit(solution)/shard_map/ppermute | solution.py:142
  364.7 16.1 %collective-permute-start.32 = (bf16[32,4096]{1,0:T(8,128)(2,1)S(1)}, bf16[32,4096]{1,0:T(8,128)(2,1)S(1)}, u32[]{:S(2)}, u32[]{:S(2)}) collective-permute-start(bf16[32,4096]{1,0:T(8,128)(2,1)S(1)} %fusion.12.refs_5_), channel_id=1, source_target_pairs={{0,16},{1,17},{2,18},{3,19},{4,20},{5,21},{6,22},{7,23},{8,24},{9,... | collective-permute-start | bytes 786440 | tf_op jit(solution)/shard_map/ppermute | solution.py:142
  388.8 16.0 %collective-permute-start.75 = (bf16[32,4096]{1,0:T(8,128)(2,1)S(1)}, bf16[32,4096]{1,0:T(8,128)(2,1)S(1)}, u32[]{:S(2)}, u32[]{:S(2)}) collective-permute-start(bf16[32,4096]{1,0:T(8,128)(2,1)S(1)} %fusion.24.refs_5_), channel_id=1, source_target_pairs={{0,19},{1,18},{2,17},{3,16},{4,23},{5,22},{6,21},{7,20},{8,27},{9,... | collective-permute-start | bytes 786440 | tf_op jit(solution)/shard_map/ppermute | solution.py:142
  408.6 13.9 %attention.5.x_ref = bf16[256,1024]{1,0:T(8,128)(2,1)S(1)} custom-call(f32[256,128]{1,0:T(8,128)S(1)} %bitcast.77, f32[256,128]{1,0:T(8,128)S(1)} %bitcast.81, s32[256,1]{1,0:T(8,128)S(1)} %add.571.row_ref, s32[1,256]{1,0:T(1,128)S(1)} %add.468.col_ref, bf16[1,4096,1024]{2,1,0:T(8,128)(2,1)} %wq_ref.7, bf16[1,4096,1024]{2,1,0:T(8,128)(2,1)} %wk_ref.7, ...), custom_call_target="tpu_custom_call" | custom-call | flops 6442450944 | bytes 29360128 | tf_op jit(solution)/shard_map/attention/pallas_call | solution.py:108
  424.6 6.3 out.5
  433.2 13.9 %attention.7.x_ref = bf16[256,1024]{1,0:T(8,128)(2,1)S(1)} custom-call(f32[256,128]{1,0:T(8,128)S(1)} %bitcast.78, f32[256,128]{1,0:T(8,128)S(1)} %bitcast.82, s32[256,1]{1,0:T(8,128)S(1)} %add.571.row_ref, s32[1,256]{1,0:T(1,128)S(1)} %add.468.col_ref, bf16[1,4096,1024]{2,1,0:T(8,128)(2,1)} %wq_ref.7, bf16[1,4096,1024]{2,1,0:T(8,128)(2,1)} %wk_ref.7, ...), custom_call_target="tpu_custom_call" | custom-call | flops 6442450944 | bytes 29360128 | tf_op jit(solution)/shard_map/attention/pallas_call | solution.py:108
  460.3 6.8 %collective-permute-done.38 = bf16[32,4096]{1,0:T(8,128)(2,1)S(1)} collective-permute-done((bf16[32,4096]{1,0:T(8,128)(2,1)}, bf16[32,4096]{1,0:T(8,128)(2,1)S(1)}, u32[]{:S(2)}, u32[]{:S(2)}) %collective-permute-start.38) | collective-permute-done | bytes 262176 | tf_op jit(solution)/shard_map/ppermute | solution.py:142
  467.1 10.5 %collective-permute-done.36 = bf16[32,4096]{1,0:T(8,128)(2,1)S(1)} collective-permute-done((bf16[32,4096]{1,0:T(8,128)(2,1)}, bf16[32,4096]{1,0:T(8,128)(2,1)S(1)}, u32[]{:S(2)}, u32[]{:S(2)}) %collective-permute-start.36) | collective-permute-done | bytes 262176 | tf_op jit(solution)/shard_map/ppermute | solution.py:142
  483.8 16.3 %collective-permute-start.39 = (bf16[32,4096]{1,0:T(8,128)(2,1)S(1)}, bf16[32,4096]{1,0:T(8,128)(2,1)S(1)}, u32[]{:S(2)}, u32[]{:S(2)}) collective-permute-start(bf16[32,4096]{1,0:T(8,128)(2,1)S(1)} %fusion.16.refs_5_), channel_id=1, source_target_pairs={{0,17},{1,16},{2,19},{3,18},{4,21},{5,20},{6,23},{7,22},{8,25},{9,... | collective-permute-start | bytes 786440 | tf_op jit(solution)/shard_map/ppermute | solution.py:142
  507.3 8.6 %collective-permute-start.43 = (bf16[32,4096]{1,0:T(8,128)(2,1)S(1)}, bf16[32,4096]{1,0:T(8,128)(2,1)S(1)}, u32[]{:S(2)}, u32[]{:S(2)}) collective-permute-start(bf16[32,4096]{1,0:T(8,128)(2,1)S(1)} %fusion.16.refs_5_), channel_id=1, source_target_pairs={{0,16},{1,17},{2,18},{3,19},{4,20},{5,21},{6,22},{7,23},{8,24},{9,... | collective-permute-start | bytes 786440 | tf_op jit(solution)/shard_map/ppermute | solution.py:142
  523.1 12.2 %collective-permute-start.86 = (bf16[32,4096]{1,0:T(8,128)(2,1)S(1)}, bf16[32,4096]{1,0:T(8,128)(2,1)S(1)}, u32[]{:S(2)}, u32[]{:S(2)}) collective-permute-start(bf16[32,4096]{1,0:T(8,128)(2,1)S(1)} %fusion.28.refs_5_), channel_id=1, source_target_pairs={{0,19},{1,18},{2,17},{3,16},{4,23},{5,22},{6,21},{7,20},{8,27},{9,... | collective-permute-start | bytes 786440 | tf_op jit(solution)/shard_map/ppermute | solution.py:142
  540.7 16.1 %gate.5.x_ref = bf16[256,2048]{1,0:T(8,128)(2,1)S(1)} custom-call(bf16[1,4096,2048]{2,1,0:T(8,128)(2,1)} %wg_ref.7, bf16[1,4096,2048]{2,1,0:T(8,128)(2,1)} %wu_ref.7, bf16[32,4096]{1,0:T(8,128)(2,1)S(1)} %collective-permute-done.39.refs_0_, bf16[32,4096]{1,0:T(8,128)(2,1)S(1)} %collective-permute-done.40.refs_1_, ...), custom_call_target="tpu_custom_call" | custom-call | flops 8589934592 | bytes 37748736 | tf_op jit(solution)/shard_map/gate/pallas_call | solution.py:108
  558.8 8.5 %down.5 = (bf16[128,4096]{1,0:T(8,128)(2,1)S(1)}, bf16[32,4096]{1,0:T(8,128)(2,1)S(1)}, bf16[32,4096]{1,0:T(8,128)(2,1)S(1)}, bf16[32,4096]{1,0:T(8,128)(2,1)S(1)}, bf16[32,4096]{1,0:T(8,128)(2,1)S(1)}) custom-call(bf16[256,2048]{1,0:T(8,128)(2,1)S(1)} %gate.5.x_ref, bf16[1,2048,4096]{2,1,0:T(8,128)(2,1)} %w_ref.15), custom_call_target="tpu_custom_call" | custom-call | flops 4294967296 | bytes 20971520 | tf_op jit(solution)/shard_map/down/pallas_call | solution.py:127
  568.1 16.1 %gate.7.x_ref = bf16[256,2048]{1,0:T(8,128)(2,1)S(1)} custom-call(bf16[1,4096,2048]{2,1,0:T(8,128)(2,1)} %wg_ref.7, bf16[1,4096,2048]{2,1,0:T(8,128)(2,1)} %wu_ref.7, bf16[32,4096]{1,0:T(8,128)(2,1)S(1)} %collective-permute-done.84.refs_0_, bf16[32,4096]{1,0:T(8,128)(2,1)S(1)} %collective-permute-done.85.refs_1_, ...), custom_call_target="tpu_custom_call" | custom-call | flops 8589934592 | bytes 37748736 | tf_op jit(solution)/shard_map/gate/pallas_call | solution.py:108
  584.1 8.5 %down.7 = (bf16[128,4096]{1,0:T(8,128)(2,1)S(1)}, bf16[32,4096]{1,0:T(8,128)(2,1)S(1)}, bf16[32,4096]{1,0:T(8,128)(2,1)S(1)}, bf16[32,4096]{1,0:T(8,128)(2,1)S(1)}, bf16[32,4096]{1,0:T(8,128)(2,1)S(1)}) custom-call(bf16[256,2048]{1,0:T(8,128)(2,1)S(1)} %gate.7.x_ref, bf16[1,2048,4096]{2,1,0:T(8,128)(2,1)} %w_ref.15), custom_call_target="tpu_custom_call" | custom-call | flops 4294967296 | bytes 20971520 | tf_op jit(solution)/shard_map/down/pallas_call | solution.py:127
  599.2 8.3 %collective-permute-done.49 = bf16[32,4096]{1,0:T(8,128)(2,1)S(1)} collective-permute-done((bf16[32,4096]{1,0:T(8,128)(2,1)S(1)}, bf16[32,4096]{1,0:T(8,128)(2,1)S(1)}, u32[]{:S(2)}, u32[]{:S(2)}) %collective-permute-start.49) | collective-permute-done | bytes 262176 | tf_op jit(solution)/shard_map/ppermute | solution.py:142
  612.8 23.6 %collective-permute-done.94 = bf16[32,4096]{1,0:T(8,128)(2,1)S(1)} collective-permute-done((bf16[32,4096]{1,0:T(8,128)(2,1)S(1)}, bf16[32,4096]{1,0:T(8,128)(2,1)S(1)}, u32[]{:S(2)}, u32[]{:S(2)}) %collective-permute-start.94) | collective-permute-done | bytes 262176 | tf_op jit(solution)/shard_map/ppermute | solution.py:142
  636.4 18.0 %collective-permute-done.92 = bf16[32,4096]{1,0:T(8,128)(2,1)S(1)} collective-permute-done((bf16[32,4096]{1,0:T(8,128)(2,1)S(1)}, bf16[32,4096]{1,0:T(8,128)(2,1)S(1)}, u32[]{:S(2)}, u32[]{:S(2)}) %collective-permute-start.92) | collective-permute-done | bytes 262176 | tf_op jit(solution)/shard_map/ppermute | solution.py:142
  (321 shorter events, 249.1 us)
Async XLA Ops:
  3.9 40.4 %collective-permute-start.16 = (bf16[1,4096]{1,0:T(2,128)(2,1)}, bf16[1,4096]{1,0:T(2,128)(2,1)S(1)}, u32[]{:S(2)}, u32[]{:S(2)}) collective-permute-start(bf16[1,4096]{1,0:T(2,128)(2,1)} %param.31), channel_id=1, source_target_pairs={{0,16},{16,0},{1,17},{17,1},{2,18},{18,2},{3,19},{19,3},{4,20},{20... | collective-permute-start | bytes 24584 | tf_op jit(solution)/shard_map/ppermute | solution.py:224
  5.4 40.2 %collective-permute-start.11 = (bf16[1,4096]{1,0:T(2,128)(2,1)}, bf16[1,4096]{1,0:T(2,128)(2,1)S(1)}, u32[]{:S(2)}, u32[]{:S(2)}) collective-permute-start(bf16[1,4096]{1,0:T(2,128)(2,1)} %param.26), channel_id=1, source_target_pairs={{0,16},{16,0},{1,17},{17,1},{2,18},{18,2},{3,19},{19,3},{4,20},{20... | collective-permute-start | bytes 24584 | tf_op jit(solution)/shard_map/ppermute | solution.py:224
  77.2 33.2 %collective-permute-start.52 = (bf16[256,512]{1,0:T(8,128)(2,1)S(1)}, bf16[256,512]{1,0:T(8,128)(2,1)S(1)}, u32[]{:S(2)}, u32[]{:S(2)}) collective-permute-start(bf16[256,512]{1,0:T(8,128)(2,1)S(1)} %broadcast_select_fusion), channel_id=1, source_target_pairs={{0,3},{1,2},{2,1},{3,0},{4,7},{5,6},{6,5},{7,4},{8,11},{9,10},{10,... | collective-permute-start | bytes 786440 | tf_op jit(solution)/shard_map/ppermute | solution.py:142
  89.3 32.4 %collective-permute-start.55 = (bf16[256,512]{1,0:T(8,128)(2,1)S(1)}, bf16[256,512]{1,0:T(8,128)(2,1)S(1)}, u32[]{:S(2)}, u32[]{:S(2)}) collective-permute-start(bf16[256,512]{1,0:T(8,128)(2,1)S(1)} %broadcast_select_fusion), channel_id=1, source_target_pairs={{16,2},{17,3},{18,0},{19,1},{20,6},{21,7},{22,4},{23,5},{24,10},{2... | collective-permute-start | bytes 786440 | tf_op jit(solution)/shard_map/ppermute | solution.py:142
  113.0 39.4 %collective-permute-start.12 = (bf16[128,4096]{1,0:T(8,128)(2,1)S(1)}, bf16[128,4096]{1,0:T(8,128)(2,1)S(1)}, u32[]{:S(2)}, u32[]{:S(2)}) collective-permute-start(bf16[128,4096]{1,0:T(8,128)(2,1)S(1)} %get-tuple-element.55), channel_id=1, source_target_pairs={{0,1},{1,0},{2,3},{3,2},{4,5},{5,4},{6,7},{7,6},{8,9},{9,8},{10,11... | collective-permute-start | bytes 3145736 | tf_op jit(solution)/shard_map/ppermute | solution.py:142
  117.3 40.5 %collective-permute-start.10 = (bf16[32,4096]{1,0:T(8,128)(2,1)S(1)}, bf16[32,4096]{1,0:T(8,128)(2,1)S(1)}, u32[]{:S(2)}, u32[]{:S(2)}) collective-permute-start(bf16[32,4096]{1,0:T(8,128)(2,1)S(1)} %constant_dynamic-slice_fusion.9), channel_id=1, source_target_pairs={{0,16},{1,17},{2,18},{3,19},{4,20},{5,21},{6,22},{7,23},{8,24},{9,... | collective-permute-start | bytes 786440 | tf_op jit(solution)/shard_map/ppermute | solution.py:142
  149.0 38.2 %collective-permute-start.58 = (bf16[128,4096]{1,0:T(8,128)(2,1)S(1)}, bf16[128,4096]{1,0:T(8,128)(2,1)S(1)}, u32[]{:S(2)}, u32[]{:S(2)}) collective-permute-start(bf16[128,4096]{1,0:T(8,128)(2,1)S(1)} %get-tuple-element.76), channel_id=1, source_target_pairs={{0,1},{1,0},{2,3},{3,2},{4,5},{5,4},{6,7},{7,6},{8,9},{9,8},{10,11... | collective-permute-start | bytes 3145736 | tf_op jit(solution)/shard_map/ppermute | solution.py:142
  155.2 31.0 %collective-permute-start.13 = (bf16[32,4096]{1,0:T(8,128)(2,1)S(1)}, bf16[32,4096]{1,0:T(8,128)(2,1)S(1)}, u32[]{:S(2)}, u32[]{:S(2)}) collective-permute-start(bf16[32,4096]{1,0:T(8,128)(2,1)S(1)} %get-tuple-element.149), channel_id=1, source_target_pairs={{0,2},{1,3},{2,0},{3,1},{4,6},{5,7},{6,4},{7,5},{8,10},{9,11},{10,... | collective-permute-start | bytes 786440 | tf_op jit(solution)/shard_map/ppermute | solution.py:142
  157.7 58.9 %collective-permute-start.57 = (bf16[32,4096]{1,0:T(8,128)(2,1)S(1)}, bf16[32,4096]{1,0:T(8,128)(2,1)S(1)}, u32[]{:S(2)}, u32[]{:S(2)}) collective-permute-start(bf16[32,4096]{1,0:T(8,128)(2,1)S(1)} %constant_dynamic-slice_fusion.4), channel_id=1, source_target_pairs={{0,16},{1,17},{2,18},{3,19},{4,20},{5,21},{6,22},{7,23},{8,24},{9,... | collective-permute-start | bytes 786440 | tf_op jit(solution)/shard_map/ppermute | solution.py:142
  223.5 35.4 %collective-permute-start.62 = (bf16[32,4096]{1,0:T(8,128)(2,1)S(1)}, bf16[32,4096]{1,0:T(8,128)(2,1)S(1)}, u32[]{:S(2)}, u32[]{:S(2)}) collective-permute-start(bf16[32,4096]{1,0:T(8,128)(2,1)S(1)} %fusion.20.refs_4_), channel_id=1, source_target_pairs={{0,1},{1,0},{2,3},{3,2},{4,5},{5,4},{6,7},{7,6},{8,9},{9,8},{10,11... | collective-permute-start | bytes 786440 | tf_op jit(solution)/shard_map/ppermute | solution.py:142
  236.5 35.9 %collective-permute-start.64 = (bf16[32,4096]{1,0:T(8,128)(2,1)S(1)}, bf16[32,4096]{1,0:T(8,128)(2,1)S(1)}, u32[]{:S(2)}, u32[]{:S(2)}) collective-permute-start(bf16[32,4096]{1,0:T(8,128)(2,1)S(1)} %fusion.20.refs_4_), channel_id=1, source_target_pairs={{0,3},{1,2},{2,1},{3,0},{4,7},{5,6},{6,5},{7,4},{8,11},{9,10},{10,... | collective-permute-start | bytes 786440 | tf_op jit(solution)/shard_map/ppermute | solution.py:142
  240.3 35.7 %collective-permute-start.65 = (bf16[32,4096]{1,0:T(8,128)(2,1)S(1)}, bf16[32,4096]{1,0:T(8,128)(2,1)S(1)}, u32[]{:S(2)}, u32[]{:S(2)}) collective-permute-start(bf16[32,4096]{1,0:T(8,128)(2,1)S(1)} %fusion.20.refs_4_), channel_id=1, source_target_pairs={{16,3},{17,2},{18,1},{19,0},{20,7},{21,6},{22,5},{23,4},{24,11},{2... | collective-permute-start | bytes 786440 | tf_op jit(solution)/shard_map/ppermute | solution.py:142
  241.6 34.4 %collective-permute-start.66 = (bf16[32,4096]{1,0:T(8,128)(2,1)S(1)}, bf16[32,4096]{1,0:T(8,128)(2,1)S(1)}, u32[]{:S(2)}, u32[]{:S(2)}) collective-permute-start(bf16[32,4096]{1,0:T(8,128)(2,1)S(1)} %fusion.20.refs_4_), channel_id=1, source_target_pairs={{16,0},{17,1},{18,2},{19,3},{20,4},{21,5},{22,6},{23,7},{24,8},{25... | collective-permute-start | bytes 786440 | tf_op jit(solution)/shard_map/ppermute | solution.py:142
  272.5 32.6 %collective-permute-start.24 = (bf16[128,4096]{1,0:T(8,128)(2,1)S(1)}, bf16[128,4096]{1,0:T(8,128)(2,1)S(1)}, u32[]{:S(2)}, u32[]{:S(2)}) collective-permute-start(bf16[128,4096]{1,0:T(8,128)(2,1)S(1)} %get-tuple-element.60), channel_id=1, source_target_pairs={{0,1},{1,0},{2,3},{3,2},{4,5},{5,4},{6,7},{7,6},{8,9},{9,8},{10,11... | collective-permute-start | bytes 3145736 | tf_op jit(solution)/shard_map/ppermute | solution.py:142
  303.1 36.5 %collective-permute-start.69 = (bf16[128,4096]{1,0:T(8,128)(2,1)S(1)}, bf16[128,4096]{1,0:T(8,128)(2,1)S(1)}, u32[]{:S(2)}, u32[]{:S(2)}) collective-permute-start(bf16[128,4096]{1,0:T(8,128)(2,1)S(1)} %get-tuple-element.84), channel_id=1, source_target_pairs={{0,1},{1,0},{2,3},{3,2},{4,5},{5,4},{6,7},{7,6},{8,9},{9,8},{10,11... | collective-permute-start | bytes 3145736 | tf_op jit(solution)/shard_map/ppermute | solution.py:142
  305.2 39.9 %collective-permute-start.27 = (bf16[32,4096]{1,0:T(8,128)(2,1)S(1)}, bf16[32,4096]{1,0:T(8,128)(2,1)S(1)}, u32[]{:S(2)}, u32[]{:S(2)}) collective-permute-start(bf16[32,4096]{1,0:T(8,128)(2,1)S(1)} %get-tuple-element.147), channel_id=1, source_target_pairs={{0,16},{1,17},{2,18},{3,19},{4,20},{5,21},{6,22},{7,23},{8,24},{9,... | collective-permute-start | bytes 786440 | tf_op jit(solution)/shard_map/ppermute | solution.py:142
  306.6 39.9 %collective-permute-start.26 = (bf16[32,4096]{1,0:T(8,128)(2,1)S(1)}, bf16[32,4096]{1,0:T(8,128)(2,1)S(1)}, u32[]{:S(2)}, u32[]{:S(2)}) collective-permute-start(bf16[32,4096]{1,0:T(8,128)(2,1)S(1)} %get-tuple-element.148), channel_id=1, source_target_pairs={{0,18},{1,19},{2,16},{3,17},{4,22},{5,23},{6,20},{7,21},{8,26},{9,... | collective-permute-start | bytes 786440 | tf_op jit(solution)/shard_map/ppermute | solution.py:142
  307.9 38.6 %collective-permute-start.25 = (bf16[32,4096]{1,0:T(8,128)(2,1)S(1)}, bf16[32,4096]{1,0:T(8,128)(2,1)S(1)}, u32[]{:S(2)}, u32[]{:S(2)}) collective-permute-start(bf16[32,4096]{1,0:T(8,128)(2,1)S(1)} %get-tuple-element.146), channel_id=1, source_target_pairs={{0,2},{1,3},{2,0},{3,1},{4,6},{5,7},{6,4},{7,5},{8,10},{9,11},{10,... | collective-permute-start | bytes 786440 | tf_op jit(solution)/shard_map/ppermute | solution.py:142
  347.5 33.6 %collective-permute-start.28 = (bf16[32,4096]{1,0:T(8,128)(2,1)S(1)}, bf16[32,4096]{1,0:T(8,128)(2,1)S(1)}, u32[]{:S(2)}, u32[]{:S(2)}) collective-permute-start(bf16[32,4096]{1,0:T(8,128)(2,1)S(1)} %fusion.12.refs_5_), channel_id=1, source_target_pairs={{0,17},{1,16},{2,19},{3,18},{4,21},{5,20},{6,23},{7,22},{8,25},{9,... | collective-permute-start | bytes 786440 | tf_op jit(solution)/shard_map/ppermute | solution.py:142
  348.8 33.6 %collective-permute-start.29 = (bf16[32,4096]{1,0:T(8,128)(2,1)S(1)}, bf16[32,4096]{1,0:T(8,128)(2,1)S(1)}, u32[]{:S(2)}, u32[]{:S(2)}) collective-permute-start(bf16[32,4096]{1,0:T(8,128)(2,1)S(1)} %fusion.12.refs_5_), channel_id=1, source_target_pairs={{16,17},{17,16},{18,19},{19,18},{20,21},{21,20},{22,23},{23,22},{2... | collective-permute-start | bytes 786440 | tf_op jit(solution)/shard_map/ppermute | solution.py:142
  383.3 39.2 %collective-permute-start.73 = (bf16[32,4096]{1,0:T(8,128)(2,1)S(1)}, bf16[32,4096]{1,0:T(8,128)(2,1)S(1)}, u32[]{:S(2)}, u32[]{:S(2)}) collective-permute-start(bf16[32,4096]{1,0:T(8,128)(2,1)S(1)} %fusion.24.refs_5_), channel_id=1, source_target_pairs={{0,17},{1,16},{2,19},{3,18},{4,21},{5,20},{6,23},{7,22},{8,25},{9,... | collective-permute-start | bytes 786440 | tf_op jit(solution)/shard_map/ppermute | solution.py:142
  388.1 35.7 %collective-permute-start.74 = (bf16[32,4096]{1,0:T(8,128)(2,1)S(1)}, bf16[32,4096]{1,0:T(8,128)(2,1)S(1)}, u32[]{:S(2)}, u32[]{:S(2)}) collective-permute-start(bf16[32,4096]{1,0:T(8,128)(2,1)S(1)} %fusion.24.refs_5_), channel_id=1, source_target_pairs={{16,17},{17,16},{18,19},{19,18},{20,21},{21,20},{22,23},{23,22},{2... | collective-permute-start | bytes 786440 | tf_op jit(solution)/shard_map/ppermute | solution.py:142
  388.8 42.0 %collective-permute-start.75 = (bf16[32,4096]{1,0:T(8,128)(2,1)S(1)}, bf16[32,4096]{1,0:T(8,128)(2,1)S(1)}, u32[]{:S(2)}, u32[]{:S(2)}) collective-permute-start(bf16[32,4096]{1,0:T(8,128)(2,1)S(1)} %fusion.24.refs_5_), channel_id=1, source_target_pairs={{0,19},{1,18},{2,17},{3,16},{4,23},{5,22},{6,21},{7,20},{8,27},{9,... | collective-permute-start | bytes 786440 | tf_op jit(solution)/shard_map/ppermute | solution.py:142
  483.8 33.6 %collective-permute-start.39 = (bf16[32,4096]{1,0:T(8,128)(2,1)S(1)}, bf16[32,4096]{1,0:T(8,128)(2,1)S(1)}, u32[]{:S(2)}, u32[]{:S(2)}) collective-permute-start(bf16[32,4096]{1,0:T(8,128)(2,1)S(1)} %fusion.16.refs_5_), channel_id=1, source_target_pairs={{0,17},{1,16},{2,19},{3,18},{4,21},{5,20},{6,23},{7,22},{8,25},{9,... | collective-permute-start | bytes 786440 | tf_op jit(solution)/shard_map/ppermute | solution.py:142
  519.5 37.3 %collective-permute-start.84 = (bf16[32,4096]{1,0:T(8,128)(2,1)S(1)}, bf16[32,4096]{1,0:T(8,128)(2,1)S(1)}, u32[]{:S(2)}, u32[]{:S(2)}) collective-permute-start(bf16[32,4096]{1,0:T(8,128)(2,1)S(1)} %fusion.28.refs_5_), channel_id=1, source_target_pairs={{0,17},{1,16},{2,19},{3,18},{4,21},{5,20},{6,23},{7,22},{8,25},{9,... | collective-permute-start | bytes 786440 | tf_op jit(solution)/shard_map/ppermute | solution.py:142
  522.4 35.7 %collective-permute-start.85 = (bf16[32,4096]{1,0:T(8,128)(2,1)S(1)}, bf16[32,4096]{1,0:T(8,128)(2,1)S(1)}, u32[]{:S(2)}, u32[]{:S(2)}) collective-permute-start(bf16[32,4096]{1,0:T(8,128)(2,1)S(1)} %fusion.28.refs_5_), channel_id=1, source_target_pairs={{16,17},{17,16},{18,19},{19,18},{20,21},{21,20},{22,23},{23,22},{2... | collective-permute-start | bytes 786440 | tf_op jit(solution)/shard_map/ppermute | solution.py:142
  523.1 44.1 %collective-permute-start.86 = (bf16[32,4096]{1,0:T(8,128)(2,1)S(1)}, bf16[32,4096]{1,0:T(8,128)(2,1)S(1)}, u32[]{:S(2)}, u32[]{:S(2)}) collective-permute-start(bf16[32,4096]{1,0:T(8,128)(2,1)S(1)} %fusion.28.refs_5_), channel_id=1, source_target_pairs={{0,19},{1,18},{2,17},{3,16},{4,23},{5,22},{6,21},{7,20},{8,27},{9,... | collective-permute-start | bytes 786440 | tf_op jit(solution)/shard_map/ppermute | solution.py:142
  535.4 32.7 %collective-permute-start.87 = (bf16[32,4096]{1,0:T(8,128)(2,1)S(1)}, bf16[32,4096]{1,0:T(8,128)(2,1)S(1)}, u32[]{:S(2)}, u32[]{:S(2)}) collective-permute-start(bf16[32,4096]{1,0:T(8,128)(2,1)S(1)} %fusion.28.refs_5_), channel_id=1, source_target_pairs={{16,19},{17,18},{18,17},{19,16},{20,23},{21,22},{22,21},{23,20},{2... | collective-permute-start | bytes 786440 | tf_op jit(solution)/shard_map/ppermute | solution.py:142
  536.1 32.0 %collective-permute-start.88 = (bf16[32,4096]{1,0:T(8,128)(2,1)S(1)}, bf16[32,4096]{1,0:T(8,128)(2,1)S(1)}, u32[]{:S(2)}, u32[]{:S(2)}) collective-permute-start(bf16[32,4096]{1,0:T(8,128)(2,1)S(1)} %fusion.28.refs_5_), channel_id=1, source_target_pairs={{0,16},{1,17},{2,18},{3,19},{4,20},{5,21},{6,22},{7,23},{8,24},{9,... | collective-permute-start | bytes 786440 | tf_op jit(solution)/shard_map/ppermute | solution.py:142
  597.2 39.1 %collective-permute-start.94 = (bf16[32,4096]{1,0:T(8,128)(2,1)S(1)}, bf16[32,4096]{1,0:T(8,128)(2,1)S(1)}, u32[]{:S(2)}, u32[]{:S(2)}) collective-permute-start(bf16[32,4096]{1,0:T(8,128)(2,1)S(1)} %get-tuple-element.129), channel_id=1, source_target_pairs={{16,0},{17,1},{18,2},{19,3},{20,4},{21,5},{22,6},{23,7},{24,8},{25... | collective-permute-start | bytes 786440 | tf_op jit(solution)/shard_map/ppermute | solution.py:142
  598.5 37.8 %collective-permute-start.93 = (bf16[32,4096]{1,0:T(8,128)(2,1)S(1)}, bf16[32,4096]{1,0:T(8,128)(2,1)S(1)}, u32[]{:S(2)}, u32[]{:S(2)}) collective-permute-start(bf16[32,4096]{1,0:T(8,128)(2,1)S(1)} %get-tuple-element.130), channel_id=1, source_target_pairs={{16,18},{17,19},{18,16},{19,17},{20,22},{21,23},{22,20},{23,21},{2... | collective-permute-start | bytes 786440 | tf_op jit(solution)/shard_map/ppermute | solution.py:142
  607.5 46.8 %collective-permute-start.92 = (bf16[32,4096]{1,0:T(8,128)(2,1)S(1)}, bf16[32,4096]{1,0:T(8,128)(2,1)S(1)}, u32[]{:S(2)}, u32[]{:S(2)}) collective-permute-start(bf16[32,4096]{1,0:T(8,128)(2,1)S(1)} %get-tuple-element.128), channel_id=1, source_target_pairs={{16,2},{17,3},{18,0},{19,1},{20,6},{21,7},{22,4},{23,5},{24,10},{2... | collective-permute-start | bytes 786440 | tf_op jit(solution)/shard_map/ppermute | solution.py:142
  (85 other events, 1510.4 us)

commit v5 on v4

--- a/solution.py
+++ b/solution.py
@@ -12,8 +12,8 @@
 EPSILON = 1e-05
 ROTARY_FREQ_BASE = 10000.0
 BOTH = ("section", "tensor")
-WIDE = 256
-OUT_WIDE = 1024
+WIDE = 512
+OUT_WIDE = 2048
 VMEM_LIMIT = 50 * 2**20
 
 
@@ -142,24 +142,25 @@
     return lax.ppermute(value, BOTH, links)
 
 
-def slot_order(count):
+def slot_order(count, direct=False):
     bits = [1 << bit for bit in range(count.bit_length() - 1)]
     groups, left = [], list(range(count))
     for bit in bits[:-1]:
-        groups.append([j for j in left if j & bit])
-        left = [j for j in left if not j & bit]
+        straight = [bit] if direct else []
+        groups.append([j for j in left if j & bit and j not in straight])
+        left = [j for j in left if not j & bit or j in straight]
     return groups, left
 
 
-def row_cuts(length):
+def row_cuts(length, direct=False):
     sections, tensors = lax.axis_size("section"), lax.axis_size("tensor")
     share = length // tensors
-    groups, left = slot_order(tensors)
+    groups, left = slot_order(tensors, direct)
     return [len(g) * share for g in groups] + [share // sections] * (sections * len(left))
 
 
-def gather_rows(own, layer):
-    groups, left = slot_order(lax.axis_size("tensor"))
+def gather_rows(own, layer, direct=False):
+    groups, left = slot_order(lax.axis_size("tensor"), direct)
     pieces = []
     for j in sum(groups, []) + left:
         for source in range(lax.axis_size("section")):
@@ -168,9 +169,9 @@
     return pieces
 
 
-def sum_nearby(partial, layer):
+def sum_nearby(partial, layer, direct=False):
     sections, tensors = lax.axis_size("section"), lax.axis_size("tensor")
-    groups, left = slot_order(tensors)
+    groups, left = slot_order(tensors, direct)
     rows = partial[-1].shape[0]
     held = {}
     for group, array in zip(groups, partial):
@@ -197,11 +198,14 @@
     return [[value(held[j, h]).astype(jnp.bfloat16) for h in range(sections)] for j in left]
 
 
-def send_to_owners(nearby, layer):
+def send_to_owners(nearby, layer, direct=False):
     sections, tensors = lax.axis_size("section"), lax.axis_size("tensor")
-    near, far = nearby if len(nearby) == 2 else (nearby[0], [])
-    arrived = [send(piece, layer, h, tensors // 2) for h, piece in enumerate(far)]
-    return arrived + [send(near[h], layer, h, 0) for h in range(sections) if h != layer]
+    return [
+        send(piece, layer, h, j)
+        for j, pieces in zip(slot_order(tensors, direct)[1], nearby)
+        for h, piece in enumerate(pieces)
+        if j or h != layer
+    ]
 
 
 def sum_arrived(nearby, arrived, layer):
@@ -270,7 +274,6 @@
     tables = (cosine, sine, positions[:, None], positions[None, :])
 
     rows = share // sections
-    cuts = row_cuts(length)
     gains_attn, gains_mlp = layer_gains(gain_attn), layer_gains(gain_mlp)
 
     def embed(looked):
@@ -299,12 +302,15 @@
             mine = jnp.where(section == h, send(own[h], 0, h, 0), mine)
         return pieces, mine
 
-    def compute(half, pieces):
+    def compute(half, pieces, ready):
+        cuts = row_cuts(length, half + 1 == halves)
         if half % 2:
             inner = inward(gate_kernel, "gate", (), (w_gate, w_up), pieces)
+            inner = after(inner, ready) if ready else inner
             return outward("down", inner, w_down, cuts)
         weights = (w_query, w_key, w_value)
         inner = inward(attention_kernel, "attention", tables, weights, pieces)
+        inner = after(inner, ready) if ready else inner
         return outward("out", inner, w_out, cuts)
 
     def add(base, sums):
@@ -327,10 +333,10 @@
                     arrived[c] = after(arrived[c], normed)
                 hidden[c] = add(hidden[c], sum_arrived(nearby[c], arrived[c], (half - 1) // 2))
                 normed = rms_norm(hidden[c], gains[half])
-                pieces = gather_rows(normed, half // 2)
-            partial = compute(half, pieces)
-            nearby[c] = sum_nearby(partial, half // 2)
-            arrived[c] = send_to_owners(nearby[c], half // 2)
+                pieces = gather_rows(normed, half // 2, half + 1 == halves)
+            partial = compute(half, pieces, [hidden[c]] if half == 0 else [])
+            nearby[c] = sum_nearby(partial, half // 2, half + 1 == halves)
+            arrived[c] = send_to_owners(nearby[c], half // 2, half + 1 == halves)
     for c in range(per_device):
         hidden[c] = add(hidden[c], sum_arrived(nearby[c], arrived[c], sections - 1))
 

time: 683 us -> 688 us (level)
  Pallas kernels: 177 us -> 164 us
  waiting for transfers between devices: 192 us -> 202 us
    ppermute x90 -> x94, waiting for transfers between devices: 187 us -> 197 us  [send(): return lax.ppermute(value, BOTH, links)]
    pallas_call x8, Pallas kernels: 120 us -> 111 us  [inward(): pl.pallas_call(functools.partial(kernel, len(pieces)), out_shape=jax.Shap...]
    ppermute x90 -> x94, starting transfers between devices: 239 us -> 244 us  [send(): return lax.ppermute(value, BOTH, links)]
  transfers between devices with their start and end apart: 103 -> 107, of which waited for: 24 -> 23; matrix products, arithmetic and copies ran while one was open for 6% -> 6% of each run, Pallas kernels for 26% -> 23%
where the time goes in v5:
time: 688 us; the launch traced here: 678 us
  starting transfers between devices  259 us (38%)
  waiting for transfers between devices  202 us (29%)
  Pallas kernels  164 us (24%)
  local copies, waits for them, and re-layouts  25.6 us (4%)
  other arithmetic  22.1 us (3%)
    ppermute x94, starting transfers between devices, send(): return lax.ppermute(value, BOTH, links)  244 us
    ppermute x94, waiting for transfers between devices, send(): return lax.ppermute(value, BOTH, links)  197 us
    pallas_call x8, Pallas kernels, inward(): pl.pallas_call(functools.partial(kernel, len(pieces)), out_shape=jax.Shap...  111 us
    pallas_call x8, Pallas kernels, outward(): pl.pallas_call(down_kernel, out_shape=[jax.ShapeDtypeStruct((rows, width)...  53.1 us
    gather x2, local copies, waits for them, and re-layouts, body(): jnp.take(embed_table, tokens[c], axis=0)  18 us
  transfers between devices with their start and end apart: 107, of which 23 were waited for; matrix products, arithmetic and copies ran while one was open for 6% of the time, Pallas kernels for 23%

profile of v5, /device:TPU:0, one launch (start us, length us, event | category | flops | bytes accessed | tf_op | source)
XLA Modules:
  0.0 678.3 jit_solution(5436638799511795629)
XLA Ops:
  15.2 9.0 %gather_fusion.5 = bf16[256,512]{1,0:T(8,128)(2,1)S(1)} fusion(bf16[16000,512]{1,0:T(8,128)(2,1)} %param.25, s32[1024]{0:T(1024)S(1)} %pad_clamp_fusion.2), kind=kCustom, calls=%fused_computation.1.clone | custom fusion | bytes 525312 | tf_op jit(solution)/shard_map/jit(_take)/gather | solution.py:321
  34.6 9.0 %gather_fusion.6 = bf16[256,512]{1,0:T(8,128)(2,1)S(1)} fusion(bf16[16000,512]{1,0:T(8,128)(2,1)} %param.25, s32[1024]{0:T(1024)S(1)} %pad_clamp_fusion), kind=kCustom, calls=%fused_computation.3.clone | custom fusion | bytes 525312 | tf_op jit(solution)/shard_map/jit(_take)/gather | solution.py:321
  57.6 17.1 %collective-permute-done.8 = bf16[256,512]{1,0:T(8,128)(2,1)S(1)} collective-permute-done((bf16[256,512]{1,0:T(8,128)(2,1)S(1)}, bf16[256,512]{1,0:T(8,128)(2,1)S(1)}, u32[]{:S(2)}, u32[]{:S(2)}) %collective-permute-start.8) | collective-permute-done | bytes 262176 | tf_op jit(solution)/shard_map/ppermute | solution.py:142
  76.4 6.2 collective-permute-start.54
  90.1 13.1 %attention.4.x_ref = bf16[256,1024]{1,0:T(8,128)(2,1)S(1)} custom-call(f32[256,128]{1,0:T(8,128)S(1)} %bitcast.75, f32[256,128]{1,0:T(8,128)S(1)} %bitcast.79, s32[256,1]{1,0:T(8,128)S(1)} %add.571.row_ref, s32[1,256]{1,0:T(1,128)S(1)} %add.468.col_ref, bf16[1,4096,1024]{2,1,0:T(8,128)(2,1)} %wq_ref.7, bf16[1,4096,1024]{2,1,0:T(8,128)(2,1)} %wk_ref.7, ...), custom_call_target="tpu_custom_call" | custom-call | flops 6442450944 | bytes 29360128 | tf_op jit(solution)/shard_map/attention/pallas_call | solution.py:108
  106.6 7.2 %collective-permute-start.10 = (bf16[32,4096]{1,0:T(8,128)(2,1)S(1)}, bf16[32,4096]{1,0:T(8,128)(2,1)S(1)}, u32[]{:S(2)}, u32[]{:S(2)}) collective-permute-start(bf16[32,4096]{1,0:T(8,128)(2,1)S(1)} %constant_dynamic-slice_fusion.9), channel_id=1, source_target_pairs={{0,16},{1,17},{2,18},{3,19},{4,20},{5,21},{6,22},{7,23},{8,24},{9,... | collective-permute-start | bytes 786440 | tf_op jit(solution)/shard_map/ppermute | solution.py:142
  135.9 13.1 %attention.6.x_ref = bf16[256,1024]{1,0:T(8,128)(2,1)S(1)} custom-call(f32[256,128]{1,0:T(8,128)S(1)} %bitcast.76, f32[256,128]{1,0:T(8,128)S(1)} %bitcast.80, s32[256,1]{1,0:T(8,128)S(1)} %add.571.row_ref, s32[1,256]{1,0:T(1,128)S(1)} %add.468.col_ref, bf16[1,4096,1024]{2,1,0:T(8,128)(2,1)} %wq_ref.7, bf16[1,4096,1024]{2,1,0:T(8,128)(2,1)} %wk_ref.7, ...), custom_call_target="tpu_custom_call" | custom-call | flops 6442450944 | bytes 29360128 | tf_op jit(solution)/shard_map/attention/pallas_call | solution.py:108
  165.6 21.6 %collective-permute-done.15 = bf16[32,4096]{1,0:T(8,128)(2,1)S(1)} collective-permute-done((bf16[32,4096]{1,0:T(8,128)(2,1)}, bf16[32,4096]{1,0:T(8,128)(2,1)S(1)}, u32[]{:S(2)}, u32[]{:S(2)}) %collective-permute-start.15) | collective-permute-done | bytes 262176 | tf_op jit(solution)/shard_map/ppermute | solution.py:142
  209.1 14.9 %collective-permute-done.62 = bf16[32,4096]{1,0:T(8,128)(2,1)S(1)} collective-permute-done((bf16[32,4096]{1,0:T(8,128)(2,1)S(1)}, bf16[32,4096]{1,0:T(8,128)(2,1)S(1)}, u32[]{:S(2)}, u32[]{:S(2)}) %collective-permute-start.62) | collective-permute-done | bytes 262176 | tf_op jit(solution)/shard_map/ppermute | solution.py:142
  235.2 8.2 %collective-permute-start.64 = (bf16[32,4096]{1,0:T(8,128)(2,1)S(1)}, bf16[32,4096]{1,0:T(8,128)(2,1)S(1)}, u32[]{:S(2)}, u32[]{:S(2)}) collective-permute-start(bf16[32,4096]{1,0:T(8,128)(2,1)S(1)} %fusion.20.refs_4_), channel_id=1, source_target_pairs={{0,1},{1,0},{2,3},{3,2},{4,5},{5,4},{6,7},{7,6},{8,9},{9,8},{10,11... | collective-permute-start | bytes 786440 | tf_op jit(solution)/shard_map/ppermute | solution.py:142
  251.3 14.5 %gate.4.x_ref = bf16[256,2048]{1,0:T(8,128)(2,1)S(1)} custom-call(bf16[1,4096,2048]{2,1,0:T(8,128)(2,1)} %wg_ref.7, bf16[1,4096,2048]{2,1,0:T(8,128)(2,1)} %wu_ref.7, bf16[32,4096]{1,0:T(8,128)(2,1)S(1)} %collective-permute-done.17.refs_0_, bf16[32,4096]{1,0:T(8,128)(2,1)S(1)} %collective-permute-done.18.refs_1_, ...), custom_call_target="tpu_custom_call" | custom-call | flops 8589934592 | bytes 37748736 | tf_op jit(solution)/shard_map/gate/pallas_call | solution.py:108
  269.3 8.2 %down.4 = (bf16[128,4096]{1,0:T(8,128)(2,1)S(1)}, bf16[32,4096]{1,0:T(8,128)(2,1)S(1)}, bf16[32,4096]{1,0:T(8,128)(2,1)S(1)}, bf16[32,4096]{1,0:T(8,128)(2,1)S(1)}, bf16[32,4096]{1,0:T(8,128)(2,1)S(1)}) custom-call(bf16[256,2048]{1,0:T(8,128)(2,1)S(1)} %gate.4.x_ref, bf16[1,2048,4096]{2,1,0:T(8,128)(2,1)} %w_ref.15), custom_call_target="tpu_custom_call" | custom-call | flops 4294967296 | bytes 20971520 | tf_op jit(solution)/shard_map/down/pallas_call | solution.py:127
  281.5 14.5 %gate.6.x_ref = bf16[256,2048]{1,0:T(8,128)(2,1)S(1)} custom-call(bf16[1,4096,2048]{2,1,0:T(8,128)(2,1)} %wg_ref.7, bf16[1,4096,2048]{2,1,0:T(8,128)(2,1)} %wu_ref.7, bf16[32,4096]{1,0:T(8,128)(2,1)S(1)} %collective-permute-done.64.refs_0_, bf16[32,4096]{1,0:T(8,128)(2,1)S(1)} %collective-permute-done.65.refs_1_, ...), custom_call_target="tpu_custom_call" | custom-call | flops 8589934592 | bytes 37748736 | tf_op jit(solution)/shard_map/gate/pallas_call | solution.py:108
  296.0 8.2 %down.6 = (bf16[128,4096]{1,0:T(8,128)(2,1)S(1)}, bf16[32,4096]{1,0:T(8,128)(2,1)S(1)}, bf16[32,4096]{1,0:T(8,128)(2,1)S(1)}, bf16[32,4096]{1,0:T(8,128)(2,1)S(1)}, bf16[32,4096]{1,0:T(8,128)(2,1)S(1)}) custom-call(bf16[256,2048]{1,0:T(8,128)(2,1)S(1)} %gate.6.x_ref, bf16[1,2048,4096]{2,1,0:T(8,128)(2,1)} %w_ref.15), custom_call_target="tpu_custom_call" | custom-call | flops 4294967296 | bytes 20971520 | tf_op jit(solution)/shard_map/down/pallas_call | solution.py:127
  314.2 19.1 %collective-permute-done.27 = bf16[32,4096]{1,0:T(8,128)(2,1)S(1)} collective-permute-done((bf16[32,4096]{1,0:T(8,128)(2,1)S(1)}, bf16[32,4096]{1,0:T(8,128)(2,1)S(1)}, u32[]{:S(2)}, u32[]{:S(2)}) %collective-permute-start.27) | collective-permute-done | bytes 262176 | tf_op jit(solution)/shard_map/ppermute | solution.py:142
  349.4 12.2 %collective-permute-done.73 = bf16[32,4096]{1,0:T(8,128)(2,1)S(1)} collective-permute-done((bf16[32,4096]{1,0:T(8,128)(2,1)S(1)}, bf16[32,4096]{1,0:T(8,128)(2,1)S(1)}, u32[]{:S(2)}, u32[]{:S(2)}) %collective-permute-start.73) | collective-permute-done | bytes 262176 | tf_op jit(solution)/shard_map/ppermute | solution.py:142
  362.7 10.7 %collective-permute-start.32 = (bf16[32,4096]{1,0:T(8,128)(2,1)S(1)}, bf16[32,4096]{1,0:T(8,128)(2,1)S(1)}, u32[]{:S(2)}, u32[]{:S(2)}) collective-permute-start(bf16[32,4096]{1,0:T(8,128)(2,1)S(1)} %fusion.12.refs_5_), channel_id=1, source_target_pairs={{0,16},{1,17},{2,18},{3,19},{4,20},{5,21},{6,22},{7,23},{8,24},{9,... | collective-permute-start | bytes 786440 | tf_op jit(solution)/shard_map/ppermute | solution.py:142
  386.3 10.0 %collective-permute-start.79 = (bf16[32,4096]{1,0:T(8,128)(2,1)S(1)}, bf16[32,4096]{1,0:T(8,128)(2,1)S(1)}, u32[]{:S(2)}, u32[]{:S(2)}) collective-permute-start(bf16[32,4096]{1,0:T(8,128)(2,1)S(1)} %fusion.24.refs_5_), channel_id=1, source_target_pairs={{0,16},{1,17},{2,18},{3,19},{4,20},{5,21},{6,22},{7,23},{8,24},{9,... | collective-permute-start | bytes 786440 | tf_op jit(solution)/shard_map/ppermute | solution.py:142
  396.2 13.2 %attention.5.x_ref = bf16[256,1024]{1,0:T(8,128)(2,1)S(1)} custom-call(f32[256,128]{1,0:T(8,128)S(1)} %bitcast.77, f32[256,128]{1,0:T(8,128)S(1)} %bitcast.81, s32[256,1]{1,0:T(8,128)S(1)} %add.571.row_ref, s32[1,256]{1,0:T(1,128)S(1)} %add.468.col_ref, bf16[1,4096,1024]{2,1,0:T(8,128)(2,1)} %wq_ref.7, bf16[1,4096,1024]{2,1,0:T(8,128)(2,1)} %wk_ref.7, ...), custom_call_target="tpu_custom_call" | custom-call | flops 6442450944 | bytes 29360128 | tf_op jit(solution)/shard_map/attention/pallas_call | solution.py:108
  423.5 13.2 %attention.7.x_ref = bf16[256,1024]{1,0:T(8,128)(2,1)S(1)} custom-call(f32[256,128]{1,0:T(8,128)S(1)} %bitcast.78, f32[256,128]{1,0:T(8,128)S(1)} %bitcast.82, s32[256,1]{1,0:T(8,128)S(1)} %add.571.row_ref, s32[1,256]{1,0:T(1,128)S(1)} %add.468.col_ref, bf16[1,4096,1024]{2,1,0:T(8,128)(2,1)} %wq_ref.7, bf16[1,4096,1024]{2,1,0:T(8,128)(2,1)} %wk_ref.7, ...), custom_call_target="tpu_custom_call" | custom-call | flops 6442450944 | bytes 29360128 | tf_op jit(solution)/shard_map/attention/pallas_call | solution.py:108
  449.2 20.6 %collective-permute-done.37 = bf16[32,4096]{1,0:T(8,128)(2,1)S(1)} collective-permute-done((bf16[32,4096]{1,0:T(8,128)(2,1)}, bf16[32,4096]{1,0:T(8,128)(2,1)S(1)}, u32[]{:S(2)}, u32[]{:S(2)}) %collective-permute-start.37) | collective-permute-done | bytes 262176 | tf_op jit(solution)/shard_map/ppermute | solution.py:142
  476.3 21.8 %collective-permute-start.39 = (bf16[32,4096]{1,0:T(8,128)(2,1)S(1)}, bf16[32,4096]{1,0:T(8,128)(2,1)S(1)}, u32[]{:S(2)}, u32[]{:S(2)}) collective-permute-start(bf16[32,4096]{1,0:T(8,128)(2,1)S(1)} %fusion.16.refs_3_), channel_id=1, source_target_pairs={{0,19},{1,18},{2,17},{3,16},{4,23},{5,22},{6,21},{7,20},{8,27},{9,... | collective-permute-start | bytes 786440 | tf_op jit(solution)/shard_map/ppermute | solution.py:142
  501.9 13.3 %collective-permute-done.84 = bf16[32,4096]{1,0:T(8,128)(2,1)S(1)} collective-permute-done((bf16[32,4096]{1,0:T(8,128)(2,1)S(1)}, bf16[32,4096]{1,0:T(8,128)(2,1)S(1)}, u32[]{:S(2)}, u32[]{:S(2)}) %collective-permute-start.84) | collective-permute-done | bytes 262176 | tf_op jit(solution)/shard_map/ppermute | solution.py:142
  518.7 10.0 %collective-permute-start.44 = (bf16[32,4096]{1,0:T(8,128)(2,1)S(1)}, bf16[32,4096]{1,0:T(8,128)(2,1)S(1)}, u32[]{:S(2)}, u32[]{:S(2)}) collective-permute-start(bf16[32,4096]{1,0:T(8,128)(2,1)S(1)} %fusion.16.refs_3_), channel_id=1, source_target_pairs={{0,18},{1,19},{2,16},{3,17},{4,22},{5,23},{6,20},{7,21},{8,26},{9,... | collective-permute-start | bytes 786440 | tf_op jit(solution)/shard_map/ppermute | solution.py:142
  541.1 14.5 %gate.5.x_ref = bf16[256,2048]{1,0:T(8,128)(2,1)S(1)} custom-call(bf16[1,4096,2048]{2,1,0:T(8,128)(2,1)} %wg_ref.7, bf16[1,4096,2048]{2,1,0:T(8,128)(2,1)} %wu_ref.7, bf16[32,4096]{1,0:T(8,128)(2,1)S(1)} %collective-permute-done.39.refs_0_, bf16[32,4096]{1,0:T(8,128)(2,1)S(1)} %collective-permute-done.40.refs_1_, ...), custom_call_target="tpu_custom_call" | custom-call | flops 8589934592 | bytes 37748736 | tf_op jit(solution)/shard_map/gate/pallas_call | solution.py:108
  555.6 12.3 %collective-permute-start.91 = (bf16[32,4096]{1,0:T(8,128)(2,1)S(1)}, bf16[32,4096]{1,0:T(8,128)(2,1)S(1)}, u32[]{:S(2)}, u32[]{:S(2)}) collective-permute-start(bf16[32,4096]{1,0:T(8,128)(2,1)S(1)} %fusion.28.refs_3_), channel_id=1, source_target_pairs={{0,18},{1,19},{2,16},{3,17},{4,22},{5,23},{6,20},{7,21},{8,26},{9,... | collective-permute-start | bytes 786440 | tf_op jit(solution)/shard_map/ppermute | solution.py:142
  568.5 8.2 %down.5 = (bf16[64,4096]{1,0:T(8,128)(2,1)S(1)}, bf16[32,4096]{1,0:T(8,128)(2,1)S(1)}, bf16[32,4096]{1,0:T(8,128)(2,1)S(1)}, bf16[32,4096]{1,0:T(8,128)(2,1)S(1)...) custom-call(bf16[256,2048]{1,0:T(8,128)(2,1)S(1)} %gate.5.x_ref, ...), custom_call_target="tpu_custom_call" | custom-call | flops 4294967296 | bytes 20971520 | tf_op jit(solution)/shard_map/down/pallas_call | solution.py:127
  580.8 14.5 %gate.7.x_ref = bf16[256,2048]{1,0:T(8,128)(2,1)S(1)} custom-call(bf16[1,4096,2048]{2,1,0:T(8,128)(2,1)} %wg_ref.7, bf16[1,4096,2048]{2,1,0:T(8,128)(2,1)} %wu_ref.7, bf16[32,4096]{1,0:T(8,128)(2,1)S(1)} %collective-permute-done.86.refs_0_, bf16[32,4096]{1,0:T(8,128)(2,1)S(1)} %collective-permute-done.87.refs_1_, ...), custom_call_target="tpu_custom_call" | custom-call | flops 8589934592 | bytes 37748736 | tf_op jit(solution)/shard_map/gate/pallas_call | solution.py:108
  595.3 8.2 %down.7 = (bf16[64,4096]{1,0:T(8,128)(2,1)S(1)}, bf16[32,4096]{1,0:T(8,128)(2,1)S(1)}, bf16[32,4096]{1,0:T(8,128)(2,1)S(1)}, bf16[32,4096]{1,0:T(8,128)(2,1)S(1)...) custom-call(bf16[256,2048]{1,0:T(8,128)(2,1)S(1)} %gate.7.x_ref, ...), custom_call_target="tpu_custom_call" | custom-call | flops 4294967296 | bytes 20971520 | tf_op jit(solution)/shard_map/down/pallas_call | solution.py:127
  610.5 27.8 %collective-permute-done.50 = bf16[32,4096]{1,0:T(8,128)(2,1)S(1)} collective-permute-done((bf16[32,4096]{1,0:T(8,128)(2,1)S(1)}, bf16[32,4096]{1,0:T(8,128)(2,1)S(1)}, u32[]{:S(2)}, u32[]{:S(2)}) %collective-permute-start.50) | collective-permute-done | bytes 262176 | tf_op jit(solution)/shard_map/ppermute | solution.py:142
  639.9 11.0 %collective-permute-done.94 = bf16[32,4096]{1,0:T(8,128)(2,1)S(1)} collective-permute-done((bf16[32,4096]{1,0:T(8,128)(2,1)S(1)}, bf16[32,4096]{1,0:T(8,128)(2,1)S(1)}, u32[]{:S(2)}, u32[]{:S(2)}) %collective-permute-start.94) | collective-permute-done | bytes 262176 | tf_op jit(solution)/shard_map/ppermute | solution.py:142
  650.9 8.9 %collective-permute-done.97 = bf16[32,4096]{1,0:T(8,128)(2,1)S(1)} collective-permute-done((bf16[32,4096]{1,0:T(8,128)(2,1)S(1)}, bf16[32,4096]{1,0:T(8,128)(2,1)S(1)}, u32[]{:S(2)}, u32[]{:S(2)}) %collective-permute-start.97) | collective-permute-done | bytes 262176 | tf_op jit(solution)/shard_map/ppermute | solution.py:142
  (337 shorter events, 258.5 us)
Async XLA Ops:
  3.9 39.8 %collective-permute-start.16 = (bf16[1,4096]{1,0:T(2,128)(2,1)}, bf16[1,4096]{1,0:T(2,128)(2,1)S(1)}, u32[]{:S(2)}, u32[]{:S(2)}) collective-permute-start(bf16[1,4096]{1,0:T(2,128)(2,1)} %param.31), channel_id=1, source_target_pairs={{0,16},{16,0},{1,17},{17,1},{2,18},{18,2},{3,19},{19,3},{4,20},{20... | collective-permute-start | bytes 24584 | tf_op jit(solution)/shard_map/ppermute | solution.py:228
  5.4 39.6 %collective-permute-start.11 = (bf16[1,4096]{1,0:T(2,128)(2,1)}, bf16[1,4096]{1,0:T(2,128)(2,1)S(1)}, u32[]{:S(2)}, u32[]{:S(2)}) collective-permute-start(bf16[1,4096]{1,0:T(2,128)(2,1)} %param.26), channel_id=1, source_target_pairs={{0,16},{16,0},{1,17},{17,1},{2,18},{18,2},{3,19},{19,3},{4,20},{20... | collective-permute-start | bytes 24584 | tf_op jit(solution)/shard_map/ppermute | solution.py:228
  45.0 29.7 %collective-permute-start.8 = (bf16[256,512]{1,0:T(8,128)(2,1)S(1)}, bf16[256,512]{1,0:T(8,128)(2,1)S(1)}, u32[]{:S(2)}, u32[]{:S(2)}) collective-permute-start(bf16[256,512]{1,0:T(8,128)(2,1)S(1)} %broadcast_select_fusion.1), channel_id=1, source_target_pairs={{16,2},{17,3},{18,0},{19,1},{20,6},{21,7},{22,4},{23,5},{24,10},{2... | collective-permute-start | bytes 786440 | tf_op jit(solution)/shard_map/ppermute | solution.py:142
  154.0 39.1 %collective-permute-start.60 = (bf16[128,4096]{1,0:T(8,128)(2,1)S(1)}, bf16[128,4096]{1,0:T(8,128)(2,1)}, u32[]{:S(2)}, u32[]{:S(2)}) collective-permute-start(bf16[128,4096]{1,0:T(8,128)(2,1)S(1)} %get-tuple-element.86), channel_id=1, source_target_pairs={{0,1},{1,0},{2,3},{3,2},{4,5},{5,4},{6,7},{7,6},{8,9},{9,8},{10,11... | collective-permute-start | bytes 3145736 | tf_op jit(solution)/shard_map/ppermute | solution.py:142
  161.5 30.1 %collective-permute-start.14 = (bf16[32,4096]{1,0:T(8,128)(2,1)}, bf16[32,4096]{1,0:T(8,128)(2,1)}, u32[]{:S(2)}, u32[]{:S(2)}) collective-permute-start(bf16[32,4096]{1,0:T(8,128)(2,1)} %get-tuple-element.157), channel_id=1, source_target_pairs={{0,2},{1,3},{2,0},{3,1},{4,6},{5,7},{6,4},{7,5},{8,10},{9,11},{10,... | collective-permute-start | bytes 786440 | tf_op jit(solution)/shard_map/ppermute | solution.py:142
  204.4 29.3 %collective-permute-start.18 = (bf16[32,4096]{1,0:T(8,128)(2,1)S(1)}, bf16[32,4096]{1,0:T(8,128)(2,1)S(1)}, u32[]{:S(2)}, u32[]{:S(2)}) collective-permute-start(bf16[32,4096]{1,0:T(8,128)(2,1)S(1)} %fusion.8.refs_4_), channel_id=1, source_target_pairs={{16,1},{17,0},{18,3},{19,2},{20,5},{21,4},{22,7},{23,6},{24,9},{25... | collective-permute-start | bytes 786440 | tf_op jit(solution)/shard_map/ppermute | solution.py:142
  205.7 29.5 %collective-permute-start.19 = (bf16[32,4096]{1,0:T(8,128)(2,1)S(1)}, bf16[32,4096]{1,0:T(8,128)(2,1)S(1)}, u32[]{:S(2)}, u32[]{:S(2)}) collective-permute-start(bf16[32,4096]{1,0:T(8,128)(2,1)S(1)} %fusion.8.refs_4_), channel_id=1, source_target_pairs={{0,3},{1,2},{2,1},{3,0},{4,7},{5,6},{6,5},{7,4},{8,11},{9,10},{10,... | collective-permute-start | bytes 786440 | tf_op jit(solution)/shard_map/ppermute | solution.py:142
  235.2 30.6 %collective-permute-start.64 = (bf16[32,4096]{1,0:T(8,128)(2,1)S(1)}, bf16[32,4096]{1,0:T(8,128)(2,1)S(1)}, u32[]{:S(2)}, u32[]{:S(2)}) collective-permute-start(bf16[32,4096]{1,0:T(8,128)(2,1)S(1)} %fusion.20.refs_4_), channel_id=1, source_target_pairs={{0,1},{1,0},{2,3},{3,2},{4,5},{5,4},{6,7},{7,6},{8,9},{9,8},{10,11... | collective-permute-start | bytes 786440 | tf_op jit(solution)/shard_map/ppermute | solution.py:142
  244.7 32.9 %collective-permute-start.66 = (bf16[32,4096]{1,0:T(8,128)(2,1)S(1)}, bf16[32,4096]{1,0:T(8,128)(2,1)S(1)}, u32[]{:S(2)}, u32[]{:S(2)}) collective-permute-start(bf16[32,4096]{1,0:T(8,128)(2,1)S(1)} %fusion.20.refs_4_), channel_id=1, source_target_pairs={{0,3},{1,2},{2,1},{3,0},{4,7},{5,6},{6,5},{7,4},{8,11},{9,10},{10,... | collective-permute-start | bytes 786440 | tf_op jit(solution)/shard_map/ppermute | solution.py:142
  248.7 32.9 %collective-permute-start.67 = (bf16[32,4096]{1,0:T(8,128)(2,1)S(1)}, bf16[32,4096]{1,0:T(8,128)(2,1)S(1)}, u32[]{:S(2)}, u32[]{:S(2)}) collective-permute-start(bf16[32,4096]{1,0:T(8,128)(2,1)S(1)} %fusion.20.refs_4_), channel_id=1, source_target_pairs={{16,3},{17,2},{18,1},{19,0},{20,7},{21,6},{22,5},{23,4},{24,11},{2... | collective-permute-start | bytes 786440 | tf_op jit(solution)/shard_map/ppermute | solution.py:142
  250.0 31.6 %collective-permute-start.68 = (bf16[32,4096]{1,0:T(8,128)(2,1)S(1)}, bf16[32,4096]{1,0:T(8,128)(2,1)S(1)}, u32[]{:S(2)}, u32[]{:S(2)}) collective-permute-start(bf16[32,4096]{1,0:T(8,128)(2,1)S(1)} %fusion.20.refs_4_), channel_id=1, source_target_pairs={{16,0},{17,1},{18,2},{19,3},{20,4},{21,5},{22,6},{23,7},{24,8},{25... | collective-permute-start | bytes 786440 | tf_op jit(solution)/shard_map/ppermute | solution.py:142
  304.3 34.0 %collective-permute-start.71 = (bf16[128,4096]{1,0:T(8,128)(2,1)S(1)}, bf16[128,4096]{1,0:T(8,128)(2,1)S(1)}, u32[]{:S(2)}, u32[]{:S(2)}) collective-permute-start(bf16[128,4096]{1,0:T(8,128)(2,1)S(1)} %get-tuple-element.94), channel_id=1, source_target_pairs={{0,1},{1,0},{2,3},{3,2},{4,5},{5,4},{6,7},{7,6},{8,9},{9,8},{10,11... | collective-permute-start | bytes 3145736 | tf_op jit(solution)/shard_map/ppermute | solution.py:142
  376.0 33.4 %collective-permute-start.75 = (bf16[32,4096]{1,0:T(8,128)(2,1)S(1)}, bf16[32,4096]{1,0:T(8,128)(2,1)S(1)}, u32[]{:S(2)}, u32[]{:S(2)}) collective-permute-start(bf16[32,4096]{1,0:T(8,128)(2,1)S(1)} %fusion.24.refs_5_), channel_id=1, source_target_pairs={{0,17},{1,16},{2,19},{3,18},{4,21},{5,20},{6,23},{7,22},{8,25},{9,... | collective-permute-start | bytes 786440 | tf_op jit(solution)/shard_map/ppermute | solution.py:142
  380.4 34.6 %collective-permute-start.76 = (bf16[32,4096]{1,0:T(8,128)(2,1)S(1)}, bf16[32,4096]{1,0:T(8,128)(2,1)S(1)}, u32[]{:S(2)}, u32[]{:S(2)}) collective-permute-start(bf16[32,4096]{1,0:T(8,128)(2,1)S(1)} %fusion.24.refs_5_), channel_id=1, source_target_pairs={{16,17},{17,16},{18,19},{19,18},{20,21},{21,20},{22,23},{23,22},{2... | collective-permute-start | bytes 786440 | tf_op jit(solution)/shard_map/ppermute | solution.py:142
  381.0 40.1 %collective-permute-start.77 = (bf16[32,4096]{1,0:T(8,128)(2,1)S(1)}, bf16[32,4096]{1,0:T(8,128)(2,1)S(1)}, u32[]{:S(2)}, u32[]{:S(2)}) collective-permute-start(bf16[32,4096]{1,0:T(8,128)(2,1)S(1)} %fusion.24.refs_5_), channel_id=1, source_target_pairs={{0,19},{1,18},{2,17},{3,16},{4,23},{5,22},{6,21},{7,20},{8,27},{9,... | collective-permute-start | bytes 786440 | tf_op jit(solution)/shard_map/ppermute | solution.py:142
  385.6 37.9 %collective-permute-start.78 = (bf16[32,4096]{1,0:T(8,128)(2,1)S(1)}, bf16[32,4096]{1,0:T(8,128)(2,1)S(1)}, u32[]{:S(2)}, u32[]{:S(2)}) collective-permute-start(bf16[32,4096]{1,0:T(8,128)(2,1)S(1)} %fusion.24.refs_5_), channel_id=1, source_target_pairs={{16,19},{17,18},{18,17},{19,16},{20,23},{21,22},{22,21},{23,20},{2... | collective-permute-start | bytes 786440 | tf_op jit(solution)/shard_map/ppermute | solution.py:142
  386.3 37.2 %collective-permute-start.79 = (bf16[32,4096]{1,0:T(8,128)(2,1)S(1)}, bf16[32,4096]{1,0:T(8,128)(2,1)S(1)}, u32[]{:S(2)}, u32[]{:S(2)}) collective-permute-start(bf16[32,4096]{1,0:T(8,128)(2,1)S(1)} %fusion.24.refs_5_), channel_id=1, source_target_pairs={{0,16},{1,17},{2,18},{3,19},{4,20},{5,21},{6,22},{7,23},{8,24},{9,... | collective-permute-start | bytes 786440 | tf_op jit(solution)/shard_map/ppermute | solution.py:142
  441.6 29.9 %collective-permute-start.82 = (bf16[128,4096]{1,0:T(8,128)(2,1)S(1)}, bf16[128,4096]{1,0:T(8,128)(2,1)}, u32[]{:S(2)}, u32[]{:S(2)}) collective-permute-start(bf16[128,4096]{1,0:T(8,128)(2,1)S(1)} %get-tuple-element.102), channel_id=1, source_target_pairs={{16,17},{17,16},{18,19},{19,18},{20,21},{21,20},{22,23},{23,22},{2... | collective-permute-start | bytes 3145736 | tf_op jit(solution)/shard_map/ppermute | solution.py:142
  474.2 41.0 %collective-permute-start.84 = (bf16[32,4096]{1,0:T(8,128)(2,1)S(1)}, bf16[32,4096]{1,0:T(8,128)(2,1)S(1)}, u32[]{:S(2)}, u32[]{:S(2)}) collective-permute-start(bf16[32,4096]{1,0:T(8,128)(2,1)S(1)} %get-tuple-element.141), channel_id=1, source_target_pairs={{16,2},{17,3},{18,0},{19,1},{20,6},{21,7},{22,4},{23,5},{24,10},{2... | collective-permute-start | bytes 786440 | tf_op jit(solution)/shard_map/ppermute | solution.py:142
  475.5 41.0 %collective-permute-start.85 = (bf16[32,4096]{1,0:T(8,128)(2,1)S(1)}, bf16[32,4096]{1,0:T(8,128)(2,1)S(1)}, u32[]{:S(2)}, u32[]{:S(2)}) collective-permute-start(bf16[32,4096]{1,0:T(8,128)(2,1)S(1)} %get-tuple-element.140), channel_id=1, source_target_pairs={{16,18},{17,19},{18,16},{19,17},{20,22},{21,23},{22,20},{23,21},{2... | collective-permute-start | bytes 786440 | tf_op jit(solution)/shard_map/ppermute | solution.py:142
  476.3 42.3 %collective-permute-start.39 = (bf16[32,4096]{1,0:T(8,128)(2,1)S(1)}, bf16[32,4096]{1,0:T(8,128)(2,1)S(1)}, u32[]{:S(2)}, u32[]{:S(2)}) collective-permute-start(bf16[32,4096]{1,0:T(8,128)(2,1)S(1)} %fusion.16.refs_3_), channel_id=1, source_target_pairs={{0,19},{1,18},{2,17},{3,16},{4,23},{5,22},{6,21},{7,20},{8,27},{9,... | collective-permute-start | bytes 786440 | tf_op jit(solution)/shard_map/ppermute | solution.py:142
  498.1 30.6 %collective-permute-start.40 = (bf16[32,4096]{1,0:T(8,128)(2,1)S(1)}, bf16[32,4096]{1,0:T(8,128)(2,1)S(1)}, u32[]{:S(2)}, u32[]{:S(2)}) collective-permute-start(bf16[32,4096]{1,0:T(8,128)(2,1)S(1)} %fusion.16.refs_3_), channel_id=1, source_target_pairs={{16,19},{17,18},{18,17},{19,16},{20,23},{21,22},{22,21},{23,20},{2... | collective-permute-start | bytes 786440 | tf_op jit(solution)/shard_map/ppermute | solution.py:142
  498.8 30.7 %collective-permute-start.41 = (bf16[32,4096]{1,0:T(8,128)(2,1)S(1)}, bf16[32,4096]{1,0:T(8,128)(2,1)S(1)}, u32[]{:S(2)}, u32[]{:S(2)}) collective-permute-start(bf16[32,4096]{1,0:T(8,128)(2,1)S(1)} %fusion.16.refs_3_), channel_id=1, source_target_pairs={{0,16},{1,17},{2,18},{3,19},{4,20},{5,21},{6,22},{7,23},{8,24},{9,... | collective-permute-start | bytes 786440 | tf_op jit(solution)/shard_map/ppermute | solution.py:142
  533.9 33.9 %collective-permute-start.87 = (bf16[32,4096]{1,0:T(8,128)(2,1)S(1)}, bf16[32,4096]{1,0:T(8,128)(2,1)S(1)}, u32[]{:S(2)}, u32[]{:S(2)}) collective-permute-start(bf16[32,4096]{1,0:T(8,128)(2,1)S(1)} %fusion.28.refs_3_), channel_id=1, source_target_pairs={{16,19},{17,18},{18,17},{19,16},{20,23},{21,22},{22,21},{23,20},{2... | collective-permute-start | bytes 786440 | tf_op jit(solution)/shard_map/ppermute | solution.py:142
  534.6 42.2 %collective-permute-start.88 = (bf16[32,4096]{1,0:T(8,128)(2,1)S(1)}, bf16[32,4096]{1,0:T(8,128)(2,1)S(1)}, u32[]{:S(2)}, u32[]{:S(2)}) collective-permute-start(bf16[32,4096]{1,0:T(8,128)(2,1)S(1)} %fusion.28.refs_3_), channel_id=1, source_target_pairs={{0,16},{1,17},{2,18},{3,19},{4,20},{5,21},{6,22},{7,23},{8,24},{9,... | collective-permute-start | bytes 786440 | tf_op jit(solution)/shard_map/ppermute | solution.py:142
  537.7 39.8 %collective-permute-start.89 = (bf16[32,4096]{1,0:T(8,128)(2,1)S(1)}, bf16[32,4096]{1,0:T(8,128)(2,1)S(1)}, u32[]{:S(2)}, u32[]{:S(2)}) collective-permute-start(bf16[32,4096]{1,0:T(8,128)(2,1)S(1)} %fusion.28.refs_3_), channel_id=1, source_target_pairs={{0,17},{1,16},{2,19},{3,18},{4,21},{5,20},{6,23},{7,22},{8,25},{9,... | collective-permute-start | bytes 786440 | tf_op jit(solution)/shard_map/ppermute | solution.py:142
  540.4 37.8 %collective-permute-start.90 = (bf16[32,4096]{1,0:T(8,128)(2,1)S(1)}, bf16[32,4096]{1,0:T(8,128)(2,1)S(1)}, u32[]{:S(2)}, u32[]{:S(2)}) collective-permute-start(bf16[32,4096]{1,0:T(8,128)(2,1)S(1)} %fusion.28.refs_3_), channel_id=1, source_target_pairs={{16,17},{17,16},{18,19},{19,18},{20,21},{21,20},{22,23},{23,22},{2... | collective-permute-start | bytes 786440 | tf_op jit(solution)/shard_map/ppermute | solution.py:142
  605.1 33.2 %collective-permute-start.50 = (bf16[32,4096]{1,0:T(8,128)(2,1)S(1)}, bf16[32,4096]{1,0:T(8,128)(2,1)S(1)}, u32[]{:S(2)}, u32[]{:S(2)}) collective-permute-start(bf16[32,4096]{1,0:T(8,128)(2,1)S(1)} %get-tuple-element.164), channel_id=1, source_target_pairs={{16,2},{17,3},{18,0},{19,1},{20,6},{21,7},{22,4},{23,5},{24,10},{2... | collective-permute-start | bytes 786440 | tf_op jit(solution)/shard_map/ppermute | solution.py:142
  606.5 33.4 %collective-permute-start.95 = (bf16[32,4096]{1,0:T(8,128)(2,1)S(1)}, bf16[32,4096]{1,0:T(8,128)(2,1)S(1)}, u32[]{:S(2)}, u32[]{:S(2)}) collective-permute-start(bf16[32,4096]{1,0:T(8,128)(2,1)S(1)} %get-tuple-element.112), channel_id=1, source_target_pairs={{16,17},{17,16},{18,19},{19,18},{20,21},{21,20},{22,23},{23,22},{2... | collective-permute-start | bytes 786440 | tf_op jit(solution)/shard_map/ppermute | solution.py:142
  607.2 43.7 %collective-permute-start.94 = (bf16[32,4096]{1,0:T(8,128)(2,1)S(1)}, bf16[32,4096]{1,0:T(8,128)(2,1)S(1)}, u32[]{:S(2)}, u32[]{:S(2)}) collective-permute-start(bf16[32,4096]{1,0:T(8,128)(2,1)S(1)} %get-tuple-element.111), channel_id=1, source_target_pairs={{16,1},{17,0},{18,3},{19,2},{20,5},{21,4},{22,7},{23,6},{24,9},{25... | collective-permute-start | bytes 786440 | tf_op jit(solution)/shard_map/ppermute | solution.py:142
  608.5 42.3 %collective-permute-start.93 = (bf16[32,4096]{1,0:T(8,128)(2,1)S(1)}, bf16[32,4096]{1,0:T(8,128)(2,1)S(1)}, u32[]{:S(2)}, u32[]{:S(2)}) collective-permute-start(bf16[32,4096]{1,0:T(8,128)(2,1)S(1)} %get-tuple-element.110), channel_id=1, source_target_pairs={{16,0},{17,1},{18,2},{19,3},{20,4},{21,5},{22,6},{23,7},{24,8},{25... | collective-permute-start | bytes 786440 | tf_op jit(solution)/shard_map/ppermute | solution.py:142
  609.8 41.0 %collective-permute-start.98 = (bf16[32,4096]{1,0:T(8,128)(2,1)S(1)}, bf16[32,4096]{1,0:T(8,128)(2,1)S(1)}, u32[]{:S(2)}, u32[]{:S(2)}) collective-permute-start(bf16[32,4096]{1,0:T(8,128)(2,1)S(1)} %get-tuple-element.163), channel_id=1, source_target_pairs={{16,18},{17,19},{18,16},{19,17},{20,22},{21,23},{22,20},{23,21},{2... | collective-permute-start | bytes 786440 | tf_op jit(solution)/shard_map/ppermute | solution.py:142
  (92 other events, 1683.2 us)

commit v6 on v4

--- a/solution.py
+++ b/solution.py
@@ -299,12 +299,14 @@
             mine = jnp.where(section == h, send(own[h], 0, h, 0), mine)
         return pieces, mine
 
-    def compute(half, pieces):
+    def compute(half, pieces, ready):
         if half % 2:
             inner = inward(gate_kernel, "gate", (), (w_gate, w_up), pieces)
+            inner = after(inner, ready) if ready else inner
             return outward("down", inner, w_down, cuts)
         weights = (w_query, w_key, w_value)
         inner = inward(attention_kernel, "attention", tables, weights, pieces)
+        inner = after(inner, ready) if ready else inner
         return outward("out", inner, w_out, cuts)
 
     def add(base, sums):
@@ -328,7 +330,7 @@
                 hidden[c] = add(hidden[c], sum_arrived(nearby[c], arrived[c], (half - 1) // 2))
                 normed = rms_norm(hidden[c], gains[half])
                 pieces = gather_rows(normed, half // 2)
-            partial = compute(half, pieces)
+            partial = compute(half, pieces, [hidden[c]] if half == 0 else [])
             nearby[c] = sum_nearby(partial, half // 2)
             arrived[c] = send_to_owners(nearby[c], half // 2)
     for c in range(per_device):

time: 683 us -> 691 us (1.012)
  waiting for transfers between devices: 192 us -> 199 us
    ppermute x90, waiting for transfers between devices: 187 us -> 194 us  [send(): return lax.ppermute(value, BOTH, links)]
  transfers between devices with their start and end apart: 103 -> 103, of which waited for: 24 -> 27; matrix products, arithmetic and copies ran while one was open for 6% -> 6% of each run, Pallas kernels for 26% -> 25%
where the time goes in v6:
time: 691 us; the launch traced here: 679 us
  starting transfers between devices  249 us (36%)
  waiting for transfers between devices  199 us (29%)
  Pallas kernels  177 us (26%)
  local copies, waits for them, and re-layouts  25.4 us (4%)
  other arithmetic  22.9 us (3%)
    ppermute x90, starting transfers between devices, send(): return lax.ppermute(value, BOTH, links)  234 us
    ppermute x90, waiting for transfers between devices, send(): return lax.ppermute(value, BOTH, links)  194 us
    pallas_call x8, Pallas kernels, inward(): pl.pallas_call(functools.partial(kernel, len(pieces)), out_shape=jax.Shap...  120 us
    pallas_call x8, Pallas kernels, outward(): pl.pallas_call(down_kernel, out_shape=[jax.ShapeDtypeStruct((rows, width)...  56.9 us
    gather x2, local copies, waits for them, and re-layouts, body(): jnp.take(embed_table, tokens[c], axis=0)  18 us
  transfers between devices with their start and end apart: 103, of which 27 were waited for; matrix products, arithmetic and copies ran while one was open for 6% of the time, Pallas kernels for 25%

profile of v6, /device:TPU:0, one launch (start us, length us, event | category | flops | bytes accessed | tf_op | source)
XLA Modules:
  0.0 679.2 jit_solution(1209478846576555133)
XLA Ops:
  15.2 9.0 %gather_fusion.5 = bf16[256,512]{1,0:T(8,128)(2,1)S(1)} fusion(bf16[16000,512]{1,0:T(8,128)(2,1)} %param.25, s32[1024]{0:T(1024)S(1)} %pad_clamp_fusion.2), kind=kCustom, calls=%fused_computation.1.clone | custom fusion | bytes 525312 | tf_op jit(solution)/shard_map/jit(_take)/gather | solution.py:317
  35.2 9.0 %gather_fusion.6 = bf16[256,512]{1,0:T(8,128)(2,1)S(1)} fusion(bf16[16000,512]{1,0:T(8,128)(2,1)} %param.25, s32[1024]{0:T(1024)S(1)} %pad_clamp_fusion), kind=kCustom, calls=%fused_computation.3.clone | custom fusion | bytes 525312 | tf_op jit(solution)/shard_map/jit(_take)/gather | solution.py:317
  58.4 17.1 %collective-permute-done.8 = bf16[256,512]{1,0:T(8,128)(2,1)S(1)} collective-permute-done((bf16[256,512]{1,0:T(8,128)(2,1)}, bf16[256,512]{1,0:T(8,128)(2,1)S(1)}, u32[]{:S(2)}, u32[]{:S(2)}) %collective-permute-start.8) | collective-permute-done | bytes 262176 | tf_op jit(solution)/shard_map/ppermute | solution.py:142
  90.8 13.9 %attention.4.x_ref = bf16[256,1024]{1,0:T(8,128)(2,1)S(1)} custom-call(f32[256,128]{1,0:T(8,128)S(1)} %bitcast.75, f32[256,128]{1,0:T(8,128)S(1)} %bitcast.79, s32[256,1]{1,0:T(8,128)S(1)} %add.571.row_ref, s32[1,256]{1,0:T(1,128)S(1)} %add.468.col_ref, bf16[1,4096,1024]{2,1,0:T(8,128)(2,1)} %wq_ref.7, bf16[1,4096,1024]{2,1,0:T(8,128)(2,1)} %wk_ref.7, ...), custom_call_target="tpu_custom_call" | custom-call | flops 6442450944 | bytes 29360128 | tf_op jit(solution)/shard_map/attention/pallas_call | solution.py:108
  107.5 7.7 %collective-permute-start.10 = (bf16[32,4096]{1,0:T(8,128)(2,1)S(1)}, bf16[32,4096]{1,0:T(8,128)(2,1)S(1)}, u32[]{:S(2)}, u32[]{:S(2)}) collective-permute-start(bf16[32,4096]{1,0:T(8,128)(2,1)S(1)} %constant_dynamic-slice_fusion.9), channel_id=1, source_target_pairs={{0,16},{1,17},{2,18},{3,19},{4,20},{5,21},{6,22},{7,23},{8,24},{9,... | collective-permute-start | bytes 786440 | tf_op jit(solution)/shard_map/ppermute | solution.py:142
  137.8 13.9 %attention.6.x_ref = bf16[256,1024]{1,0:T(8,128)(2,1)S(1)} custom-call(f32[256,128]{1,0:T(8,128)S(1)} %bitcast.76, f32[256,128]{1,0:T(8,128)S(1)} %bitcast.80, s32[256,1]{1,0:T(8,128)S(1)} %add.571.row_ref, s32[1,256]{1,0:T(1,128)S(1)} %add.468.col_ref, bf16[1,4096,1024]{2,1,0:T(8,128)(2,1)} %wq_ref.7, bf16[1,4096,1024]{2,1,0:T(8,128)(2,1)} %wk_ref.7, ...), custom_call_target="tpu_custom_call" | custom-call | flops 6442450944 | bytes 29360128 | tf_op jit(solution)/shard_map/attention/pallas_call | solution.py:108
  168.3 6.8 collective-permute-done.15
  175.1 15.5 %collective-permute-done.14 = bf16[32,4096]{1,0:T(8,128)(2,1)} collective-permute-done((bf16[32,4096]{1,0:T(8,128)(2,1)}, bf16[32,4096]{1,0:T(8,128)(2,1)}, u32[]{:S(2)}, u32[]{:S(2)}) %collective-permute-start.14) | collective-permute-done | bytes 262176 | tf_op jit(solution)/shard_map/ppermute | solution.py:142
  209.2 11.3 %collective-permute-done.59 = bf16[32,4096]{1,0:T(8,128)(2,1)S(1)} collective-permute-done((bf16[32,4096]{1,0:T(8,128)(2,1)S(1)}, bf16[32,4096]{1,0:T(8,128)(2,1)S(1)}, u32[]{:S(2)}, u32[]{:S(2)}) %collective-permute-start.59) | collective-permute-done | bytes 262176 | tf_op jit(solution)/shard_map/ppermute | solution.py:142
  228.3 11.4 %collective-permute-start.22 = (bf16[32,4096]{1,0:T(8,128)(2,1)S(1)}, bf16[32,4096]{1,0:T(8,128)(2,1)S(1)}, u32[]{:S(2)}, u32[]{:S(2)}) collective-permute-start(bf16[32,4096]{1,0:T(8,128)(2,1)S(1)} %fusion.8.refs_4_), channel_id=1, source_target_pairs={{0,2},{1,3},{2,0},{3,1},{4,6},{5,7},{6,4},{7,5},{8,10},{9,11},{10,... | collective-permute-start | bytes 786440 | tf_op jit(solution)/shard_map/ppermute | solution.py:142
  245.1 6.7 collective-permute-start.64
  260.0 16.1 %gate.4.x_ref = bf16[256,2048]{1,0:T(8,128)(2,1)S(1)} custom-call(bf16[1,4096,2048]{2,1,0:T(8,128)(2,1)} %wg_ref.7, bf16[1,4096,2048]{2,1,0:T(8,128)(2,1)} %wu_ref.7, bf16[32,4096]{1,0:T(8,128)(2,1)S(1)} %collective-permute-done.17.refs_0_, bf16[32,4096]{1,0:T(8,128)(2,1)S(1)} %collective-permute-done.18.refs_1_, ...), custom_call_target="tpu_custom_call" | custom-call | flops 8589934592 | bytes 37748736 | tf_op jit(solution)/shard_map/gate/pallas_call | solution.py:108
  280.3 8.5 %down.4 = (bf16[128,4096]{1,0:T(8,128)(2,1)S(1)}, bf16[32,4096]{1,0:T(8,128)(2,1)S(1)}, bf16[32,4096]{1,0:T(8,128)(2,1)S(1)}, bf16[32,4096]{1,0:T(8,128)(2,1)S(1)}, bf16[32,4096]{1,0:T(8,128)(2,1)S(1)}) custom-call(bf16[256,2048]{1,0:T(8,128)(2,1)S(1)} %gate.4.x_ref, bf16[1,2048,4096]{2,1,0:T(8,128)(2,1)} %w_ref.15), custom_call_target="tpu_custom_call" | custom-call | flops 4294967296 | bytes 20971520 | tf_op jit(solution)/shard_map/down/pallas_call | solution.py:127
  293.6 16.1 %gate.6.x_ref = bf16[256,2048]{1,0:T(8,128)(2,1)S(1)} custom-call(bf16[1,4096,2048]{2,1,0:T(8,128)(2,1)} %wg_ref.7, bf16[1,4096,2048]{2,1,0:T(8,128)(2,1)} %wu_ref.7, bf16[32,4096]{1,0:T(8,128)(2,1)S(1)} %collective-permute-done.62.refs_0_, bf16[32,4096]{1,0:T(8,128)(2,1)S(1)} %collective-permute-done.63.refs_1_, ...), custom_call_target="tpu_custom_call" | custom-call | flops 8589934592 | bytes 37748736 | tf_op jit(solution)/shard_map/gate/pallas_call | solution.py:108
  309.7 8.5 %down.6 = (bf16[128,4096]{1,0:T(8,128)(2,1)S(1)}, bf16[32,4096]{1,0:T(8,128)(2,1)S(1)}, bf16[32,4096]{1,0:T(8,128)(2,1)S(1)}, bf16[32,4096]{1,0:T(8,128)(2,1)S(1)}, bf16[32,4096]{1,0:T(8,128)(2,1)S(1)}) custom-call(bf16[256,2048]{1,0:T(8,128)(2,1)S(1)} %gate.6.x_ref, bf16[1,2048,4096]{2,1,0:T(8,128)(2,1)} %w_ref.15), custom_call_target="tpu_custom_call" | custom-call | flops 4294967296 | bytes 20971520 | tf_op jit(solution)/shard_map/down/pallas_call | solution.py:127
  326.6 13.5 %collective-permute-done.26 = bf16[32,4096]{1,0:T(8,128)(2,1)S(1)} collective-permute-done((bf16[32,4096]{1,0:T(8,128)(2,1)S(1)}, bf16[32,4096]{1,0:T(8,128)(2,1)S(1)}, u32[]{:S(2)}, u32[]{:S(2)}) %collective-permute-start.26) | collective-permute-done | bytes 262176 | tf_op jit(solution)/shard_map/ppermute | solution.py:142
  353.6 9.2 %collective-permute-done.70 = bf16[32,4096]{1,0:T(8,128)(2,1)S(1)} collective-permute-done((bf16[32,4096]{1,0:T(8,128)(2,1)S(1)}, bf16[32,4096]{1,0:T(8,128)(2,1)S(1)}, u32[]{:S(2)}, u32[]{:S(2)}) %collective-permute-start.70) | collective-permute-done | bytes 262176 | tf_op jit(solution)/shard_map/ppermute | solution.py:142
  364.8 17.1 %collective-permute-start.32 = (bf16[32,4096]{1,0:T(8,128)(2,1)S(1)}, bf16[32,4096]{1,0:T(8,128)(2,1)S(1)}, u32[]{:S(2)}, u32[]{:S(2)}) collective-permute-start(bf16[32,4096]{1,0:T(8,128)(2,1)S(1)} %fusion.12.refs_5_), channel_id=1, source_target_pairs={{0,16},{1,17},{2,18},{3,19},{4,20},{5,21},{6,22},{7,23},{8,24},{9,... | collective-permute-start | bytes 786440 | tf_op jit(solution)/shard_map/ppermute | solution.py:142
  389.0 10.7 %collective-permute-done.32.refs_4_ = bf16[32,4096]{1,0:T(8,128)(2,1)S(1)} collective-permute-done((bf16[32,4096]{1,0:T(8,128)(2,1)S(1)}, bf16[32,4096]{1,0:T(8,128)(2,1)S(1)}, u32[]{:S(2)}, u32[]{:S(2)}) %collective-permute-start.32) | collective-permute-done | bytes 262176 | tf_op jit(solution)/shard_map/ppermute | solution.py:142
  410.1 13.9 %attention.5.x_ref = bf16[256,1024]{1,0:T(8,128)(2,1)S(1)} custom-call(f32[256,128]{1,0:T(8,128)S(1)} %bitcast.77, f32[256,128]{1,0:T(8,128)S(1)} %bitcast.81, s32[256,1]{1,0:T(8,128)S(1)} %add.571.row_ref, s32[1,256]{1,0:T(1,128)S(1)} %add.468.col_ref, bf16[1,4096,1024]{2,1,0:T(8,128)(2,1)} %wq_ref.7, bf16[1,4096,1024]{2,1,0:T(8,128)(2,1)} %wk_ref.7, ...), custom_call_target="tpu_custom_call" | custom-call | flops 6442450944 | bytes 29360128 | tf_op jit(solution)/shard_map/attention/pallas_call | solution.py:108
  434.7 13.9 %attention.7.x_ref = bf16[256,1024]{1,0:T(8,128)(2,1)S(1)} custom-call(f32[256,128]{1,0:T(8,128)S(1)} %bitcast.78, f32[256,128]{1,0:T(8,128)S(1)} %bitcast.82, s32[256,1]{1,0:T(8,128)S(1)} %add.571.row_ref, s32[1,256]{1,0:T(1,128)S(1)} %add.468.col_ref, bf16[1,4096,1024]{2,1,0:T(8,128)(2,1)} %wq_ref.7, bf16[1,4096,1024]{2,1,0:T(8,128)(2,1)} %wk_ref.7, ...), custom_call_target="tpu_custom_call" | custom-call | flops 6442450944 | bytes 29360128 | tf_op jit(solution)/shard_map/attention/pallas_call | solution.py:108
  467.5 12.2 %collective-permute-done.36 = bf16[32,4096]{1,0:T(8,128)(2,1)S(1)} collective-permute-done((bf16[32,4096]{1,0:T(8,128)(2,1)}, bf16[32,4096]{1,0:T(8,128)(2,1)S(1)}, u32[]{:S(2)}, u32[]{:S(2)}) %collective-permute-start.36) | collective-permute-done | bytes 262176 | tf_op jit(solution)/shard_map/ppermute | solution.py:142
  485.8 16.3 %collective-permute-start.39 = (bf16[32,4096]{1,0:T(8,128)(2,1)S(1)}, bf16[32,4096]{1,0:T(8,128)(2,1)S(1)}, u32[]{:S(2)}, u32[]{:S(2)}) collective-permute-start(bf16[32,4096]{1,0:T(8,128)(2,1)S(1)} %fusion.16.refs_5_), channel_id=1, source_target_pairs={{0,17},{1,16},{2,19},{3,18},{4,21},{5,20},{6,23},{7,22},{8,25},{9,... | collective-permute-start | bytes 786440 | tf_op jit(solution)/shard_map/ppermute | solution.py:142
  508.8 8.6 %collective-permute-start.43 = (bf16[32,4096]{1,0:T(8,128)(2,1)S(1)}, bf16[32,4096]{1,0:T(8,128)(2,1)S(1)}, u32[]{:S(2)}, u32[]{:S(2)}) collective-permute-start(bf16[32,4096]{1,0:T(8,128)(2,1)S(1)} %fusion.16.refs_5_), channel_id=1, source_target_pairs={{0,16},{1,17},{2,18},{3,19},{4,20},{5,21},{6,22},{7,23},{8,24},{9,... | collective-permute-start | bytes 786440 | tf_op jit(solution)/shard_map/ppermute | solution.py:142
  525.2 12.2 %collective-permute-start.86 = (bf16[32,4096]{1,0:T(8,128)(2,1)S(1)}, bf16[32,4096]{1,0:T(8,128)(2,1)S(1)}, u32[]{:S(2)}, u32[]{:S(2)}) collective-permute-start(bf16[32,4096]{1,0:T(8,128)(2,1)S(1)} %fusion.28.refs_5_), channel_id=1, source_target_pairs={{0,19},{1,18},{2,17},{3,16},{4,23},{5,22},{6,21},{7,20},{8,27},{9,... | collective-permute-start | bytes 786440 | tf_op jit(solution)/shard_map/ppermute | solution.py:142
  541.1 16.1 %gate.5.x_ref = bf16[256,2048]{1,0:T(8,128)(2,1)S(1)} custom-call(bf16[1,4096,2048]{2,1,0:T(8,128)(2,1)} %wg_ref.7, bf16[1,4096,2048]{2,1,0:T(8,128)(2,1)} %wu_ref.7, bf16[32,4096]{1,0:T(8,128)(2,1)S(1)} %collective-permute-done.39.refs_0_, bf16[32,4096]{1,0:T(8,128)(2,1)S(1)} %collective-permute-done.40.refs_1_, ...), custom_call_target="tpu_custom_call" | custom-call | flops 8589934592 | bytes 37748736 | tf_op jit(solution)/shard_map/gate/pallas_call | solution.py:108
  559.5 8.5 %down.5 = (bf16[128,4096]{1,0:T(8,128)(2,1)S(1)}, bf16[32,4096]{1,0:T(8,128)(2,1)S(1)}, bf16[32,4096]{1,0:T(8,128)(2,1)S(1)}, bf16[32,4096]{1,0:T(8,128)(2,1)S(1)}, bf16[32,4096]{1,0:T(8,128)(2,1)S(1)}) custom-call(bf16[256,2048]{1,0:T(8,128)(2,1)S(1)} %gate.5.x_ref, bf16[1,2048,4096]{2,1,0:T(8,128)(2,1)} %w_ref.15), custom_call_target="tpu_custom_call" | custom-call | flops 4294967296 | bytes 20971520 | tf_op jit(solution)/shard_map/down/pallas_call | solution.py:127
  568.8 16.1 %gate.7.x_ref = bf16[256,2048]{1,0:T(8,128)(2,1)S(1)} custom-call(bf16[1,4096,2048]{2,1,0:T(8,128)(2,1)} %wg_ref.7, bf16[1,4096,2048]{2,1,0:T(8,128)(2,1)} %wu_ref.7, bf16[32,4096]{1,0:T(8,128)(2,1)S(1)} %collective-permute-done.84.refs_0_, bf16[32,4096]{1,0:T(8,128)(2,1)S(1)} %collective-permute-done.85.refs_1_, ...), custom_call_target="tpu_custom_call" | custom-call | flops 8589934592 | bytes 37748736 | tf_op jit(solution)/shard_map/gate/pallas_call | solution.py:108
  584.9 8.5 %down.7 = (bf16[128,4096]{1,0:T(8,128)(2,1)S(1)}, bf16[32,4096]{1,0:T(8,128)(2,1)S(1)}, bf16[32,4096]{1,0:T(8,128)(2,1)S(1)}, bf16[32,4096]{1,0:T(8,128)(2,1)S(1)}, bf16[32,4096]{1,0:T(8,128)(2,1)S(1)}) custom-call(bf16[256,2048]{1,0:T(8,128)(2,1)S(1)} %gate.7.x_ref, bf16[1,2048,4096]{2,1,0:T(8,128)(2,1)} %w_ref.15), custom_call_target="tpu_custom_call" | custom-call | flops 4294967296 | bytes 20971520 | tf_op jit(solution)/shard_map/down/pallas_call | solution.py:127
  607.8 8.4 %collective-permute-done.47 = bf16[32,4096]{1,0:T(8,128)(2,1)S(1)} collective-permute-done((bf16[32,4096]{1,0:T(8,128)(2,1)S(1)}, bf16[32,4096]{1,0:T(8,128)(2,1)S(1)}, u32[]{:S(2)}, u32[]{:S(2)}) %collective-permute-start.47) | collective-permute-done | bytes 262176 | tf_op jit(solution)/shard_map/ppermute | solution.py:142
  616.5 23.6 %collective-permute-done.94 = bf16[32,4096]{1,0:T(8,128)(2,1)S(1)} collective-permute-done((bf16[32,4096]{1,0:T(8,128)(2,1)S(1)}, bf16[32,4096]{1,0:T(8,128)(2,1)S(1)}, u32[]{:S(2)}, u32[]{:S(2)}) %collective-permute-start.94) | collective-permute-done | bytes 262176 | tf_op jit(solution)/shard_map/ppermute | solution.py:142
  640.1 19.7 %collective-permute-done.92 = bf16[32,4096]{1,0:T(8,128)(2,1)S(1)} collective-permute-done((bf16[32,4096]{1,0:T(8,128)(2,1)S(1)}, bf16[32,4096]{1,0:T(8,128)(2,1)S(1)}, u32[]{:S(2)}, u32[]{:S(2)}) %collective-permute-start.92) | collective-permute-done | bytes 262176 | tf_op jit(solution)/shard_map/ppermute | solution.py:142
  (329 shorter events, 273.8 us)
Async XLA Ops:
  3.9 40.4 %collective-permute-start.16 = (bf16[1,4096]{1,0:T(2,128)(2,1)}, bf16[1,4096]{1,0:T(2,128)(2,1)S(1)}, u32[]{:S(2)}, u32[]{:S(2)}) collective-permute-start(bf16[1,4096]{1,0:T(2,128)(2,1)} %param.31), channel_id=1, source_target_pairs={{0,16},{16,0},{1,17},{17,1},{2,18},{18,2},{3,19},{19,3},{4,20},{20... | collective-permute-start | bytes 24584 | tf_op jit(solution)/shard_map/ppermute | solution.py:224
  5.4 40.2 %collective-permute-start.11 = (bf16[1,4096]{1,0:T(2,128)(2,1)}, bf16[1,4096]{1,0:T(2,128)(2,1)S(1)}, u32[]{:S(2)}, u32[]{:S(2)}) collective-permute-start(bf16[1,4096]{1,0:T(2,128)(2,1)} %param.26), channel_id=1, source_target_pairs={{0,16},{16,0},{1,17},{17,1},{2,18},{18,2},{3,19},{19,3},{4,20},{20... | collective-permute-start | bytes 24584 | tf_op jit(solution)/shard_map/ppermute | solution.py:224
  45.6 29.9 %collective-permute-start.8 = (bf16[256,512]{1,0:T(8,128)(2,1)}, bf16[256,512]{1,0:T(8,128)(2,1)S(1)}, u32[]{:S(2)}, u32[]{:S(2)}) collective-permute-start(bf16[256,512]{1,0:T(8,128)(2,1)} %broadcast_select_fusion.1), channel_id=1, source_target_pairs={{16,2},{17,3},{18,0},{19,1},{20,6},{21,7},{22,4},{23,5},{24,10},{2... | collective-permute-start | bytes 786440 | tf_op jit(solution)/shard_map/ppermute | solution.py:142
  47.8 27.7 %collective-permute-start.7 = (bf16[256,512]{1,0:T(8,128)(2,1)}, bf16[256,512]{1,0:T(8,128)(2,1)S(1)}, u32[]{:S(2)}, u32[]{:S(2)}) collective-permute-start(bf16[256,512]{1,0:T(8,128)(2,1)} %broadcast_select_fusion.1), channel_id=1, source_target_pairs={{16,1},{17,0},{18,3},{19,2},{20,5},{21,4},{22,7},{23,6},{24,9},{25... | collective-permute-start | bytes 786440 | tf_op jit(solution)/shard_map/ppermute | solution.py:142
  77.2 27.6 %collective-permute-start.52 = (bf16[256,512]{1,0:T(8,128)(2,1)S(1)}, bf16[256,512]{1,0:T(8,128)(2,1)S(1)}, u32[]{:S(2)}, u32[]{:S(2)}) collective-permute-start(bf16[256,512]{1,0:T(8,128)(2,1)S(1)} %broadcast_select_fusion), channel_id=1, source_target_pairs={{0,3},{1,2},{2,1},{3,0},{4,7},{5,6},{6,5},{7,4},{8,11},{9,10},{10,... | collective-permute-start | bytes 786440 | tf_op jit(solution)/shard_map/ppermute | solution.py:142
  133.7 27.6 %collective-permute-start.12 = (bf16[128,4096]{1,0:T(8,128)(2,1)S(1)}, bf16[128,4096]{1,0:T(8,128)(2,1)S(1)}, u32[]{:S(2)}, u32[]{:S(2)}) collective-permute-start(bf16[128,4096]{1,0:T(8,128)(2,1)S(1)} %get-tuple-element.58), channel_id=1, source_target_pairs={{0,1},{1,0},{2,3},{3,2},{4,5},{5,4},{6,7},{7,6},{8,9},{9,8},{10,11... | collective-permute-start | bytes 3145736 | tf_op jit(solution)/shard_map/ppermute | solution.py:142
  157.4 39.1 %collective-permute-start.58 = (bf16[128,4096]{1,0:T(8,128)(2,1)S(1)}, bf16[128,4096]{1,0:T(8,128)(2,1)}, u32[]{:S(2)}, u32[]{:S(2)}) collective-permute-start(bf16[128,4096]{1,0:T(8,128)(2,1)S(1)} %get-tuple-element.80), channel_id=1, source_target_pairs={{0,1},{1,0},{2,3},{3,2},{4,5},{5,4},{6,7},{7,6},{8,9},{9,8},{10,11... | collective-permute-start | bytes 3145736 | tf_op jit(solution)/shard_map/ppermute | solution.py:142
  166.4 28.4 %collective-permute-start.13 = (bf16[32,4096]{1,0:T(8,128)(2,1)S(1)}, bf16[32,4096]{1,0:T(8,128)(2,1)}, u32[]{:S(2)}, u32[]{:S(2)}) collective-permute-start(bf16[32,4096]{1,0:T(8,128)(2,1)S(1)} %get-tuple-element.153), channel_id=1, source_target_pairs={{0,2},{1,3},{2,0},{3,1},{4,6},{5,7},{6,4},{7,5},{8,10},{9,11},{10,... | collective-permute-start | bytes 786440 | tf_op jit(solution)/shard_map/ppermute | solution.py:142
  207.9 31.9 %collective-permute-start.18 = (bf16[32,4096]{1,0:T(8,128)(2,1)S(1)}, bf16[32,4096]{1,0:T(8,128)(2,1)S(1)}, u32[]{:S(2)}, u32[]{:S(2)}) collective-permute-start(bf16[32,4096]{1,0:T(8,128)(2,1)S(1)} %fusion.8.refs_4_), channel_id=1, source_target_pairs={{16,1},{17,0},{18,3},{19,2},{20,5},{21,4},{22,7},{23,6},{24,9},{25... | collective-permute-start | bytes 786440 | tf_op jit(solution)/shard_map/ppermute | solution.py:142
  241.2 34.9 %collective-permute-start.62 = (bf16[32,4096]{1,0:T(8,128)(2,1)S(1)}, bf16[32,4096]{1,0:T(8,128)(2,1)S(1)}, u32[]{:S(2)}, u32[]{:S(2)}) collective-permute-start(bf16[32,4096]{1,0:T(8,128)(2,1)S(1)} %fusion.20.refs_4_), channel_id=1, source_target_pairs={{0,1},{1,0},{2,3},{3,2},{4,5},{5,4},{6,7},{7,6},{8,9},{9,8},{10,11... | collective-permute-start | bytes 786440 | tf_op jit(solution)/shard_map/ppermute | solution.py:142
  243.1 35.7 %collective-permute-start.63 = (bf16[32,4096]{1,0:T(8,128)(2,1)S(1)}, bf16[32,4096]{1,0:T(8,128)(2,1)S(1)}, u32[]{:S(2)}, u32[]{:S(2)}) collective-permute-start(bf16[32,4096]{1,0:T(8,128)(2,1)S(1)} %fusion.20.refs_4_), channel_id=1, source_target_pairs={{16,1},{17,0},{18,3},{19,2},{20,5},{21,4},{22,7},{23,6},{24,9},{25... | collective-permute-start | bytes 786440 | tf_op jit(solution)/shard_map/ppermute | solution.py:142
  245.1 43.7 %collective-permute-start.64 = (bf16[32,4096]{1,0:T(8,128)(2,1)S(1)}, bf16[32,4096]{1,0:T(8,128)(2,1)S(1)}, u32[]{:S(2)}, u32[]{:S(2)}) collective-permute-start(bf16[32,4096]{1,0:T(8,128)(2,1)S(1)} %fusion.20.refs_4_), channel_id=1, source_target_pairs={{0,3},{1,2},{2,1},{3,0},{4,7},{5,6},{6,5},{7,4},{8,11},{9,10},{10,... | collective-permute-start | bytes 786440 | tf_op jit(solution)/shard_map/ppermute | solution.py:142
  251.8 41.8 %collective-permute-start.65 = (bf16[32,4096]{1,0:T(8,128)(2,1)S(1)}, bf16[32,4096]{1,0:T(8,128)(2,1)S(1)}, u32[]{:S(2)}, u32[]{:S(2)}) collective-permute-start(bf16[32,4096]{1,0:T(8,128)(2,1)S(1)} %fusion.20.refs_4_), channel_id=1, source_target_pairs={{16,3},{17,2},{18,1},{19,0},{20,7},{21,6},{22,5},{23,4},{24,11},{2... | collective-permute-start | bytes 786440 | tf_op jit(solution)/shard_map/ppermute | solution.py:142
  258.7 34.8 %collective-permute-start.66 = (bf16[32,4096]{1,0:T(8,128)(2,1)S(1)}, bf16[32,4096]{1,0:T(8,128)(2,1)S(1)}, u32[]{:S(2)}, u32[]{:S(2)}) collective-permute-start(bf16[32,4096]{1,0:T(8,128)(2,1)S(1)} %fusion.20.refs_4_), channel_id=1, source_target_pairs={{16,0},{17,1},{18,2},{19,3},{20,4},{21,5},{22,6},{23,7},{24,8},{25... | collective-permute-start | bytes 786440 | tf_op jit(solution)/shard_map/ppermute | solution.py:142
  288.8 31.3 %collective-permute-start.24 = (bf16[128,4096]{1,0:T(8,128)(2,1)S(1)}, bf16[128,4096]{1,0:T(8,128)(2,1)S(1)}, u32[]{:S(2)}, u32[]{:S(2)}) collective-permute-start(bf16[128,4096]{1,0:T(8,128)(2,1)S(1)} %get-tuple-element.63), channel_id=1, source_target_pairs={{0,1},{1,0},{2,3},{3,2},{4,5},{5,4},{6,7},{7,6},{8,9},{9,8},{10,11... | collective-permute-start | bytes 3145736 | tf_op jit(solution)/shard_map/ppermute | solution.py:142
  351.6 30.7 %collective-permute-start.28 = (bf16[32,4096]{1,0:T(8,128)(2,1)S(1)}, bf16[32,4096]{1,0:T(8,128)(2,1)S(1)}, u32[]{:S(2)}, u32[]{:S(2)}) collective-permute-start(bf16[32,4096]{1,0:T(8,128)(2,1)S(1)} %fusion.12.refs_5_), channel_id=1, source_target_pairs={{0,17},{1,16},{2,19},{3,18},{4,21},{5,20},{6,23},{7,22},{8,25},{9,... | collective-permute-start | bytes 786440 | tf_op jit(solution)/shard_map/ppermute | solution.py:142
  353.0 30.7 %collective-permute-start.29 = (bf16[32,4096]{1,0:T(8,128)(2,1)S(1)}, bf16[32,4096]{1,0:T(8,128)(2,1)S(1)}, u32[]{:S(2)}, u32[]{:S(2)}) collective-permute-start(bf16[32,4096]{1,0:T(8,128)(2,1)S(1)} %fusion.12.refs_5_), channel_id=1, source_target_pairs={{16,17},{17,16},{18,19},{19,18},{20,21},{21,20},{22,23},{23,22},{2... | collective-permute-start | bytes 786440 | tf_op jit(solution)/shard_map/ppermute | solution.py:142
  364.8 34.8 %collective-permute-start.32 = (bf16[32,4096]{1,0:T(8,128)(2,1)S(1)}, bf16[32,4096]{1,0:T(8,128)(2,1)S(1)}, u32[]{:S(2)}, u32[]{:S(2)}) collective-permute-start(bf16[32,4096]{1,0:T(8,128)(2,1)S(1)} %fusion.12.refs_5_), channel_id=1, source_target_pairs={{0,16},{1,17},{2,18},{3,19},{4,20},{5,21},{6,22},{7,23},{8,24},{9,... | collective-permute-start | bytes 786440 | tf_op jit(solution)/shard_map/ppermute | solution.py:142
  384.5 39.6 %collective-permute-start.73 = (bf16[32,4096]{1,0:T(8,128)(2,1)S(1)}, bf16[32,4096]{1,0:T(8,128)(2,1)S(1)}, u32[]{:S(2)}, u32[]{:S(2)}) collective-permute-start(bf16[32,4096]{1,0:T(8,128)(2,1)S(1)} %fusion.24.refs_5_), channel_id=1, source_target_pairs={{0,17},{1,16},{2,19},{3,18},{4,21},{5,20},{6,23},{7,22},{8,25},{9,... | collective-permute-start | bytes 786440 | tf_op jit(solution)/shard_map/ppermute | solution.py:142
  388.3 37.1 %collective-permute-start.74 = (bf16[32,4096]{1,0:T(8,128)(2,1)S(1)}, bf16[32,4096]{1,0:T(8,128)(2,1)S(1)}, u32[]{:S(2)}, u32[]{:S(2)}) collective-permute-start(bf16[32,4096]{1,0:T(8,128)(2,1)S(1)} %fusion.24.refs_5_), channel_id=1, source_target_pairs={{16,17},{17,16},{18,19},{19,18},{20,21},{21,20},{22,23},{23,22},{2... | collective-permute-start | bytes 786440 | tf_op jit(solution)/shard_map/ppermute | solution.py:142
  399.6 32.7 %collective-permute-start.75 = (bf16[32,4096]{1,0:T(8,128)(2,1)S(1)}, bf16[32,4096]{1,0:T(8,128)(2,1)S(1)}, u32[]{:S(2)}, u32[]{:S(2)}) collective-permute-start(bf16[32,4096]{1,0:T(8,128)(2,1)S(1)} %fusion.24.refs_5_), channel_id=1, source_target_pairs={{0,19},{1,18},{2,17},{3,16},{4,23},{5,22},{6,21},{7,20},{8,27},{9,... | collective-permute-start | bytes 786440 | tf_op jit(solution)/shard_map/ppermute | solution.py:142
  406.3 28.4 %collective-permute-start.76 = (bf16[32,4096]{1,0:T(8,128)(2,1)S(1)}, bf16[32,4096]{1,0:T(8,128)(2,1)S(1)}, u32[]{:S(2)}, u32[]{:S(2)}) collective-permute-start(bf16[32,4096]{1,0:T(8,128)(2,1)S(1)} %fusion.24.refs_5_), channel_id=1, source_target_pairs={{16,19},{17,18},{18,17},{19,16},{20,23},{21,22},{22,21},{23,20},{2... | collective-permute-start | bytes 786440 | tf_op jit(solution)/shard_map/ppermute | solution.py:142
  407.0 27.7 %collective-permute-start.77 = (bf16[32,4096]{1,0:T(8,128)(2,1)S(1)}, bf16[32,4096]{1,0:T(8,128)(2,1)S(1)}, u32[]{:S(2)}, u32[]{:S(2)}) collective-permute-start(bf16[32,4096]{1,0:T(8,128)(2,1)S(1)} %fusion.24.refs_5_), channel_id=1, source_target_pairs={{0,16},{1,17},{2,18},{3,19},{4,20},{5,21},{6,22},{7,23},{8,24},{9,... | collective-permute-start | bytes 786440 | tf_op jit(solution)/shard_map/ppermute | solution.py:142
  485.8 33.0 %collective-permute-start.39 = (bf16[32,4096]{1,0:T(8,128)(2,1)S(1)}, bf16[32,4096]{1,0:T(8,128)(2,1)S(1)}, u32[]{:S(2)}, u32[]{:S(2)}) collective-permute-start(bf16[32,4096]{1,0:T(8,128)(2,1)S(1)} %fusion.16.refs_5_), channel_id=1, source_target_pairs={{0,17},{1,16},{2,19},{3,18},{4,21},{5,20},{6,23},{7,22},{8,25},{9,... | collective-permute-start | bytes 786440 | tf_op jit(solution)/shard_map/ppermute | solution.py:142
  521.0 36.2 %collective-permute-start.84 = (bf16[32,4096]{1,0:T(8,128)(2,1)S(1)}, bf16[32,4096]{1,0:T(8,128)(2,1)S(1)}, u32[]{:S(2)}, u32[]{:S(2)}) collective-permute-start(bf16[32,4096]{1,0:T(8,128)(2,1)S(1)} %fusion.28.refs_5_), channel_id=1, source_target_pairs={{0,17},{1,16},{2,19},{3,18},{4,21},{5,20},{6,23},{7,22},{8,25},{9,... | collective-permute-start | bytes 786440 | tf_op jit(solution)/shard_map/ppermute | solution.py:142
  524.5 34.4 %collective-permute-start.85 = (bf16[32,4096]{1,0:T(8,128)(2,1)S(1)}, bf16[32,4096]{1,0:T(8,128)(2,1)S(1)}, u32[]{:S(2)}, u32[]{:S(2)}) collective-permute-start(bf16[32,4096]{1,0:T(8,128)(2,1)S(1)} %fusion.28.refs_5_), channel_id=1, source_target_pairs={{16,17},{17,16},{18,19},{19,18},{20,21},{21,20},{22,23},{23,22},{2... | collective-permute-start | bytes 786440 | tf_op jit(solution)/shard_map/ppermute | solution.py:142
  525.2 42.8 %collective-permute-start.86 = (bf16[32,4096]{1,0:T(8,128)(2,1)S(1)}, bf16[32,4096]{1,0:T(8,128)(2,1)S(1)}, u32[]{:S(2)}, u32[]{:S(2)}) collective-permute-start(bf16[32,4096]{1,0:T(8,128)(2,1)S(1)} %fusion.28.refs_5_), channel_id=1, source_target_pairs={{0,19},{1,18},{2,17},{3,16},{4,23},{5,22},{6,21},{7,20},{8,27},{9,... | collective-permute-start | bytes 786440 | tf_op jit(solution)/shard_map/ppermute | solution.py:142
  537.3 31.4 %collective-permute-start.87 = (bf16[32,4096]{1,0:T(8,128)(2,1)S(1)}, bf16[32,4096]{1,0:T(8,128)(2,1)S(1)}, u32[]{:S(2)}, u32[]{:S(2)}) collective-permute-start(bf16[32,4096]{1,0:T(8,128)(2,1)S(1)} %fusion.28.refs_5_), channel_id=1, source_target_pairs={{16,19},{17,18},{18,17},{19,16},{20,23},{21,22},{22,21},{23,20},{2... | collective-permute-start | bytes 786440 | tf_op jit(solution)/shard_map/ppermute | solution.py:142
  538.0 30.7 %collective-permute-start.88 = (bf16[32,4096]{1,0:T(8,128)(2,1)S(1)}, bf16[32,4096]{1,0:T(8,128)(2,1)S(1)}, u32[]{:S(2)}, u32[]{:S(2)}) collective-permute-start(bf16[32,4096]{1,0:T(8,128)(2,1)S(1)} %fusion.28.refs_5_), channel_id=1, source_target_pairs={{0,16},{1,17},{2,18},{3,19},{4,20},{5,21},{6,22},{7,23},{8,24},{9,... | collective-permute-start | bytes 786440 | tf_op jit(solution)/shard_map/ppermute | solution.py:142
  598.0 42.1 %collective-permute-start.94 = (bf16[32,4096]{1,0:T(8,128)(2,1)S(1)}, bf16[32,4096]{1,0:T(8,128)(2,1)S(1)}, u32[]{:S(2)}, u32[]{:S(2)}) collective-permute-start(bf16[32,4096]{1,0:T(8,128)(2,1)S(1)} %get-tuple-element.133), channel_id=1, source_target_pairs={{16,0},{17,1},{18,2},{19,3},{20,4},{21,5},{22,6},{23,7},{24,8},{25... | collective-permute-start | bytes 786440 | tf_op jit(solution)/shard_map/ppermute | solution.py:142
  599.3 40.8 %collective-permute-start.93 = (bf16[32,4096]{1,0:T(8,128)(2,1)S(1)}, bf16[32,4096]{1,0:T(8,128)(2,1)S(1)}, u32[]{:S(2)}, u32[]{:S(2)}) collective-permute-start(bf16[32,4096]{1,0:T(8,128)(2,1)S(1)} %get-tuple-element.134), channel_id=1, source_target_pairs={{16,18},{17,19},{18,16},{19,17},{20,22},{21,23},{22,20},{23,21},{2... | collective-permute-start | bytes 786440 | tf_op jit(solution)/shard_map/ppermute | solution.py:142
  606.5 53.3 %collective-permute-start.92 = (bf16[32,4096]{1,0:T(8,128)(2,1)S(1)}, bf16[32,4096]{1,0:T(8,128)(2,1)S(1)}, u32[]{:S(2)}, u32[]{:S(2)}) collective-permute-start(bf16[32,4096]{1,0:T(8,128)(2,1)S(1)} %get-tuple-element.132), channel_id=1, source_target_pairs={{16,2},{17,3},{18,0},{19,1},{20,6},{21,7},{22,4},{23,5},{24,10},{2... | collective-permute-start | bytes 786440 | tf_op jit(solution)/shard_map/ppermute | solution.py:142
  (88 other events, 1516.0 us)
